TPU v7x, 32 devices: a whole 2x2x4 slice. The times are simulated.
32 devices in a mesh: parts: 2 (over x), seq: 16 (over z, y, core).
Axes of the slice: x: 2, y: 2, z: 4, core: 2. Of those that a mesh axis runs over, the one named last changes fastest.
Arguments:
- queries: bfloat16 [4096, 1024], P(('parts', 'seq')), parts along dimension 0, may hold values from -6 to 6
- keys: bfloat16 [4096, 1024], P(('parts', 'seq')), parts along dimension 0, may hold values from -6 to 6
- values: bfloat16 [4096, 1024], P(('parts', 'seq')), parts along dimension 0, may hold values from -6 to 6
- log_forget: float32 [8, 4096], P(None, ('parts', 'seq')), parts along dimension 1, may hold values from -5 to 0
- input_gate: float32 [8, 4096], P(None, ('parts', 'seq')), parts along dimension 1, may hold values from 0.1 to 1
- ridge: float32 [8], replicated, may hold values from 0.25 to 4
- gain: float32 [1024], replicated, may hold values from 0.25 to 1.75
- out_weight: bfloat16 [1024, 2048], P('seq'), may hold values from -0.1875 to 0.1875
Outputs:
- mixed: bfloat16 [4096, 2048], P(('parts', 'seq')), parts along dimension 0
There are 2 independent parts, one for each index of `parts`. A program takes and returns all parts, laid end to end along the dimension named above; an argument that names none is the same for every part. Nothing has to cross between parts.
All inputs are finite; a program needn't handle non-finite values. Where the computation divides by a largest or mean magnitude, that divisor is 1e-20 or more.
Results may differ from a plain program's by a relative error of at most 0.007.
Values may be sent and summed in bfloat16 or wider, within the bound.
No kernel may reach another device: no remote copies, remote signals or barrier semaphores. Data moves between devices by JAX's collectives and lax.ppermute only.
A program may use at most 192 MiB of HBM per device.

v0:
```python
import functools
import jax
import jax.numpy as jnp
from jax import lax
from jax.experimental import pallas as pl
from jax.experimental.pallas import tpu as pltpu
from jax.sharding import PartitionSpec as P

NEWTON = 6
CORR = 4
F32 = jnp.float32
BF16 = jnp.bfloat16
EXACT = lax.Precision.HIGHEST
VMEM = pltpu.VMEM
GRANT = 8 * 1024 * 1024


def rows_of(shape):
    return lax.broadcasted_iota(jnp.int32, shape, 0)


def lanes_of(shape):
    return lax.broadcasted_iota(jnp.int32, shape, 1)


def split(x):
    high = x.astype(BF16)
    return high, (x - high.astype(F32)).astype(BF16)


def dot(a, b):
    return jnp.dot(a, b, preferred_element_type=F32)


def dot_t(a, b):
    return lax.dot_general(a, b, (((0,), (0,)), ((), ())), preferred_element_type=F32)


def wide(pair):
    high, low = pair
    return jnp.concatenate([high, low, high], axis=1)


def tall(pair):
    high, low = pair
    return jnp.concatenate([high, high, low], axis=0)


def unit_rows(x):
    return x * lax.rsqrt(jnp.sum(x * x, axis=-1, keepdims=True) + 1e-6)


def pick(first, own, other):
    return jnp.where(first, own, other)


def columns(ref, core, h, half, width):
    return ref[:, pl.ds(pl.multiple_of((core * half + h) * width, width), width)]


def gates(own_ref, other_ref, core, half):
    own, other = own_ref[...], other_ref[...]
    return jnp.concatenate(
        [
            jnp.where(core == 0, own[:half], own[half:]),
            jnp.where(core == 0, other[:half], other[half:]),
        ],
        axis=0,
    )


def running_sum(a):
    width = a.shape[-1]
    tri = (rows_of((width, width)) <= lanes_of((width, width))).astype(F32)
    return jnp.dot(a, tri, precision=EXACT, preferred_element_type=F32)


def pack(sym):
    width = sym.shape[0]
    half = width // 2
    top, low = sym[:half], pltpu.roll(sym[half:], half, 1)
    shape = (half, width)
    r, c = rows_of(shape), lanes_of(shape)
    body = jnp.where(r > c, low, top)
    diag = jnp.sum(jnp.where(r == c, low, 0.0), axis=0, keepdims=True)
    return body, diag


def unpack(body, diag):
    half, _ = body.shape
    r, c = rows_of(body.shape), lanes_of(body.shape)
    top = jnp.where(c > r, body, 0.0) + jnp.where(c == r, 0.5 * body, 0.0)
    low = jnp.where(c < r, body, 0.0) + jnp.where(c == r, 0.5 * diag, 0.0)
    full = jnp.concatenate([top, pltpu.roll(low, half, 1)], axis=0)
    return full + full.T


def tail_rows(diag, level):
    r = rows_of((8, diag.shape[-1]))
    return jnp.where(r == 0, diag, jnp.where(r == 1, level, 0.0))


def tail_sent(diag, level):
    one = level.astype(BF16).astype(F32)
    two = (level - one).astype(BF16).astype(F32)
    three = level - one - two
    r = rows_of((16, diag.shape[-1]))
    out = jnp.where(r == 0, diag, jnp.where(r == 1, one, jnp.where(r == 2, two, jnp.where(r == 3, three, 0.0))))
    return out.astype(BF16)


def sums_kernel(meta, ko, kr, vo, vr, fo, fr, go, gr, pg, tg, pw, tw, gf, uf, ks):
    half = gf.shape[0]
    width = gf.shape[1]
    body = width // 2
    core = meta[0]
    forget = gates(fo, fr, core, half)
    beta = gates(go, gr, core, half)
    level = running_sum(forget)
    last = level[:, width - 1 :]
    tails = (jnp.exp(last - level) * beta).T
    decay = jnp.exp(last)
    first = core == 0
    for h in range(half):
        grams, states = [], []
        for side, (kref, vref) in enumerate(((ko, vo), (kr, vr))):
            p = h + side * half
            k = unit_rows(columns(kref, core, h, half, width).astype(F32))
            tk = split(k * tails[:, p : p + 1])
            kk = split(k)
            ks[p, 0], ks[p, 1] = kk
            v = columns(vref, core, h, half, width)
            grams.append(
                dot_t(jnp.concatenate([tk[0], tk[1], tk[0]], axis=0), jnp.concatenate([kk[0], kk[0], kk[1]], axis=0))
            )
            states.append(dot_t(jnp.concatenate([tk[0], tk[1]], axis=0), jnp.concatenate([v, v], axis=0)))
        early = pick(first, grams[0], grams[1])
        late = pick(first, grams[1], grams[0])
        early_state = pick(first, states[0], states[1])
        late_state = pick(first, states[1], states[0])
        shrink = pick(first, decay[half + h : half + h + 1], decay[h : h + 1])
        gf[h] = early
        uf[h] = early_state
        packed, diag = pack(shrink * early + late)
        total = jnp.broadcast_to(last[h : h + 1] + last[half + h : half + h + 1], (1, width))
        tg[h, :body] = packed
        tg[h, body:] = tail_rows(diag, total)
        pg[h, :body] = packed.astype(BF16)
        pg[h, body:] = tail_sent(diag, total)
        state = shrink * early_state + late_state
        tw[h] = state
        pw[h] = state.astype(BF16)


def join_kernel(which, has_prefix, meta, t, got, *rest):
    if has_prefix:
        before, t_new, sent, before_new, coef = rest
    else:
        t_new, sent, before_new, coef = rest
    bit = meta[which] == 1
    half, rows, width = t.shape
    body = rows - 8
    for h in range(half):
        tail = t[h, body:]
        mine = tail[1:2]
        ends = got[h, body:].astype(F32)
        theirs = ends[1:2] + ends[2:3] + ends[3:4]
        a = jnp.where(bit, 1.0, jnp.exp(theirs))
        b = jnp.where(bit, jnp.exp(mine), 1.0)
        arrived = got[h, :body].astype(F32)
        packed = a * t[h, :body] + b * arrived
        diag = a * tail[:1] + b * ends[:1]
        t_new[h, :body] = packed
        t_new[h, body:] = tail_rows(diag, mine + theirs)
        sent[h, :body] = packed.astype(BF16)
        sent[h, body:] = tail_sent(diag, mine + theirs)
        if has_prefix:
            old = before[h, body:]
            e = jnp.where(bit, jnp.exp(old[1:2]), 0.0)
            before_new[h, :body] = before[h, :body] + e * arrived
            before_new[h, body:] = tail_rows(old[:1] + e * ends[:1], old[1:2] + jnp.where(bit, theirs, 0.0))
        else:
            e = jnp.where(bit, jnp.ones_like(mine), 0.0)
            before_new[h, :body] = e * arrived
            before_new[h, body:] = tail_rows(e * ends[:1], jnp.where(bit, theirs, 0.0))
        r = rows_of((8, width))
        coef[h] = jnp.where(r == 0, a, jnp.where(r == 1, b, jnp.where(r == 2, e, 0.0)))


def join_state_kernel(has_prefix, coef, t, got, *rest):
    if has_prefix:
        before, t_new, sent, before_new = rest
    else:
        t_new, sent, before_new = rest
    for h in range(t.shape[0]):
        c = coef[h]
        arrived = got[h].astype(F32)
        new = c[0:1] * t[h] + c[1:2] * arrived
        t_new[h] = new
        sent[h] = new.astype(BF16)
        add = c[2:3] * arrived
        before_new[h] = before[h] + add if has_prefix else add


def prepare_kernel(meta, ridge, ks, qo, qr, fo, fr, go, gr, q_s, kt, m_s, e_s, base):
    pairs, _, tokens, width = ks.shape
    half = pairs // 2
    core = meta[0]
    beta = gates(go, gr, core, half)
    level = running_sum(gates(fo, fr, core, half))
    level_t = level.T
    beta_t = beta.T
    square = (tokens, tokens)
    lower = rows_of(square) >= lanes_of(square)
    eye = (rows_of((width, width)) == lanes_of((width, width))).astype(F32)
    for side, qref in enumerate((qo, qr)):
        for h in range(half):
            p = h + side * half
            kh, kl = ks[p, 0], ks[p, 1]
            kt[p, 0], kt[p, 1] = kh.T, kl.T
            k = kh.astype(F32) + kl.astype(F32)
            bk = split(k * beta_t[:, p : p + 1])
            cross = dot_t(jnp.concatenate([bk[0], bk[1], bk[0]], axis=0), jnp.concatenate([kh, kh, kl], axis=0))
            base[p] = cross + ridge[core * half + h] * eye
            column = level_t[:, p : p + 1]
            m_s[p] = jnp.where(lower, jnp.exp(jnp.minimum(column - level[p : p + 1], 0.0)) * beta[p : p + 1], 0.0)
            e_s[p] = jnp.broadcast_to(jnp.exp(column), square)
            q_s[p] = unit_rows(columns(qref, core, h, half, width).astype(F32))


def inverse_kernel(which, meta, base, fo, fr, gf, before, got, s_s, p_s, a_s):
    half, width, _ = gf.shape
    body = width // 2
    pairs = 2 * half
    core = meta[0]
    first = core == 0
    bit = meta[which] == 1
    forget = gates(fo, fr, core, half)
    decay = jnp.exp(jnp.sum(forget, axis=1, keepdims=True))
    eye = (rows_of((width, width)) == lanes_of((width, width))).astype(F32)
    for h in range(half):
        tail = before[h, body:]
        ends = got[h, body:].astype(F32)
        e = jnp.where(bit, jnp.exp(tail[1:2]), 0.0)
        start = unpack(before[h, :body] + e * got[h, :body].astype(F32), tail[:1] + e * ends[:1])
        for side, is_early in enumerate((first, jnp.logical_not(first))):
            p = h + side * half
            other = h + (1 - side) * half
            gram = jnp.where(is_early, start, decay[other : other + 1] * start + gf[h])
            s_s[p, 0], s_s[p, 1] = split(gram)
            system = gram + base[p]
            bound = jnp.max(jnp.sum(jnp.abs(system), axis=0, keepdims=True), axis=1, keepdims=True)
            a_s[p, 0], a_s[p, 1] = split(system)
            p_s[p] = eye / bound

    def refine(_, carry):
        left = [eye - dot(a_s[p, 0], p_s[p].astype(BF16)) for p in range(pairs)]
        for p in range(pairs):
            now = p_s[p]
            p_s[p] = now + dot(now.astype(BF16), left[p].astype(BF16))
        return carry

    lax.fori_loop(0, NEWTON - 1, refine, 0)
    for start in range(0, pairs, half):
        group = range(start, start + half)
        left = []
        for p in group:
            left.append(eye - dot(wide((a_s[p, 0], a_s[p, 1])), tall(split(p_s[p]))))
        for p, rest in zip(group, left):
            now = p_s[p]
            p_s[p] = now + dot(wide(split(now)), tall(split(rest)))


def correct_kernel(meta, ridge, q_s, kt, m_s, e_s, ks, s_s, p_s, vo, vr, xs, part, x_s):
    pairs, _, width = q_s.shape
    half = pairs // 2
    core = meta[0]

    def both_of(p, i):
        return jnp.concatenate([s_s[p, i], kt[p, i]], axis=1)

    for p in range(pairs):
        x_s[p] = dot(q_s[p].astype(BF16), p_s[p].astype(BF16))

    def correct(_, carry):
        both = [dot(x_s[p].astype(BF16), both_of(p, 0)) for p in range(pairs)]
        applied = []
        for p in range(pairs):
            scores = m_s[p] * both[p][:, width:]
            applied.append(
                e_s[p] * both[p][:, :width]
                + dot(scores.astype(BF16), ks[p, 0])
                + ridge[core * half + p % half] * x_s[p]
            )
        for p in range(pairs):
            x_s[p] = x_s[p] + dot((q_s[p] - applied[p]).astype(BF16), p_s[p].astype(BF16))
        return carry

    lax.fori_loop(0, CORR - 2, correct, 0)

    for start, vref in ((0, vo), (half, vr)):
        group = range(start, start + half)
        both = [dot(wide(split(x_s[p])), tall((both_of(p, 0), both_of(p, 1)))) for p in group]
        applied = []
        for p, found in zip(group, both):
            scores = m_s[p] * found[:, width:]
            applied.append(
                e_s[p] * found[:, :width]
                + dot(wide(split(scores)), tall((ks[p, 0], ks[p, 1])))
                + ridge[core * half + p - start] * x_s[p]
            )
        solved = []
        for p, found in zip(group, applied):
            x = x_s[p] + dot((q_s[p] - found).astype(BF16), p_s[p].astype(BF16))
            solved.append(split(x))
            xs[p, 0], xs[p, 1] = solved[-1]
        scores = []
        for p, x in zip(group, solved):
            scores.append(m_s[p] * dot(wide(x), tall((kt[p, 0], kt[p, 1]))))
        for p, found in zip(group, scores):
            v = columns(vref, core, p - start, half, width)
            sh, sl = split(found)
            part[p] = dot(jnp.concatenate([sh, sl], axis=1), jnp.concatenate([v, v], axis=0))


def read_kernel(which, meta, xs, part, e_s, fo, fr, uf, before_g, before, got, gain, y_own, y_other):
    half = uf.shape[0]
    width = uf.shape[1]
    body = width // 2
    core = meta[0]
    first = core == 0
    bit = meta[which] == 1
    decay = jnp.exp(jnp.sum(gates(fo, fr, core, half), axis=1, keepdims=True))
    sides = ((y_own, first), (y_other, jnp.logical_not(first)))
    for h in range(half):
        cols = slice(h * width, (h + 1) * width)
        e = jnp.where(bit, jnp.exp(before_g[h, body + 1 : body + 2]), 0.0)
        start = before[h] + e * got[h].astype(F32)
        scale = columns(gain, core, h, half, width)
        for side, (out, is_early) in enumerate(sides):
            p = h + side * half
            other = h + (1 - side) * half
            state = jnp.where(is_early, start, decay[other : other + 1] * start + uf[h])
            read = dot(wide((xs[p, 0], xs[p, 1])), tall(split(state)))
            o = e_s[p] * read + part[p]
            o = o * lax.rsqrt(jnp.mean(o * o, axis=-1, keepdims=True) + 1e-6)
            out[:, cols] = (o * scale).astype(BF16)


def share_kernel(meta, w, out):
    size = out.shape[2]
    share = meta[meta.shape[0] - 1]
    out[0] = w[:, pl.ds(pl.multiple_of(share * size, size), size)]


def stack_kernel(a, b, out):
    out[: a.shape[0]] = a[...]
    out[a.shape[0] :] = b[...]


def gathered_rows(meta, y_own, y_other, y):
    core = meta[0]
    size = y_own.shape[1]
    y[:, pl.ds(pl.multiple_of(core * size, size), size)] = y_own[...]
    y[:, pl.ds(pl.multiple_of((1 - core) * size, size), size)] = y_other[...]


def project_kernel(table, chips, meta, y_own, y_other, own, other, *rest):
    out, y = rest[-2:]
    core = meta[0]
    place = meta[meta.shape[0] - 2]
    share = meta[meta.shape[0] - 1]
    gathered_rows(meta, y_own, y_other, y)
    width = 2 * own.shape[0]
    shares = own.shape[1] // rest[0].shape[2]
    size = rest[0].shape[2]
    tokens = y.shape[0]
    lefts = []
    for offset in range(chips):
        chip = jnp.bitwise_xor(place, offset)
        rows = y[:, pl.ds(pl.multiple_of(chip * width, width), width)].astype(F32)
        rows = jnp.where(core == 0, rows, pltpu.roll(rows, width // 2, 1))
        lefts.append(rows.astype(BF16))
    for q in range(shares):
        where = pl.ds(pl.multiple_of(jnp.bitwise_xor(share, q) * size, size), size)
        total = jnp.zeros((tokens, size), F32)
        for offset in range(0, chips, 2):
            blocks = []
            for o in (offset, offset + 1):
                for flip in (0, 1):
                    if o == 0:
                        blocks.append((own, other)[flip][:, where])
                    else:
                        piece, i = table[o, flip, q]
                        blocks.append(rest[piece][i])
            left = jnp.concatenate([lefts[offset], lefts[offset + 1]], axis=1)
            total = total + dot(left, jnp.concatenate(blocks, axis=0))
        out[:, where] = total.astype(BF16)


def project_copy_kernel(table, meta, y_own, y_other, own, other, *rest):
    pieces = rest[:-4]
    out, w, y, sem = rest[-4:]
    core = meta[0]
    place = meta[meta.shape[0] - 2]
    share = meta[meta.shape[0] - 1]
    rows = own.shape[0]
    size = pieces[0].shape[2]

    def at(offset, flip):
        row = (jnp.bitwise_xor(place, offset) * 2 + jnp.bitwise_xor(core, flip)) * rows
        return pl.ds(pl.multiple_of(row, rows), rows)

    copies = [
        pltpu.make_async_copy(own, w.at[at(0, 0)], sem.at[0]),
        pltpu.make_async_copy(other, w.at[at(0, 1)], sem.at[1]),
    ]
    for (offset, flip, q), (piece, i) in table.items():
        where = pl.ds(pl.multiple_of(jnp.bitwise_xor(share, q) * size, size), size)
        copies.append(
            pltpu.make_async_copy(pieces[piece].at[i], w.at[at(offset, flip), where], sem.at[len(copies)])
        )
    for copy in copies:
        copy.start()
    gathered_rows(meta, y_own, y_other, y)
    for copy in copies:
        copy.wait()
    out[...] = dot(y[...], w[...]).astype(BF16)


SMEM = pltpu.SMEM


def call(kernel, outs, scalars, ins, scratch=()):
    spec = pl.BlockSpec(memory_space=VMEM)
    near = [pltpu.with_memory_space_constraint(a, VMEM) for a in ins]
    return pl.pallas_call(
        kernel,
        out_shape=outs,
        in_specs=[pl.BlockSpec(memory_space=SMEM)] * len(scalars) + [spec] * len(near),
        out_specs=jax.tree.map(lambda _: spec, outs),
        scratch_shapes=scratch,
        compiler_params=pltpu.CompilerParams(vmem_limit_bytes=GRANT),
    )(*scalars, *near)


def on_device(mesh, queries, keys, values, log_forget, input_gate, ridge, gain, out_weight):
    sections, parts = mesh.shape["seq"], mesh.shape["parts"]
    tokens, features = keys.shape
    heads = log_forget.shape[0]
    width = features // heads
    half = heads // 2
    pairs = 2 * half
    body = width // 2
    chips = sections // 2
    bits = chips.bit_length() - 1
    rows, out_columns = out_weight.shape
    index = lax.axis_index("seq")
    steps = lax.iota(jnp.int32, bits + 3)
    meta = jnp.where(
        steps == bits + 2, lax.axis_index("parts"), jnp.where(steps == bits + 1, index >> 1, (index >> steps) & 1)
    )

    def swap(array, distance, axis="seq"):
        count = mesh.shape[axis]
        return lax.ppermute(array, axis, [(i, i ^ distance) for i in range(count)])

    keys_o = swap(keys, 1)
    forget_o, gate_o = swap(log_forget, 1), swap(input_gate, 1)
    values_o, queries_o = swap(values, 1), swap(queries, 1)
    forgets = (log_forget, forget_o)
    gate_args = (*forgets, input_gate, gate_o)

    packed = (half, body + 8, width)
    sent = (half, body + 16, width)
    full = (half, width, width)
    many = (pairs, width, width)
    two = (pairs, 2, width, width)

    pg, tg, pw, tw, gf, uf, ks = call(
        sums_kernel,
        (VMEM(sent, BF16), VMEM(packed, F32), VMEM(full, BF16), VMEM(full, F32), VMEM(full, F32), VMEM(full, F32),
         VMEM(two, BF16)),
        (meta,),
        (keys, keys_o, values, values_o, *gate_args),
    )

    before = before_w = None
    for r in range(bits):
        got = swap(pg, 2 << r)
        got_w = swap(pw, 2 << r)
        if r == bits - 1:
            break
        extra = () if before is None else (before,)
        tg, pg, before, coef = call(
            functools.partial(join_kernel, r + 1, bool(extra)),
            (VMEM(packed, F32), VMEM(sent, BF16), VMEM(packed, F32), VMEM((half, 8, width), F32)),
            (meta,),
            (tg, got, *extra),
        )
        extra = () if before_w is None else (before_w,)
        tw, pw, before_w = call(
            functools.partial(join_state_kernel, bool(extra)),
            (VMEM(full, F32), VMEM(full, BF16), VMEM(full, F32)),
            (),
            (coef, tw, got_w, *extra),
        )
    last = bits

    size = out_columns // parts
    own = call(share_kernel, VMEM((1, rows, size), BF16), (meta,), (out_weight,))
    groups = []
    held = ((0,), own)
    for bit in reversed(range(1, bits)):
        fresh = (tuple(o ^ (1 << bit) for o in held[0]), swap(held[1], 2 << bit))
        groups.append(fresh)
        if bit > 1:
            held = (
                held[0] + fresh[0],
                call(stack_kernel, VMEM((2 * len(held[0]), rows, size), BF16), (), (held[1], fresh[1])),
            )
    groups.append((tuple(o ^ 1 for o in held[0]), swap(held[1], 2)))
    groups.append((tuple(o ^ 1 for o in fresh[0]), swap(fresh[1], 2)))
    table, pieces = {}, []
    for offsets, array in groups:
        shares = [(0, array)]
        step = 1
        while step < parts:
            shares += [(q ^ step, swap(a, step, "parts")) for q, a in shares]
            step *= 2
        for q, a in shares:
            for flip, b in ((0, a), (1, swap(a, 1))):
                for i, offset in enumerate(offsets):
                    table[offset, flip, q] = (len(pieces), i)
                pieces.append(b)
    weight_o = swap(out_weight, 1)

    q_s, kt, m_s, e_s, base = call(
        prepare_kernel,
        (VMEM(many, F32), VMEM(two, BF16), VMEM(many, F32), VMEM(many, F32), VMEM(many, F32)),
        (meta, ridge),
        (ks, queries, queries_o, *gate_args),
    )
    s_s, p_s = call(
        functools.partial(inverse_kernel, last),
        (VMEM(two, BF16), VMEM(many, F32)),
        (meta,),
        (base, *forgets, gf, before, got),
        (VMEM(two, BF16),),
    )
    xs, part = call(
        correct_kernel,
        (VMEM(two, BF16), VMEM(many, F32)),
        (meta, ridge),
        (q_s, kt, m_s, e_s, ks, s_s, p_s, values, values_o),
        (VMEM(many, F32),),
    )
    y_own, y_other = call(
        functools.partial(read_kernel, last),
        (VMEM((tokens, half * width), BF16),) * 2,
        (meta,),
        (xs, part, e_s, *forgets, uf, before, before_w, got_w, gain.reshape(1, features)),
    )
    y_got = swap(y_other, 1)

    result = jax.ShapeDtypeStruct((tokens, out_columns), BF16)
    y_full = VMEM((tokens, features), BF16)
    if 2 * rows == width:
        return call(
            functools.partial(project_kernel, table, chips),
            result,
            (meta,),
            (y_own, y_got, out_weight, weight_o, *pieces),
            (y_full,),
        )
    near = pl.BlockSpec(memory_space=VMEM)
    return pl.pallas_call(
        functools.partial(project_copy_kernel, table),
        out_shape=result,
        in_specs=[pl.BlockSpec(memory_space=SMEM), near, near] + [pl.BlockSpec(memory_space=pl.ANY)] * (2 + len(pieces)),
        out_specs=near,
        scratch_shapes=[
            VMEM((features, out_columns), BF16), y_full, pltpu.SemaphoreType.DMA((2 + len(table),))
        ],
    )(meta, y_own, y_got, out_weight, weight_o, *pieces)


def solution(mesh):
    rows = P(("parts", "seq"), None)
    gate = P(None, ("parts", "seq"))

    def body(*args):
        return on_device(mesh, *args)

    return jax.shard_map(
        body,
        mesh=mesh,
        in_specs=(rows, rows, rows, gate, gate, P(), P(), P("seq", None)),
        out_specs=rows,
        check_vma=False,
    )
```

profile of v0, /device:TPU:0, one launch (start us, length us, event | category | flops | bytes accessed | tf_op | source)
XLA Modules:
  0.0 73.1 jit_solution(3929924655825644519)
XLA Ops:
  0.5 0.9 %copy-done = bf16[64,2048]{1,0:T(8,128)(2,1)S(1)} copy-done((bf16[64,2048]{1,0:T(8,128)(2,1)S(1)}, bf16[64,2048]{1,0:T(8,128)(2,1)}, u32[]{:S(2)}) %copy-start) | copy-done | bytes 262168
  2.1 4.1 %collective-permute-start.13 = (bf16[1,64,1024]{2,1,0:T(8,128)(2,1)S(1)}, bf16[1,64,1024]{2,1,0:T(8,128)(2,1)S(1)}, u32[]{:S(2)}, u32[]{:S(2)}) collective-permute-start(bf16[1,64,1024]{2,1,0:T(8,128)(2,1)S(1)} %shard_map.91.a), channel_id=1, source_target_pairs={{0,8},{1,9},{2,10},{3,11},{4,12},{5,13},{6,14},{7,15},{8,0},{9,1},... | collective-permute-start | bytes 393224 | tf_op jit(solution)/shard_map/ppermute | solution.py:466
  6.2 6.5 %collective-permute-done.13.b.rest_0_ = bf16[1,64,1024]{2,1,0:T(8,128)(2,1)S(1)} collective-permute-done((bf16[1,64,1024]{2,1,0:T(8,128)(2,1)S(1)}, bf16[1,64,1024]{2,1,0:T(8,128)(2,1)S(1)}, u32[]{:S(2)}, u32[]{:S(2)}) %collective-permute-start.13) | collective-permute-done | bytes 131104 | tf_op jit(solution)/shard_map/ppermute | solution.py:466
  12.7 0.8 %collective-permute-start.17 = (bf16[2,64,1024]{2,1,0:T(8,128)(2,1)S(1)}, bf16[2,64,1024]{2,1,0:T(8,128)(2,1)S(1)}, u32[]{:S(2)}, u32[]{:S(2)}) collective-permute-start(bf16[2,64,1024]{2,1,0:T(8,128)(2,1)S(1)} %shard_map.92), channel_id=1, source_target_pairs={{0,4},{1,5},{2,6},{3,7},{4,0},{5,1},{6,2},{7,3},{8,12},{9,13},{10,... | collective-permute-start | bytes 786440 | tf_op jit(solution)/shard_map/ppermute | solution.py:466
  13.5 1.2 %collective-permute-done.2.fr = f32[8,128]{1,0:T(8,128)S(1)} collective-permute-done((f32[8,128]{1,0:T(8,128)S(1)}, f32[8,128]{1,0:T(8,128)S(1)}, u32[]{:S(2)}, u32[]{:S(2)}) %collective-permute-start.2) | collective-permute-done | bytes 4128 | tf_op jit(solution)/shard_map/ppermute | solution.py:466
  14.8 1.0 %collective-permute-done.3.gr = f32[8,128]{1,0:T(8,128)S(1)} collective-permute-done((f32[8,128]{1,0:T(8,128)S(1)}, f32[8,128]{1,0:T(8,128)S(1)}, u32[]{:S(2)}, u32[]{:S(2)}) %collective-permute-start.3) | collective-permute-done | bytes 4128 | tf_op jit(solution)/shard_map/ppermute | solution.py:466
  15.8 2.0 %shard_map.82 = (bf16[4,80,128]{2,1,0:T(8,128)(2,1)S(1)}, f32[4,72,128]{2,1,0:T(8,128)S(1)}, bf16[4,128,128]{2,1,0:T(8,128)(2,1)S(1)}, f32[4,128,128]{2,1,0:T(8,...) custom-call(s32[6]{0:T(128)S(1)} %compare_select_fusion.1.meta, ...), custom_call_target="tpu_custom_call" | custom-call | tf_op jit(solution)/shard_map/pallas_call | solution.py:437
  17.9 1.6 %collective-permute-start.8 = (bf16[4,128,128]{2,1,0:T(8,128)(2,1)S(1)}, bf16[4,128,128]{2,1,0:T(8,128)(2,1)S(1)}, u32[]{:S(2)}, u32[]{:S(2)}) collective-permute-start(bf16[4,128,128]{2,1,0:T(8,128)(2,1)S(1)} %get-tuple-element.57), channel_id=1, source_target_pairs={{0,2},{1,3},{2,0},{3,1},{4,6},{5,7},{6,4},{7,5},{8,10},{9,11},{10,... | collective-permute-start | bytes 393224 | tf_op jit(solution)/shard_map/ppermute | solution.py:466
  20.0 1.5 %collective-permute-start.15 = (bf16[1,64,1024]{2,1,0:T(8,128)(2,1)S(1)}, bf16[1,64,1024]{2,1,0:T(8,128)(2,1)S(1)}, u32[]{:S(2)}, u32[]{:S(2)}) collective-permute-start(bf16[1,64,1024]{2,1,0:T(8,128)(2,1)S(1)} %collective-permute-done.13.b.rest_0_), channel_id=1, source_target_pairs={{0,16},{16,0},{1,17},{17,1},{2,18},{18,2},{3,19},{19,3},{4,20},{20... | collective-permute-start | bytes 393224 | tf_op jit(solution)/shard_map/ppermute | solution.py:466
  21.5 3.8 %collective-permute-done.5.got = bf16[4,80,128]{2,1,0:T(8,128)(2,1)S(1)} collective-permute-done((bf16[4,80,128]{2,1,0:T(8,128)(2,1)S(1)}, bf16[4,80,128]{2,1,0:T(8,128)(2,1)S(1)}, u32[]{:S(2)}, u32[]{:S(2)}) %collective-permute-start.5) | collective-permute-done | bytes 81952 | tf_op jit(solution)/shard_map/ppermute | solution.py:466
  25.3 1.6 %collective-permute-start.21 = (bf16[2,64,1024]{2,1,0:T(8,128)(2,1)S(1)}, bf16[2,64,1024]{2,1,0:T(8,128)(2,1)S(1)}, u32[]{:S(2)}, u32[]{:S(2)}) collective-permute-start(bf16[2,64,1024]{2,1,0:T(8,128)(2,1)S(1)} %shard_map.92), channel_id=1, source_target_pairs={{0,2},{1,3},{2,0},{3,1},{4,6},{5,7},{6,4},{7,5},{8,10},{9,11},{10,... | collective-permute-start | bytes 786440 | tf_op jit(solution)/shard_map/ppermute | solution.py:466
  28.1 1.4 %collective-permute-start.6 = (bf16[4,80,128]{2,1,0:T(8,128)(2,1)S(1)}, bf16[4,80,128]{2,1,0:T(8,128)(2,1)S(1)}, u32[]{:S(2)}, u32[]{:S(2)}) collective-permute-start(bf16[4,80,128]{2,1,0:T(8,128)(2,1)S(1)} %get-tuple-element.45), channel_id=1, source_target_pairs={{0,4},{1,5},{2,6},{3,7},{4,0},{5,1},{6,2},{7,3},{8,12},{9,13},{10,... | collective-permute-start | bytes 245768 | tf_op jit(solution)/shard_map/ppermute | solution.py:466
  29.4 0.7 collective-permute-start.9
  30.1 3.3 %collective-permute-done.6.got = bf16[4,80,128]{2,1,0:T(8,128)(2,1)S(1)} collective-permute-done((bf16[4,80,128]{2,1,0:T(8,128)(2,1)S(1)}, bf16[4,80,128]{2,1,0:T(8,128)(2,1)S(1)}, u32[]{:S(2)}, u32[]{:S(2)}) %collective-permute-start.6) | collective-permute-done | bytes 81952 | tf_op jit(solution)/shard_map/ppermute | solution.py:466
  33.4 1.2 %shard_map.85 = (f32[4,72,128]{2,1,0:T(8,128)}, bf16[4,80,128]{2,1,0:T(8,128)(2,1)S(1)}, f32[4,72,128]{2,1,0:T(8,128)S(1)}, f32[4,8,128]{2,1,0:T(8,128)S(1)}) custom-call(s32[6]{0:T(128)S(1)} %compare_select_fusion.1.meta, f32[4,72,128]{2,1,0:T(8,128)S(1)} %get-tuple-element.44.t, bf16[4,80,128]{2,1,0:T(8,128)(2,1)S(1)} %collective-permute-done.6.got, ...), custom_call_target="tpu_custom_call" | custom-call | tf_op jit(solution)/shard_map/pallas_call | solution.py:437
  34.7 0.6 collective-permute-done.9.got
  35.3 3.2 %collective-permute-start.7 = (bf16[4,80,128]{2,1,0:T(8,128)(2,1)S(1)}, bf16[4,80,128]{2,1,0:T(8,128)(2,1)S(1)}, u32[]{:S(2)}, u32[]{:S(2)}) collective-permute-start(bf16[4,80,128]{2,1,0:T(8,128)(2,1)S(1)} %get-tuple-element.48), channel_id=1, source_target_pairs={{0,8},{1,9},{2,10},{3,11},{4,12},{5,13},{6,14},{7,15},{8,0},{9,1},... | collective-permute-start | bytes 245768 | tf_op jit(solution)/shard_map/ppermute | solution.py:466
  38.5 0.7 %shard_map.89 = (f32[4,128,128]{2,1,0:T(8,128)}, bf16[4,128,128]{2,1,0:T(8,128)(2,1)S(1)}, f32[4,128,128]{2,1,0:T(8,128)S(1)}) custom-call(f32[4,8,128]{2,1,0:T(8,128)S(1)} %get-tuple-element.54.coef, f32[4,128,128]{2,1,0:T(8,128)S(1)} %get-tuple-element.58.t, bf16[4,128,128]{2,1,0:T(8,128)(2,1)S(1)} %collective-permute-done.9.got, ...), custom_call_target="tpu_custom_call" | custom-call | tf_op jit(solution)/shard_map/pallas_call | solution.py:437
  39.3 1.5 %collective-permute-start.19 = (bf16[2,64,1024]{2,1,0:T(8,128)(2,1)S(1)}, bf16[2,64,1024]{2,1,0:T(8,128)(2,1)S(1)}, u32[]{:S(2)}, u32[]{:S(2)}) collective-permute-start(bf16[2,64,1024]{2,1,0:T(8,128)(2,1)S(1)} %collective-permute-done.17.rest_4_), channel_id=1, source_target_pairs={{0,16},{16,0},{1,17},{17,1},{2,18},{18,2},{3,19},{19,3},{4,20},{20... | collective-permute-start | bytes 786440 | tf_op jit(solution)/shard_map/ppermute | solution.py:466
  40.8 0.6 collective-permute-start.23
  41.4 3.0 %collective-permute-done.7.got = bf16[4,80,128]{2,1,0:T(8,128)(2,1)S(1)} collective-permute-done((bf16[4,80,128]{2,1,0:T(8,128)(2,1)S(1)}, bf16[4,80,128]{2,1,0:T(8,128)(2,1)S(1)}, u32[]{:S(2)}, u32[]{:S(2)}) %collective-permute-start.7) | collective-permute-done | bytes 81952 | tf_op jit(solution)/shard_map/ppermute | solution.py:466
  44.4 2.9 %collective-permute-start.27 = (bf16[2,64,1024]{2,1,0:T(8,128)(2,1)S(1)}, bf16[2,64,1024]{2,1,0:T(8,128)(2,1)S(1)}, u32[]{:S(2)}, u32[]{:S(2)}) collective-permute-start(bf16[2,64,1024]{2,1,0:T(8,128)(2,1)S(1)} %collective-permute-done.25.rest_12_), channel_id=1, source_target_pairs={{0,16},{16,0},{1,17},{17,1},{2,18},{18,2},{3,19},{19,3},{4,20},{20... | collective-permute-start | bytes 786440 | tf_op jit(solution)/shard_map/ppermute | solution.py:466
  47.4 1.2 %collective-permute-done.10.got = bf16[4,128,128]{2,1,0:T(8,128)(2,1)S(1)} collective-permute-done((bf16[4,128,128]{2,1,0:T(8,128)(2,1)S(1)}, bf16[4,128,128]{2,1,0:T(8,128)(2,1)S(1)}, u32[]{:S(2)}, u32[]{:S(2)}) %collective-permute-start.10) | collective-permute-done | bytes 131104 | tf_op jit(solution)/shard_map/ppermute | solution.py:466
  49.1 5.0 %collective-permute-done.23.rest_10_ = bf16[2,64,1024]{2,1,0:T(8,128)(2,1)S(1)} collective-permute-done((bf16[2,64,1024]{2,1,0:T(8,128)(2,1)S(1)}, bf16[2,64,1024]{2,1,0:T(8,128)(2,1)S(1)}, u32[]{:S(2)}, u32[]{:S(2)}) %collective-permute-start.23) | collective-permute-done | bytes 262176 | tf_op jit(solution)/shard_map/ppermute | solution.py:466
  54.6 3.9 %collective-permute-done.27.rest_14_ = bf16[2,64,1024]{2,1,0:T(8,128)(2,1)S(1)} collective-permute-done((bf16[2,64,1024]{2,1,0:T(8,128)(2,1)S(1)}, bf16[2,64,1024]{2,1,0:T(8,128)(2,1)S(1)}, u32[]{:S(2)}, u32[]{:S(2)}) %collective-permute-start.27) | collective-permute-done | bytes 262176 | tf_op jit(solution)/shard_map/ppermute | solution.py:466
  58.5 2.0 %shard_map.83 = (f32[8,128,128]{2,1,0:T(8,128)S(1)}, bf16[8,2,128,128]{3,2,1,0:T(8,128)(2,1)S(1)}, f32[8,128,128]{2,1,0:T(8,128)S(1)}, f32[8,128,128]{2,1,0:T(8,128)S(1)}, f32[8,128,128]{2,1,0:T(8,128)S(1)}) custom-call(s32[6]{0:T(128)S(1)} %compare_select_fusion.1.meta, f32[8]{0:T(128)S(1)} %copy-done.8, bf16[8,2,128,128]{3,2,1,0:T(8,128)(2,1)S(1)} %get-tuple-element.35.ks, ...), custom_call_target="tpu_custom_call" | custom-call | tf_op jit(solution)/shard_map/pallas_call | solution.py:437
  60.5 3.6 %shard_map.86 = (bf16[8,2,128,128]{3,2,1,0:T(8,128)(2,1)S(1)}, f32[8,128,128]{2,1,0:T(8,128)S(1)}) custom-call(s32[6]{0:T(128)S(1)} %compare_select_fusion.1.meta, f32[8,128,128]{2,1,0:T(8,128)S(1)} %get-tuple-element.40.base, f32[8,128]{1,0:T(8,128)S(1)} %copy-done.5, f32[8,128]{1,0:T(8,128)S(1)} %collective-permute-done.2.fr, ...), custom_call_target="tpu_custom_call" | custom-call | tf_op jit(solution)/shard_map/pallas_call | solution.py:437
  64.2 3.4 %shard_map.87 = (bf16[8,2,128,128]{3,2,1,0:T(8,128)(2,1)S(1)}, f32[8,128,128]{2,1,0:T(8,128)S(1)}) custom-call(s32[6]{0:T(128)S(1)} %compare_select_fusion.1.meta, f32[8]{0:T(128)S(1)} %copy-done.8, f32[8,128,128]{2,1,0:T(8,128)S(1)} %get-tuple-element.36.q_s, bf16[8,2,128,128]{3,2,1,0:T(8,128)(2,1)S(1)} %get-tuple-element.37.kt, ...), custom_call_target="tpu_custom_call" | custom-call | tf_op jit(solution)/shard_map/pallas_call | solution.py:437
  67.6 0.7 copy-done.7
  68.3 1.1 %shard_map.90 = (bf16[128,512]{1,0:T(8,128)(2,1)S(1)}, bf16[128,512]{1,0:T(8,128)(2,1)S(1)}) custom-call(s32[6]{0:T(128)S(1)} %compare_select_fusion.1.meta, bf16[8,2,128,128]{3,2,1,0:T(8,128)(2,1)S(1)} %get-tuple-element.51.xs, f32[8,128,128]{2,1,0:T(8,128)S(1)} %get-tuple-element.52.part, f32[8,128,128]{2,1,0:T(8,128)S(1)} %get-tuple-element.39.e_s, ...), custom_call_target="tpu_custom_call" | custom-call | tf_op jit(solution)/shard_map/pallas_call | solution.py:437
  70.0 1.0 %collective-permute-done.11.y_other = bf16[128,512]{1,0:T(8,128)(2,1)S(1)} collective-permute-done((bf16[128,512]{1,0:T(8,128)(2,1)S(1)}, bf16[128,512]{1,0:T(8,128)(2,1)S(1)}, u32[]{:S(2)}, u32[]{:S(2)}) %collective-permute-start.11) | collective-permute-done | bytes 131104 | tf_op jit(solution)/shard_map/ppermute | solution.py:466
  71.0 2.1 %shard_map.93 = bf16[128,2048]{1,0:T(8,128)(2,1)} custom-call(s32[6]{0:T(128)S(1)} %compare_select_fusion.1.meta, bf16[128,512]{1,0:T(8,128)(2,1)S(1)} %get-tuple-element.63.y_own, bf16[128,512]{1,0:T(8,128)(2,1)S(1)} %collective-permute-done.11.y_other, bf16[64,2048]{1,0:T(8,128)(2,1)S(1)} %copy-done.1, bf16[64,2048]{1,0:T(8,128)(2,1)S(1)} %collective-permute-done.12.other, ...), custom_call_target="tpu_custom_call" | custom-call | tf_op jit(solution)/shard_map/pallas_call | solution.py:437
  (57 shorter events, 4.6 us)
Async XLA Ops:
  0.0 15.8 %collective-permute-start.1 = (bf16[128,1024]{1,0:T(8,128)(2,1)}, bf16[128,1024]{1,0:T(8,128)(2,1)S(1)}, u32[]{:S(2)}, u32[]{:S(2)}) collective-permute-start(bf16[128,1024]{1,0:T(8,128)(2,1)} %vo.3), channel_id=1, source_target_pairs={{0,1},{1,0},{2,3},{3,2},{4,5},{5,4},{6,7},{7,6},{8,9},{9,8},{10,11... | collective-permute-start | bytes 786440 | tf_op jit(solution)/shard_map/ppermute | solution.py:466
  0.5 15.3 %collective-permute-start = (bf16[128,1024]{1,0:T(8,128)(2,1)}, bf16[128,1024]{1,0:T(8,128)(2,1)S(1)}, u32[]{:S(2)}, u32[]{:S(2)}) collective-permute-start(bf16[128,1024]{1,0:T(8,128)(2,1)} %ko.1), channel_id=1, source_target_pairs={{0,1},{1,0},{2,3},{3,2},{4,5},{5,4},{6,7},{7,6},{8,9},{9,8},{10,11... | collective-permute-start | bytes 786440 | tf_op jit(solution)/shard_map/ppermute | solution.py:466
  2.0 13.8 %copy-start.2 = (bf16[128,1024]{1,0:T(8,128)(2,1)S(1)}, bf16[128,1024]{1,0:T(8,128)(2,1)}, u32[]{:S(2)}) copy-start(bf16[128,1024]{1,0:T(8,128)(2,1)} %vo.3) | copy-start | bytes 786436
  2.0 13.8 %copy-start.4 = (bf16[128,1024]{1,0:T(8,128)(2,1)S(1)}, bf16[128,1024]{1,0:T(8,128)(2,1)}, u32[]{:S(2)}) copy-start(bf16[128,1024]{1,0:T(8,128)(2,1)} %ko.1) | copy-start | bytes 786436
  2.1 10.6 %collective-permute-start.13 = (bf16[1,64,1024]{2,1,0:T(8,128)(2,1)S(1)}, bf16[1,64,1024]{2,1,0:T(8,128)(2,1)S(1)}, u32[]{:S(2)}, u32[]{:S(2)}) collective-permute-start(bf16[1,64,1024]{2,1,0:T(8,128)(2,1)S(1)} %shard_map.91.a), channel_id=1, source_target_pairs={{0,8},{1,9},{2,10},{3,11},{4,12},{5,13},{6,14},{7,15},{8,0},{9,1},... | collective-permute-start | bytes 393224 | tf_op jit(solution)/shard_map/ppermute | solution.py:466
  6.2 15.3 %collective-permute-start.4 = (bf16[128,1024]{1,0:T(8,128)(2,1)S(1)}, bf16[128,1024]{1,0:T(8,128)(2,1)S(1)}, u32[]{:S(2)}, u32[]{:S(2)}) collective-permute-start(bf16[128,1024]{1,0:T(8,128)(2,1)S(1)} %copy-done.3), channel_id=1, source_target_pairs={{0,1},{1,0},{2,3},{3,2},{4,5},{5,4},{6,7},{7,6},{8,9},{9,8},{10,11... | collective-permute-start | bytes 786440 | tf_op jit(solution)/shard_map/ppermute | solution.py:466
  12.7 14.2 %collective-permute-start.17 = (bf16[2,64,1024]{2,1,0:T(8,128)(2,1)S(1)}, bf16[2,64,1024]{2,1,0:T(8,128)(2,1)S(1)}, u32[]{:S(2)}, u32[]{:S(2)}) collective-permute-start(bf16[2,64,1024]{2,1,0:T(8,128)(2,1)S(1)} %shard_map.92), channel_id=1, source_target_pairs={{0,4},{1,5},{2,6},{3,7},{4,0},{5,1},{6,2},{7,3},{8,12},{9,13},{10,... | collective-permute-start | bytes 786440 | tf_op jit(solution)/shard_map/ppermute | solution.py:466
  13.5 1.2 %collective-permute-start.2 = (f32[8,128]{1,0:T(8,128)S(1)}, f32[8,128]{1,0:T(8,128)S(1)}, u32[]{:S(2)}, u32[]{:S(2)}) collective-permute-start(f32[8,128]{1,0:T(8,128)S(1)} %copy-done.5), channel_id=1, source_target_pairs={{0,1},{1,0},{2,3},{3,2},{4,5},{5,4},{6,7},{7,6},{8,9},{9,8},{10,11... | collective-permute-start | bytes 12296 | tf_op jit(solution)/shard_map/ppermute | solution.py:466
  14.7 1.2 %collective-permute-start.3 = (f32[8,128]{1,0:T(8,128)S(1)}, f32[8,128]{1,0:T(8,128)S(1)}, u32[]{:S(2)}, u32[]{:S(2)}) collective-permute-start(f32[8,128]{1,0:T(8,128)S(1)} %copy-done.6), channel_id=1, source_target_pairs={{0,1},{1,0},{2,3},{3,2},{4,5},{5,4},{6,7},{7,6},{8,9},{9,8},{10,11... | collective-permute-start | bytes 12296 | tf_op jit(solution)/shard_map/ppermute | solution.py:466
  17.9 7.4 %collective-permute-start.8 = (bf16[4,128,128]{2,1,0:T(8,128)(2,1)S(1)}, bf16[4,128,128]{2,1,0:T(8,128)(2,1)S(1)}, u32[]{:S(2)}, u32[]{:S(2)}) collective-permute-start(bf16[4,128,128]{2,1,0:T(8,128)(2,1)S(1)} %get-tuple-element.57), channel_id=1, source_target_pairs={{0,2},{1,3},{2,0},{3,1},{4,6},{5,7},{6,4},{7,5},{8,10},{9,11},{10,... | collective-permute-start | bytes 393224 | tf_op jit(solution)/shard_map/ppermute | solution.py:466
  19.5 5.8 %collective-permute-start.5 = (bf16[4,80,128]{2,1,0:T(8,128)(2,1)S(1)}, bf16[4,80,128]{2,1,0:T(8,128)(2,1)S(1)}, u32[]{:S(2)}, u32[]{:S(2)}) collective-permute-start(bf16[4,80,128]{2,1,0:T(8,128)(2,1)S(1)} %get-tuple-element.43), channel_id=1, source_target_pairs={{0,2},{1,3},{2,0},{3,1},{4,6},{5,7},{6,4},{7,5},{8,10},{9,11},{10,... | collective-permute-start | bytes 245768 | tf_op jit(solution)/shard_map/ppermute | solution.py:466
  20.0 8.1 %collective-permute-start.15 = (bf16[1,64,1024]{2,1,0:T(8,128)(2,1)S(1)}, bf16[1,64,1024]{2,1,0:T(8,128)(2,1)S(1)}, u32[]{:S(2)}, u32[]{:S(2)}) collective-permute-start(bf16[1,64,1024]{2,1,0:T(8,128)(2,1)S(1)} %collective-permute-done.13.b.rest_0_), channel_id=1, source_target_pairs={{0,16},{16,0},{1,17},{17,1},{2,18},{18,2},{3,19},{19,3},{4,20},{20... | collective-permute-start | bytes 393224 | tf_op jit(solution)/shard_map/ppermute | solution.py:466
  21.5 7.9 %collective-permute-start.14 = (bf16[1,64,1024]{2,1,0:T(8,128)(2,1)S(1)}, bf16[1,64,1024]{2,1,0:T(8,128)(2,1)S(1)}, u32[]{:S(2)}, u32[]{:S(2)}) collective-permute-start(bf16[1,64,1024]{2,1,0:T(8,128)(2,1)S(1)} %collective-permute-done.13.b.rest_0_), channel_id=1, source_target_pairs={{0,1},{1,0},{2,3},{3,2},{4,5},{5,4},{6,7},{7,6},{8,9},{9,8},{10,11... | collective-permute-start | bytes 393224 | tf_op jit(solution)/shard_map/ppermute | solution.py:466
  25.3 14.0 %collective-permute-start.12 = (bf16[64,2048]{1,0:T(8,128)(2,1)S(1)}, bf16[64,2048]{1,0:T(8,128)(2,1)S(1)}, u32[]{:S(2)}, u32[]{:S(2)}) collective-permute-start(bf16[64,2048]{1,0:T(8,128)(2,1)S(1)} %copy-done.1), channel_id=1, source_target_pairs={{0,1},{1,0},{2,3},{3,2},{4,5},{5,4},{6,7},{7,6},{8,9},{9,8},{10,11... | collective-permute-start | bytes 786440 | tf_op jit(solution)/shard_map/ppermute | solution.py:466
  25.3 15.5 %collective-permute-start.21 = (bf16[2,64,1024]{2,1,0:T(8,128)(2,1)S(1)}, bf16[2,64,1024]{2,1,0:T(8,128)(2,1)S(1)}, u32[]{:S(2)}, u32[]{:S(2)}) collective-permute-start(bf16[2,64,1024]{2,1,0:T(8,128)(2,1)S(1)} %shard_map.92), channel_id=1, source_target_pairs={{0,2},{1,3},{2,0},{3,1},{4,6},{5,7},{6,4},{7,5},{8,10},{9,11},{10,... | collective-permute-start | bytes 786440 | tf_op jit(solution)/shard_map/ppermute | solution.py:466
  26.9 17.6 %collective-permute-start.25 = (bf16[2,64,1024]{2,1,0:T(8,128)(2,1)S(1)}, bf16[2,64,1024]{2,1,0:T(8,128)(2,1)S(1)}, u32[]{:S(2)}, u32[]{:S(2)}) collective-permute-start(bf16[2,64,1024]{2,1,0:T(8,128)(2,1)S(1)} %collective-permute-done.17.rest_4_), channel_id=1, source_target_pairs={{0,2},{1,3},{2,0},{3,1},{4,6},{5,7},{6,4},{7,5},{8,10},{9,11},{10,... | collective-permute-start | bytes 786440 | tf_op jit(solution)/shard_map/ppermute | solution.py:466
  28.1 5.4 %collective-permute-start.6 = (bf16[4,80,128]{2,1,0:T(8,128)(2,1)S(1)}, bf16[4,80,128]{2,1,0:T(8,128)(2,1)S(1)}, u32[]{:S(2)}, u32[]{:S(2)}) collective-permute-start(bf16[4,80,128]{2,1,0:T(8,128)(2,1)S(1)} %get-tuple-element.45), channel_id=1, source_target_pairs={{0,4},{1,5},{2,6},{3,7},{4,0},{5,1},{6,2},{7,3},{8,12},{9,13},{10,... | collective-permute-start | bytes 245768 | tf_op jit(solution)/shard_map/ppermute | solution.py:466
  29.4 5.9 %collective-permute-start.9 = (bf16[4,128,128]{2,1,0:T(8,128)(2,1)S(1)}, bf16[4,128,128]{2,1,0:T(8,128)(2,1)S(1)}, u32[]{:S(2)}, u32[]{:S(2)}) collective-permute-start(bf16[4,128,128]{2,1,0:T(8,128)(2,1)S(1)} %get-tuple-element.59), channel_id=1, source_target_pairs={{0,4},{1,5},{2,6},{3,7},{4,0},{5,1},{6,2},{7,3},{8,12},{9,13},{10,... | collective-permute-start | bytes 393224 | tf_op jit(solution)/shard_map/ppermute | solution.py:466
  33.4 7.4 %collective-permute-start.16 = (bf16[1,64,1024]{2,1,0:T(8,128)(2,1)S(1)}, bf16[1,64,1024]{2,1,0:T(8,128)(2,1)S(1)}, u32[]{:S(2)}, u32[]{:S(2)}) collective-permute-start(bf16[1,64,1024]{2,1,0:T(8,128)(2,1)S(1)} %collective-permute-done.15.rest_2_), channel_id=1, source_target_pairs={{0,1},{1,0},{2,3},{3,2},{4,5},{5,4},{6,7},{7,6},{8,9},{9,8},{10,11... | collective-permute-start | bytes 393224 | tf_op jit(solution)/shard_map/ppermute | solution.py:466
  35.3 9.1 %collective-permute-start.7 = (bf16[4,80,128]{2,1,0:T(8,128)(2,1)S(1)}, bf16[4,80,128]{2,1,0:T(8,128)(2,1)S(1)}, u32[]{:S(2)}, u32[]{:S(2)}) collective-permute-start(bf16[4,80,128]{2,1,0:T(8,128)(2,1)S(1)} %get-tuple-element.48), channel_id=1, source_target_pairs={{0,8},{1,9},{2,10},{3,11},{4,12},{5,13},{6,14},{7,15},{8,0},{9,1},... | collective-permute-start | bytes 245768 | tf_op jit(solution)/shard_map/ppermute | solution.py:466
  39.3 9.3 %collective-permute-start.19 = (bf16[2,64,1024]{2,1,0:T(8,128)(2,1)S(1)}, bf16[2,64,1024]{2,1,0:T(8,128)(2,1)S(1)}, u32[]{:S(2)}, u32[]{:S(2)}) collective-permute-start(bf16[2,64,1024]{2,1,0:T(8,128)(2,1)S(1)} %collective-permute-done.17.rest_4_), channel_id=1, source_target_pairs={{0,16},{16,0},{1,17},{17,1},{2,18},{18,2},{3,19},{19,3},{4,20},{20... | collective-permute-start | bytes 786440 | tf_op jit(solution)/shard_map/ppermute | solution.py:466
  40.8 17.7 %copy-start.8 = (f32[8]{0:T(128)S(1)}, f32[8]{0:T(128)}, u32[]{:S(2)}) copy-start(f32[8]{0:T(128)} %ridge.3) | copy-start | bytes 100
  40.8 7.8 %collective-permute-start.10 = (bf16[4,128,128]{2,1,0:T(8,128)(2,1)S(1)}, bf16[4,128,128]{2,1,0:T(8,128)(2,1)S(1)}, u32[]{:S(2)}, u32[]{:S(2)}) collective-permute-start(bf16[4,128,128]{2,1,0:T(8,128)(2,1)S(1)} %get-tuple-element.62), channel_id=1, source_target_pairs={{0,8},{1,9},{2,10},{3,11},{4,12},{5,13},{6,14},{7,15},{8,0},{9,1},... | collective-permute-start | bytes 393224 | tf_op jit(solution)/shard_map/ppermute | solution.py:466
  40.8 13.3 %collective-permute-start.23 = (bf16[2,64,1024]{2,1,0:T(8,128)(2,1)S(1)}, bf16[2,64,1024]{2,1,0:T(8,128)(2,1)S(1)}, u32[]{:S(2)}, u32[]{:S(2)}) collective-permute-start(bf16[2,64,1024]{2,1,0:T(8,128)(2,1)S(1)} %collective-permute-done.21.rest_8_), channel_id=1, source_target_pairs={{0,16},{16,0},{1,17},{17,1},{2,18},{18,2},{3,19},{19,3},{4,20},{20... | collective-permute-start | bytes 786440 | tf_op jit(solution)/shard_map/ppermute | solution.py:466
  44.4 9.7 %collective-permute-start.18 = (bf16[2,64,1024]{2,1,0:T(8,128)(2,1)S(1)}, bf16[2,64,1024]{2,1,0:T(8,128)(2,1)S(1)}, u32[]{:S(2)}, u32[]{:S(2)}) collective-permute-start(bf16[2,64,1024]{2,1,0:T(8,128)(2,1)S(1)} %collective-permute-done.17.rest_4_), channel_id=1, source_target_pairs={{0,1},{1,0},{2,3},{3,2},{4,5},{5,4},{6,7},{7,6},{8,9},{9,8},{10,11... | collective-permute-start | bytes 786440 | tf_op jit(solution)/shard_map/ppermute | solution.py:466
  44.4 14.0 %collective-permute-start.27 = (bf16[2,64,1024]{2,1,0:T(8,128)(2,1)S(1)}, bf16[2,64,1024]{2,1,0:T(8,128)(2,1)S(1)}, u32[]{:S(2)}, u32[]{:S(2)}) collective-permute-start(bf16[2,64,1024]{2,1,0:T(8,128)(2,1)S(1)} %collective-permute-done.25.rest_12_), channel_id=1, source_target_pairs={{0,16},{16,0},{1,17},{17,1},{2,18},{18,2},{3,19},{19,3},{4,20},{20... | collective-permute-start | bytes 786440 | tf_op jit(solution)/shard_map/ppermute | solution.py:466
  48.5 20.8 %collective-permute-start.22 = (bf16[2,64,1024]{2,1,0:T(8,128)(2,1)S(1)}, bf16[2,64,1024]{2,1,0:T(8,128)(2,1)S(1)}, u32[]{:S(2)}, u32[]{:S(2)}) collective-permute-start(bf16[2,64,1024]{2,1,0:T(8,128)(2,1)S(1)} %collective-permute-done.21.rest_8_), channel_id=1, source_target_pairs={{0,1},{1,0},{2,3},{3,2},{4,5},{5,4},{6,7},{7,6},{8,9},{9,8},{10,11... | collective-permute-start | bytes 786440 | tf_op jit(solution)/shard_map/ppermute | solution.py:466
  48.6 22.4 %collective-permute-start.26 = (bf16[2,64,1024]{2,1,0:T(8,128)(2,1)S(1)}, bf16[2,64,1024]{2,1,0:T(8,128)(2,1)S(1)}, u32[]{:S(2)}, u32[]{:S(2)}) collective-permute-start(bf16[2,64,1024]{2,1,0:T(8,128)(2,1)S(1)} %collective-permute-done.25.rest_12_), channel_id=1, source_target_pairs={{0,1},{1,0},{2,3},{3,2},{4,5},{5,4},{6,7},{7,6},{8,9},{9,8},{10,11... | collective-permute-start | bytes 786440 | tf_op jit(solution)/shard_map/ppermute | solution.py:466
  54.1 16.9 %collective-permute-start.20 = (bf16[2,64,1024]{2,1,0:T(8,128)(2,1)S(1)}, bf16[2,64,1024]{2,1,0:T(8,128)(2,1)S(1)}, u32[]{:S(2)}, u32[]{:S(2)}) collective-permute-start(bf16[2,64,1024]{2,1,0:T(8,128)(2,1)S(1)} %collective-permute-done.19.rest_6_), channel_id=1, source_target_pairs={{0,1},{1,0},{2,3},{3,2},{4,5},{5,4},{6,7},{7,6},{8,9},{9,8},{10,11... | collective-permute-start | bytes 786440 | tf_op jit(solution)/shard_map/ppermute | solution.py:466
  54.1 16.9 %collective-permute-start.24 = (bf16[2,64,1024]{2,1,0:T(8,128)(2,1)S(1)}, bf16[2,64,1024]{2,1,0:T(8,128)(2,1)S(1)}, u32[]{:S(2)}, u32[]{:S(2)}) collective-permute-start(bf16[2,64,1024]{2,1,0:T(8,128)(2,1)S(1)} %collective-permute-done.23.rest_10_), channel_id=1, source_target_pairs={{0,1},{1,0},{2,3},{3,2},{4,5},{5,4},{6,7},{7,6},{8,9},{9,8},{10,11... | collective-permute-start | bytes 786440 | tf_op jit(solution)/shard_map/ppermute | solution.py:466
  58.5 12.5 %collective-permute-start.28 = (bf16[2,64,1024]{2,1,0:T(8,128)(2,1)S(1)}, bf16[2,64,1024]{2,1,0:T(8,128)(2,1)S(1)}, u32[]{:S(2)}, u32[]{:S(2)}) collective-permute-start(bf16[2,64,1024]{2,1,0:T(8,128)(2,1)S(1)} %collective-permute-done.27.rest_14_), channel_id=1, source_target_pairs={{0,1},{1,0},{2,3},{3,2},{4,5},{5,4},{6,7},{7,6},{8,9},{9,8},{10,11... | collective-permute-start | bytes 786440 | tf_op jit(solution)/shard_map/ppermute | solution.py:466
  69.4 1.6 %collective-permute-start.11 = (bf16[128,512]{1,0:T(8,128)(2,1)S(1)}, bf16[128,512]{1,0:T(8,128)(2,1)S(1)}, u32[]{:S(2)}, u32[]{:S(2)}) collective-permute-start(bf16[128,512]{1,0:T(8,128)(2,1)S(1)} %get-tuple-element.64), channel_id=1, source_target_pairs={{0,1},{1,0},{2,3},{3,2},{4,5},{5,4},{6,7},{7,6},{8,9},{9,8},{10,11... | collective-permute-start | bytes 393224 | tf_op jit(solution)/shard_map/ppermute | solution.py:466
  (6 other events, 44.2 us)
where the time goes:
time: 73.3 us; the launch traced here: 73.1 us
  waiting for transfers between devices  30.5 us (42%)
  starting transfers between devices  23.2 us (32%)
  Pallas kernels  17.6 us (24%)
  local copies, waits for them, and re-layouts  1.67 us (2%)
    ppermute x29, waiting for transfers between devices, swap(): return lax.ppermute(array, axis, [(i, i ^ distance) for i in range(count)])  30.5 us
    ppermute x29, starting transfers between devices, swap(): return lax.ppermute(array, axis, [(i, i ^ distance) for i in range(count)])  23.2 us
    pallas_call x12, Pallas kernels, call(): pl.pallas_call(kernel, out_shape=outs, in_specs=[pl.BlockSpec(memory_spac...  17.6 us
    unnamed x18, local copies, waits for them, and re-layouts  1.67 us
  transfers between devices with their start and end apart: 29, of which 11 were waited for; matrix products, arithmetic and copies ran while one was open for 0% of the time, Pallas kernels for 21%

commit v1 on v0

--- a/solution.py
+++ b/solution.py
@@ -109,9 +109,11 @@
     return out.astype(BF16)
 
 
-def sums_kernel(meta, ko, kr, vo, vr, fo, fr, go, gr, pg, tg, pw, tw, gf, uf, ks):
+def sums_kernel(meta, ko, kr, vr, fo, fr, go, gr, values, pg, tg, pw, tw, gf, uf, ks, vo, sem):
     half = gf.shape[0]
     width = gf.shape[1]
+    fetch = pltpu.make_async_copy(values, vo, sem)
+    fetch.start()
     body = width // 2
     core = meta[0]
     forget = gates(fo, fr, core, half)
@@ -121,42 +123,48 @@
     tails = (jnp.exp(last - level) * beta).T
     decay = jnp.exp(last)
     first = core == 0
+    weighted = {}
     for h in range(half):
-        grams, states = [], []
-        for side, (kref, vref) in enumerate(((ko, vo), (kr, vr))):
+        grams = []
+        for side, kref in enumerate((ko, kr)):
             p = h + side * half
             k = unit_rows(columns(kref, core, h, half, width).astype(F32))
             tk = split(k * tails[:, p : p + 1])
             kk = split(k)
             ks[p, 0], ks[p, 1] = kk
-            v = columns(vref, core, h, half, width)
+            weighted[p] = jnp.concatenate(tk, axis=0)
             grams.append(
                 dot_t(jnp.concatenate([tk[0], tk[1], tk[0]], axis=0), jnp.concatenate([kk[0], kk[0], kk[1]], axis=0))
             )
-            states.append(dot_t(jnp.concatenate([tk[0], tk[1]], axis=0), jnp.concatenate([v, v], axis=0)))
         early = pick(first, grams[0], grams[1])
         late = pick(first, grams[1], grams[0])
-        early_state = pick(first, states[0], states[1])
-        late_state = pick(first, states[1], states[0])
         shrink = pick(first, decay[half + h : half + h + 1], decay[h : h + 1])
         gf[h] = early
-        uf[h] = early_state
         packed, diag = pack(shrink * early + late)
         total = jnp.broadcast_to(last[h : h + 1] + last[half + h : half + h + 1], (1, width))
         tg[h, :body] = packed
         tg[h, body:] = tail_rows(diag, total)
         pg[h, :body] = packed.astype(BF16)
         pg[h, body:] = tail_sent(diag, total)
+    fetch.wait()
+    for h in range(half):
+        states = []
+        for side, vref in enumerate((vo, vr)):
+            v = columns(vref, core, h, half, width)
+            states.append(dot_t(weighted[h + side * half], jnp.concatenate([v, v], axis=0)))
+        early_state = pick(first, states[0], states[1])
+        late_state = pick(first, states[1], states[0])
+        shrink = pick(first, decay[half + h : half + h + 1], decay[h : h + 1])
+        uf[h] = early_state
         state = shrink * early_state + late_state
         tw[h] = state
         pw[h] = state.astype(BF16)
 
 
-def join_kernel(which, has_prefix, meta, t, got, *rest):
-    if has_prefix:
-        before, t_new, sent, before_new, coef = rest
-    else:
-        t_new, sent, before_new, coef = rest
+def join_kernel(which, has_prefix, goes_on, meta, t, got, *rest):
+    sent, before_new, coef = rest[has_prefix : has_prefix + 3]
+    before = rest[0]
+    t_new = rest[-1]
     bit = meta[which] == 1
     half, rows, width = t.shape
     body = rows - 8
@@ -170,8 +178,9 @@
         arrived = got[h, :body].astype(F32)
         packed = a * t[h, :body] + b * arrived
         diag = a * tail[:1] + b * ends[:1]
-        t_new[h, :body] = packed
-        t_new[h, body:] = tail_rows(diag, mine + theirs)
+        if goes_on:
+            t_new[h, :body] = packed
+            t_new[h, body:] = tail_rows(diag, mine + theirs)
         sent[h, :body] = packed.astype(BF16)
         sent[h, body:] = tail_sent(diag, mine + theirs)
         if has_prefix:
@@ -187,16 +196,16 @@
         coef[h] = jnp.where(r == 0, a, jnp.where(r == 1, b, jnp.where(r == 2, e, 0.0)))
 
 
-def join_state_kernel(has_prefix, coef, t, got, *rest):
-    if has_prefix:
-        before, t_new, sent, before_new = rest
-    else:
-        t_new, sent, before_new = rest
+def join_state_kernel(has_prefix, goes_on, coef, t, got, *rest):
+    sent, before_new = rest[has_prefix : has_prefix + 2]
+    before = rest[0]
+    t_new = rest[-1]
     for h in range(t.shape[0]):
         c = coef[h]
         arrived = got[h].astype(F32)
         new = c[0:1] * t[h] + c[1:2] * arrived
-        t_new[h] = new
+        if goes_on:
+            t_new[h] = new
         sent[h] = new.astype(BF16)
         add = c[2:3] * arrived
         before_new[h] = before[h] + add if has_prefix else add
@@ -323,7 +332,9 @@
             part[p] = dot(jnp.concatenate([sh, sl], axis=1), jnp.concatenate([v, v], axis=0))
 
 
-def read_kernel(which, meta, xs, part, e_s, fo, fr, uf, before_g, before, got, gain, y_own, y_other):
+def read_kernel(which, meta, xs, part, e_s, fo, fr, uf, before_g, before, got, far_gain, y_own, y_other, gain, sem):
+    fetch = pltpu.make_async_copy(far_gain, gain, sem)
+    fetch.start()
     half = uf.shape[0]
     width = uf.shape[1]
     body = width // 2
@@ -332,25 +343,30 @@
     bit = meta[which] == 1
     decay = jnp.exp(jnp.sum(gates(fo, fr, core, half), axis=1, keepdims=True))
     sides = ((y_own, first), (y_other, jnp.logical_not(first)))
+    normed = {}
     for h in range(half):
-        cols = slice(h * width, (h + 1) * width)
         e = jnp.where(bit, jnp.exp(before_g[h, body + 1 : body + 2]), 0.0)
         start = before[h] + e * got[h].astype(F32)
-        scale = columns(gain, core, h, half, width)
-        for side, (out, is_early) in enumerate(sides):
+        for side, (_, is_early) in enumerate(sides):
             p = h + side * half
             other = h + (1 - side) * half
             state = jnp.where(is_early, start, decay[other : other + 1] * start + uf[h])
             read = dot(wide((xs[p, 0], xs[p, 1])), tall(split(state)))
             o = e_s[p] * read + part[p]
-            o = o * lax.rsqrt(jnp.mean(o * o, axis=-1, keepdims=True) + 1e-6)
-            out[:, cols] = (o * scale).astype(BF16)
-
-
-def share_kernel(meta, w, out):
+            normed[p] = o * lax.rsqrt(jnp.mean(o * o, axis=-1, keepdims=True) + 1e-6)
+    fetch.wait()
+    for h in range(half):
+        scale = columns(gain, core, h, half, width)
+        for side, (out, _) in enumerate(sides):
+            out[:, h * width : (h + 1) * width] = (normed[h + side * half] * scale).astype(BF16)
+
+
+def share_kernel(meta, w, out, sem):
     size = out.shape[2]
     share = meta[meta.shape[0] - 1]
-    out[0] = w[:, pl.ds(pl.multiple_of(share * size, size), size)]
+    fetch = pltpu.make_async_copy(w.at[:, pl.ds(pl.multiple_of(share * size, size), size)], out.at[0], sem)
+    fetch.start()
+    fetch.wait()
 
 
 def stack_kernel(a, b, out):
@@ -365,15 +381,14 @@
     y[:, pl.ds(pl.multiple_of((1 - core) * size, size), size)] = y_other[...]
 
 
-def project_kernel(table, chips, meta, y_own, y_other, own, other, *rest):
+def project_kernel(table, chips, shares, meta, y_own, y_other, own, other, *rest):
     out, y = rest[-2:]
     core = meta[0]
     place = meta[meta.shape[0] - 2]
     share = meta[meta.shape[0] - 1]
     gathered_rows(meta, y_own, y_other, y)
     width = 2 * own.shape[0]
-    shares = own.shape[1] // rest[0].shape[2]
-    size = rest[0].shape[2]
+    size = own.shape[1] // shares
     tokens = y.shape[0]
     lefts = []
     for offset in range(chips):
@@ -390,6 +405,8 @@
                 for flip in (0, 1):
                     if o == 0:
                         blocks.append((own, other)[flip][:, where])
+                    elif (o, flip, None) in table:
+                        blocks.append(rest[table[o, flip, None][0]][:, where])
                     else:
                         piece, i = table[o, flip, q]
                         blocks.append(rest[piece][i])
@@ -431,17 +448,19 @@
 SMEM = pltpu.SMEM
 
 
-def call(kernel, outs, scalars, ins, scratch=()):
+def call(kernel, outs, scalars, ins, scratch=(), far=()):
     spec = pl.BlockSpec(memory_space=VMEM)
     near = [pltpu.with_memory_space_constraint(a, VMEM) for a in ins]
     return pl.pallas_call(
         kernel,
         out_shape=outs,
-        in_specs=[pl.BlockSpec(memory_space=SMEM)] * len(scalars) + [spec] * len(near),
+        in_specs=[pl.BlockSpec(memory_space=SMEM)] * len(scalars)
+        + [spec] * len(near)
+        + [pl.BlockSpec(memory_space=pl.ANY)] * len(far),
         out_specs=jax.tree.map(lambda _: spec, outs),
         scratch_shapes=scratch,
         compiler_params=pltpu.CompilerParams(vmem_limit_bytes=GRANT),
-    )(*scalars, *near)
+    )(*scalars, *near, *far)
 
 
 def on_device(mesh, queries, keys, values, log_forget, input_gate, ridge, gain, out_weight):
@@ -482,46 +501,66 @@
         (VMEM(sent, BF16), VMEM(packed, F32), VMEM(full, BF16), VMEM(full, F32), VMEM(full, F32), VMEM(full, F32),
          VMEM(two, BF16)),
         (meta,),
-        (keys, keys_o, values, values_o, *gate_args),
+        (keys, keys_o, values_o, *gate_args),
+        (VMEM(values.shape, BF16), pltpu.SemaphoreType.DMA),
+        (values,),
     )
 
     before = before_w = None
+    tg, tw = (tg,), (tw,)
     for r in range(bits):
         got = swap(pg, 2 << r)
         got_w = swap(pw, 2 << r)
         if r == bits - 1:
             break
         extra = () if before is None else (before,)
-        tg, pg, before, coef = call(
-            functools.partial(join_kernel, r + 1, bool(extra)),
-            (VMEM(packed, F32), VMEM(sent, BF16), VMEM(packed, F32), VMEM((half, 8, width), F32)),
+        goes_on = r < bits - 2
+        pg, before, coef, *tg = call(
+            functools.partial(join_kernel, r + 1, len(extra), goes_on),
+            (VMEM(sent, BF16), VMEM(packed, F32), VMEM((half, 8, width), F32), *[VMEM(packed, F32)] * goes_on),
             (meta,),
-            (tg, got, *extra),
+            (*tg, got, *extra),
         )
         extra = () if before_w is None else (before_w,)
-        tw, pw, before_w = call(
-            functools.partial(join_state_kernel, bool(extra)),
-            (VMEM(full, F32), VMEM(full, BF16), VMEM(full, F32)),
+        pw, before_w, *tw = call(
+            functools.partial(join_state_kernel, len(extra), goes_on),
+            (VMEM(full, BF16), VMEM(full, F32), *[VMEM(full, F32)] * goes_on),
             (),
-            (coef, tw, got_w, *extra),
+            (coef, *tw, got_w, *extra),
         )
     last = bits
 
     size = out_columns // parts
-    own = call(share_kernel, VMEM((1, rows, size), BF16), (meta,), (out_weight,))
+    own = call(share_kernel, VMEM((1, rows, size), BF16), (meta,), (), (pltpu.SemaphoreType.DMA,), (out_weight,))
+
+    def stack(a, b):
+        return call(stack_kernel, VMEM((a.shape[0] + b.shape[0], rows, size), BF16), (), (a, b))
+
+    table, pieces = {}, []
+
+    def keep(offsets, q, array, flip):
+        for i, offset in enumerate(offsets):
+            table[offset, flip, q] = (len(pieces), i)
+        pieces.append(array)
+
     groups = []
-    held = ((0,), own)
-    for bit in reversed(range(1, bits)):
-        fresh = (tuple(o ^ (1 << bit) for o in held[0]), swap(held[1], 2 << bit))
-        groups.append(fresh)
-        if bit > 1:
-            held = (
-                held[0] + fresh[0],
-                call(stack_kernel, VMEM((2 * len(held[0]), rows, size), BF16), (), (held[1], fresh[1])),
-            )
-    groups.append((tuple(o ^ 1 for o in held[0]), swap(held[1], 2)))
-    groups.append((tuple(o ^ 1 for o in fresh[0]), swap(fresh[1], 2)))
-    table, pieces = {}, []
+    if bits == 3:
+        far, mid = swap(own, 8), swap(own, 4)
+        farther = swap(far, 4)
+        near = swap(out_weight, 2)
+        both = stack(far, mid)
+        groups.append(((4, 2), both))
+        groups.append(((5, 3), swap(both, 2)))
+        groups.append(((6, 7), stack(farther, swap(farther, 2))))
+        keep((1,), None, near, 0)
+        keep((1,), None, swap(near, 1), 1)
+    else:
+        held = ((0,), own)
+        for bit in reversed(range(bits)):
+            fresh = (tuple(o ^ (1 << bit) for o in held[0]), swap(held[1], 2 << bit))
+            groups.append(fresh)
+            if bit:
+                held = (held[0] + fresh[0], stack(held[1], fresh[1]))
     for offsets, array in groups:
         shares = [(0, array)]
         step = 1
@@ -529,10 +568,8 @@
             shares += [(q ^ step, swap(a, step, "parts")) for q, a in shares]
             step *= 2
         for q, a in shares:
-            for flip, b in ((0, a), (1, swap(a, 1))):
-                for i, offset in enumerate(offsets):
-                    table[offset, flip, q] = (len(pieces), i)
-                pieces.append(b)
+            keep(offsets, q, a, 0)
+            keep(offsets, q, swap(a, 1), 1)
     weight_o = swap(out_weight, 1)
 
     q_s, kt, m_s, e_s, base = call(
@@ -559,26 +596,28 @@
         functools.partial(read_kernel, last),
         (VMEM((tokens, half * width), BF16),) * 2,
         (meta,),
-        (xs, part, e_s, *forgets, uf, before, before_w, got_w, gain.reshape(1, features)),
+        (xs, part, e_s, *forgets, uf, before, before_w, got_w),
+        (VMEM((1, features), F32), pltpu.SemaphoreType.DMA),
+        (gain.reshape(1, features),),
     )
     y_got = swap(y_other, 1)
 
     result = jax.ShapeDtypeStruct((tokens, out_columns), BF16)
     y_full = VMEM((tokens, features), BF16)
-    if 2 * rows == width:
+    if bits == 3 and 2 * rows == width:
         return call(
-            functools.partial(project_kernel, table, chips),
+            functools.partial(project_kernel, table, chips, parts),
             result,
             (meta,),
             (y_own, y_got, out_weight, weight_o, *pieces),
             (y_full,),
         )
-    near = pl.BlockSpec(memory_space=VMEM)
+    here = pl.BlockSpec(memory_space=VMEM)
     return pl.pallas_call(
         functools.partial(project_copy_kernel, table),
         out_shape=result,
-        in_specs=[pl.BlockSpec(memory_space=SMEM), near, near] + [pl.BlockSpec(memory_space=pl.ANY)] * (2 + len(pieces)),
-        out_specs=near,
+        in_specs=[pl.BlockSpec(memory_space=SMEM), here, here] + [pl.BlockSpec(memory_space=pl.ANY)] * (2 + len(pieces)),
+        out_specs=here,
         scratch_shapes=[
             VMEM((features, out_columns), BF16), y_full, pltpu.SemaphoreType.DMA((2 + len(table),))
         ],

time: 73.3 us -> 67.9 us (0.926)
  waiting for transfers between devices: 30.5 us -> 24 us
  starting transfers between devices: 23.2 us -> 24.1 us
    ppermute x29, waiting for transfers between devices: 30.5 us -> 24 us  [swap(): return lax.ppermute(array, axis, [(i, i ^ distance) for i in range(count)])]
    ppermute x29, starting transfers between devices: 23.2 us -> 24.1 us  [swap(): return lax.ppermute(array, axis, [(i, i ^ distance) for i in range(count)])]
    pallas_call x12 -> x13, Pallas kernels: 17.6 us -> 17.8 us  [call(): pl.pallas_call(kernel, out_shape=outs, in_specs=[pl.BlockSpec(memory_spac...]
    unnamed x18 -> x14, local copies, waits for them, and re-layouts: 1.67 us -> 1.65 us
  transfers between devices with their start and end apart: 29 -> 29, of which waited for: 11 -> 10; matrix products, arithmetic and copies ran while one was open for 0% -> 0% of each run, Pallas kernels for 21% -> 23%
where the time goes in v1:
time: 67.9 us; the launch traced here: 67.7 us
  starting transfers between devices  24.1 us (35%)
  waiting for transfers between devices  24 us (35%)
  Pallas kernels  17.8 us (26%)
  local copies, waits for them, and re-layouts  1.65 us (2%)
    ppermute x29, starting transfers between devices, swap(): return lax.ppermute(array, axis, [(i, i ^ distance) for i in range(count)])  24.1 us
    ppermute x29, waiting for transfers between devices, swap(): return lax.ppermute(array, axis, [(i, i ^ distance) for i in range(count)])  24 us
    pallas_call x13, Pallas kernels, call(): pl.pallas_call(kernel, out_shape=outs, in_specs=[pl.BlockSpec(memory_spac...  17.8 us
    unnamed x14, local copies, waits for them, and re-layouts  1.65 us
  transfers between devices with their start and end apart: 29, of which 10 were waited for; matrix products, arithmetic and copies ran while one was open for 0% of the time, Pallas kernels for 23%

profile of v1, /device:TPU:0, one launch (start us, length us, event | category | flops | bytes accessed | tf_op | source)
XLA Modules:
  0.0 67.7 jit_solution(12874462386583932796)
XLA Ops:
  0.6 1.5 %shard_map.91 = bf16[1,64,1024]{2,1,0:T(8,128)(2,1)S(1)} custom-call(s32[6]{0:T(128)S(1)} %compare_select_fusion.1.meta, bf16[64,2048]{1,0:T(8,128)(2,1)} %own.1), custom_call_target="tpu_custom_call" | custom-call | tf_op jit(solution)/shard_map/pallas_call | solution.py:454
  2.0 4.1 %collective-permute-start.15 = (bf16[1,64,1024]{2,1,0:T(8,128)(2,1)S(1)}, bf16[1,64,1024]{2,1,0:T(8,128)(2,1)S(1)}, u32[]{:S(2)}, u32[]{:S(2)}) collective-permute-start(bf16[1,64,1024]{2,1,0:T(8,128)(2,1)S(1)} %shard_map.91), channel_id=1, source_target_pairs={{0,8},{1,9},{2,10},{3,11},{4,12},{5,13},{6,14},{7,15},{8,0},{9,1},... | collective-permute-start | bytes 393224 | tf_op jit(solution)/shard_map/ppermute | solution.py:485
  7.5 1.5 %collective-permute-start.13 = (bf16[64,2048]{1,0:T(8,128)(2,1)}, bf16[64,2048]{1,0:T(8,128)(2,1)S(1)}, u32[]{:S(2)}, u32[]{:S(2)}) collective-permute-start(bf16[64,2048]{1,0:T(8,128)(2,1)} %own.1), channel_id=1, source_target_pairs={{0,2},{1,3},{2,0},{3,1},{4,6},{5,7},{6,4},{7,5},{8,10},{9,11},{10,... | collective-permute-start | bytes 786440 | tf_op jit(solution)/shard_map/ppermute | solution.py:485
  9.0 3.7 %collective-permute-done.15.a = bf16[1,64,1024]{2,1,0:T(8,128)(2,1)S(1)} collective-permute-done((bf16[1,64,1024]{2,1,0:T(8,128)(2,1)S(1)}, bf16[1,64,1024]{2,1,0:T(8,128)(2,1)S(1)}, u32[]{:S(2)}, u32[]{:S(2)}) %collective-permute-start.15) | collective-permute-done | bytes 131104 | tf_op jit(solution)/shard_map/ppermute | solution.py:485
  12.7 0.7 %collective-permute-start.16 = (bf16[1,64,1024]{2,1,0:T(8,128)(2,1)S(1)}, bf16[1,64,1024]{2,1,0:T(8,128)(2,1)S(1)}, u32[]{:S(2)}, u32[]{:S(2)}) collective-permute-start(bf16[1,64,1024]{2,1,0:T(8,128)(2,1)S(1)} %shard_map.91), channel_id=1, source_target_pairs={{0,4},{1,5},{2,6},{3,7},{4,0},{5,1},{6,2},{7,3},{8,12},{9,13},{10,... | collective-permute-start | bytes 393224 | tf_op jit(solution)/shard_map/ppermute | solution.py:485
  13.4 1.3 %collective-permute-start.24 = (bf16[1,64,1024]{2,1,0:T(8,128)(2,1)S(1)}, bf16[1,64,1024]{2,1,0:T(8,128)(2,1)S(1)}, u32[]{:S(2)}, u32[]{:S(2)}) collective-permute-start(bf16[1,64,1024]{2,1,0:T(8,128)(2,1)S(1)} %collective-permute-done.15.a), channel_id=1, source_target_pairs={{0,4},{1,5},{2,6},{3,7},{4,0},{5,1},{6,2},{7,3},{8,12},{9,13},{10,... | collective-permute-start | bytes 393224 | tf_op jit(solution)/shard_map/ppermute | solution.py:485
  14.7 0.9 %copy-done.2 = bf16[128,1024]{1,0:T(8,128)(2,1)S(1)} copy-done((bf16[128,1024]{1,0:T(8,128)(2,1)S(1)}, bf16[128,1024]{1,0:T(8,128)(2,1)}, u32[]{:S(2)}) %copy-start.2) | copy-done | bytes 262168
  15.7 2.3 %shard_map.82 = (bf16[4,80,128]{2,1,0:T(8,128)(2,1)S(1)}, f32[4,72,128]{2,1,0:T(8,128)S(1)}, bf16[4,128,128]{2,1,0:T(8,128)(2,1)S(1)}, f32[4,128,128]{2,1,0:T(8,...) custom-call(s32[6]{0:T(128)S(1)} %compare_select_fusion.1.meta, ...), custom_call_target="tpu_custom_call" | custom-call | tf_op jit(solution)/shard_map/pallas_call | solution.py:454
  17.9 1.0 %collective-permute-done.16.b = bf16[1,64,1024]{2,1,0:T(8,128)(2,1)S(1)} collective-permute-done((bf16[1,64,1024]{2,1,0:T(8,128)(2,1)S(1)}, bf16[1,64,1024]{2,1,0:T(8,128)(2,1)S(1)}, u32[]{:S(2)}, u32[]{:S(2)}) %collective-permute-start.16) | collective-permute-done | bytes 131104 | tf_op jit(solution)/shard_map/ppermute | solution.py:485
  18.9 1.3 %collective-permute-start.5 = (bf16[4,80,128]{2,1,0:T(8,128)(2,1)S(1)}, bf16[4,80,128]{2,1,0:T(8,128)(2,1)S(1)}, u32[]{:S(2)}, u32[]{:S(2)}) collective-permute-start(bf16[4,80,128]{2,1,0:T(8,128)(2,1)S(1)} %get-tuple-element.43), channel_id=1, source_target_pairs={{0,2},{1,3},{2,0},{3,1},{4,6},{5,7},{6,4},{7,5},{8,10},{9,11},{10,... | collective-permute-start | bytes 245768 | tf_op jit(solution)/shard_map/ppermute | solution.py:485
  20.3 0.8 %collective-permute-start.8 = (bf16[4,128,128]{2,1,0:T(8,128)(2,1)S(1)}, bf16[4,128,128]{2,1,0:T(8,128)(2,1)S(1)}, u32[]{:S(2)}, u32[]{:S(2)}) collective-permute-start(bf16[4,128,128]{2,1,0:T(8,128)(2,1)S(1)} %get-tuple-element.57), channel_id=1, source_target_pairs={{0,2},{1,3},{2,0},{3,1},{4,6},{5,7},{6,4},{7,5},{8,10},{9,11},{10,... | collective-permute-start | bytes 393224 | tf_op jit(solution)/shard_map/ppermute | solution.py:485
  21.1 1.3 %collective-permute-start.20 = (bf16[2,64,1024]{2,1,0:T(8,128)(2,1)S(1)}, bf16[2,64,1024]{2,1,0:T(8,128)(2,1)S(1)}, u32[]{:S(2)}, u32[]{:S(2)}) collective-permute-start(bf16[2,64,1024]{2,1,0:T(8,128)(2,1)S(1)} %shard_map.92.rest_2_), channel_id=1, source_target_pairs={{0,2},{1,3},{2,0},{3,1},{4,6},{5,7},{6,4},{7,5},{8,10},{9,11},{10,... | collective-permute-start | bytes 786440 | tf_op jit(solution)/shard_map/ppermute | solution.py:485
  22.4 1.5 %collective-permute-start.18 = (bf16[2,64,1024]{2,1,0:T(8,128)(2,1)S(1)}, bf16[2,64,1024]{2,1,0:T(8,128)(2,1)S(1)}, u32[]{:S(2)}, u32[]{:S(2)}) collective-permute-start(bf16[2,64,1024]{2,1,0:T(8,128)(2,1)S(1)} %shard_map.92.rest_2_), channel_id=1, source_target_pairs={{0,16},{16,0},{1,17},{17,1},{2,18},{18,2},{3,19},{19,3},{4,20},{20... | collective-permute-start | bytes 786440 | tf_op jit(solution)/shard_map/ppermute | solution.py:485
  24.3 1.3 %collective-permute-start.25 = (bf16[1,64,1024]{2,1,0:T(8,128)(2,1)S(1)}, bf16[1,64,1024]{2,1,0:T(8,128)(2,1)S(1)}, u32[]{:S(2)}, u32[]{:S(2)}) collective-permute-start(bf16[1,64,1024]{2,1,0:T(8,128)(2,1)S(1)} %collective-permute-done.24.a), channel_id=1, source_target_pairs={{0,2},{1,3},{2,0},{3,1},{4,6},{5,7},{6,4},{7,5},{8,10},{9,11},{10,... | collective-permute-start | bytes 393224 | tf_op jit(solution)/shard_map/ppermute | solution.py:485
  25.6 1.5 %collective-permute-done.8.got = bf16[4,128,128]{2,1,0:T(8,128)(2,1)S(1)} collective-permute-done((bf16[4,128,128]{2,1,0:T(8,128)(2,1)S(1)}, bf16[4,128,128]{2,1,0:T(8,128)(2,1)S(1)}, u32[]{:S(2)}, u32[]{:S(2)}) %collective-permute-start.8) | collective-permute-done | bytes 131104 | tf_op jit(solution)/shard_map/ppermute | solution.py:485
  27.8 0.9 %collective-permute-start.9 = (bf16[4,128,128]{2,1,0:T(8,128)(2,1)S(1)}, bf16[4,128,128]{2,1,0:T(8,128)(2,1)S(1)}, u32[]{:S(2)}, u32[]{:S(2)}) collective-permute-start(bf16[4,128,128]{2,1,0:T(8,128)(2,1)S(1)} %get-tuple-element.59), channel_id=1, source_target_pairs={{0,4},{1,5},{2,6},{3,7},{4,0},{5,1},{6,2},{7,3},{8,12},{9,13},{10,... | collective-permute-start | bytes 393224 | tf_op jit(solution)/shard_map/ppermute | solution.py:485
  28.6 6.0 %collective-permute-done.25.b = bf16[1,64,1024]{2,1,0:T(8,128)(2,1)S(1)} collective-permute-done((bf16[1,64,1024]{2,1,0:T(8,128)(2,1)S(1)}, bf16[1,64,1024]{2,1,0:T(8,128)(2,1)S(1)}, u32[]{:S(2)}, u32[]{:S(2)}) %collective-permute-start.25) | collective-permute-done | bytes 131104 | tf_op jit(solution)/shard_map/ppermute | solution.py:485
  34.6 0.7 collective-permute-start.6
  35.3 1.6 %collective-permute-start.27 = (bf16[2,64,1024]{2,1,0:T(8,128)(2,1)S(1)}, bf16[2,64,1024]{2,1,0:T(8,128)(2,1)S(1)}, u32[]{:S(2)}, u32[]{:S(2)}) collective-permute-start(bf16[2,64,1024]{2,1,0:T(8,128)(2,1)S(1)} %shard_map.93.rest_10_), channel_id=1, source_target_pairs={{0,16},{16,0},{1,17},{17,1},{2,18},{18,2},{3,19},{19,3},{4,20},{20... | collective-permute-start | bytes 786440 | tf_op jit(solution)/shard_map/ppermute | solution.py:485
  36.9 2.2 %collective-permute-done.6.got = bf16[4,80,128]{2,1,0:T(8,128)(2,1)S(1)} collective-permute-done((bf16[4,80,128]{2,1,0:T(8,128)(2,1)S(1)}, bf16[4,80,128]{2,1,0:T(8,128)(2,1)S(1)}, u32[]{:S(2)}, u32[]{:S(2)}) %collective-permute-start.6) | collective-permute-done | bytes 81952 | tf_op jit(solution)/shard_map/ppermute | solution.py:485
  39.0 1.3 %collective-permute-start.22 = (bf16[2,64,1024]{2,1,0:T(8,128)(2,1)S(1)}, bf16[2,64,1024]{2,1,0:T(8,128)(2,1)S(1)}, u32[]{:S(2)}, u32[]{:S(2)}) collective-permute-start(bf16[2,64,1024]{2,1,0:T(8,128)(2,1)S(1)} %collective-permute-done.20.rest_6_), channel_id=1, source_target_pairs={{0,16},{16,0},{1,17},{17,1},{2,18},{18,2},{3,19},{19,3},{4,20},{20... | collective-permute-start | bytes 786440 | tf_op jit(solution)/shard_map/ppermute | solution.py:485
  41.0 2.4 %collective-permute-start.7 = (bf16[4,80,128]{2,1,0:T(8,128)(2,1)S(1)}, bf16[4,80,128]{2,1,0:T(8,128)(2,1)S(1)}, u32[]{:S(2)}, u32[]{:S(2)}) collective-permute-start(bf16[4,80,128]{2,1,0:T(8,128)(2,1)S(1)} %get-tuple-element.48), channel_id=1, source_target_pairs={{0,8},{1,9},{2,10},{3,11},{4,12},{5,13},{6,14},{7,15},{8,0},{9,1},... | collective-permute-start | bytes 245768 | tf_op jit(solution)/shard_map/ppermute | solution.py:485
  43.4 0.7 %collective-permute-start.10 = (bf16[4,128,128]{2,1,0:T(8,128)(2,1)S(1)}, bf16[4,128,128]{2,1,0:T(8,128)(2,1)S(1)}, u32[]{:S(2)}, u32[]{:S(2)}) collective-permute-start(bf16[4,128,128]{2,1,0:T(8,128)(2,1)S(1)} %get-tuple-element.62), channel_id=1, source_target_pairs={{0,8},{1,9},{2,10},{3,11},{4,12},{5,13},{6,14},{7,15},{8,0},{9,1},... | collective-permute-start | bytes 393224 | tf_op jit(solution)/shard_map/ppermute | solution.py:485
  44.1 5.3 %collective-permute-done.7.got = bf16[4,80,128]{2,1,0:T(8,128)(2,1)S(1)} collective-permute-done((bf16[4,80,128]{2,1,0:T(8,128)(2,1)S(1)}, bf16[4,80,128]{2,1,0:T(8,128)(2,1)S(1)}, u32[]{:S(2)}, u32[]{:S(2)}) %collective-permute-start.7) | collective-permute-done | bytes 81952 | tf_op jit(solution)/shard_map/ppermute | solution.py:485
  49.9 2.3 %collective-permute-done.10.got = bf16[4,128,128]{2,1,0:T(8,128)(2,1)S(1)} collective-permute-done((bf16[4,128,128]{2,1,0:T(8,128)(2,1)S(1)}, bf16[4,128,128]{2,1,0:T(8,128)(2,1)S(1)}, u32[]{:S(2)}, u32[]{:S(2)}) %collective-permute-start.10) | collective-permute-done | bytes 131104 | tf_op jit(solution)/shard_map/ppermute | solution.py:485
  52.8 2.0 %shard_map.83 = (f32[8,128,128]{2,1,0:T(8,128)S(1)}, bf16[8,2,128,128]{3,2,1,0:T(8,128)(2,1)S(1)}, f32[8,128,128]{2,1,0:T(8,128)S(1)}, f32[8,128,128]{2,1,0:T(8,128)S(1)}, f32[8,128,128]{2,1,0:T(8,128)S(1)}) custom-call(s32[6]{0:T(128)S(1)} %compare_select_fusion.1.meta, f32[8]{0:T(128)S(1)} %copy-done.6, bf16[8,2,128,128]{3,2,1,0:T(8,128)(2,1)S(1)} %get-tuple-element.35.ks, ...), custom_call_target="tpu_custom_call" | custom-call | tf_op jit(solution)/shard_map/pallas_call | solution.py:454
  54.8 3.6 %shard_map.86 = (bf16[8,2,128,128]{3,2,1,0:T(8,128)(2,1)S(1)}, f32[8,128,128]{2,1,0:T(8,128)S(1)}) custom-call(s32[6]{0:T(128)S(1)} %compare_select_fusion.1.meta, f32[8,128,128]{2,1,0:T(8,128)S(1)} %get-tuple-element.40.base, f32[8,128]{1,0:T(8,128)S(1)} %copy-done.3, f32[8,128]{1,0:T(8,128)S(1)} %collective-permute-done.2.fr, ...), custom_call_target="tpu_custom_call" | custom-call | tf_op jit(solution)/shard_map/pallas_call | solution.py:454
  58.4 3.4 %shard_map.87 = (bf16[8,2,128,128]{3,2,1,0:T(8,128)(2,1)S(1)}, f32[8,128,128]{2,1,0:T(8,128)S(1)}) custom-call(s32[6]{0:T(128)S(1)} %compare_select_fusion.1.meta, f32[8]{0:T(128)S(1)} %copy-done.6, f32[8,128,128]{2,1,0:T(8,128)S(1)} %get-tuple-element.36.q_s, bf16[8,2,128,128]{3,2,1,0:T(8,128)(2,1)S(1)} %get-tuple-element.37.kt, ...), custom_call_target="tpu_custom_call" | custom-call | tf_op jit(solution)/shard_map/pallas_call | solution.py:454
  61.8 0.7 %copy-done.5 = f32[1024]{0:T(1024)S(1)} copy-done((f32[1024]{0:T(1024)S(1)}, f32[1024]{0:T(1024)}, u32[]{:S(2)}) %copy-start.5) | copy-done | bytes 4120
  62.5 1.2 %shard_map.90 = (bf16[128,512]{1,0:T(8,128)(2,1)S(1)}, bf16[128,512]{1,0:T(8,128)(2,1)S(1)}) custom-call(s32[6]{0:T(128)S(1)} %compare_select_fusion.1.meta, bf16[8,2,128,128]{3,2,1,0:T(8,128)(2,1)S(1)} %get-tuple-element.51.xs, f32[8,128,128]{2,1,0:T(8,128)S(1)} %get-tuple-element.52.part, f32[8,128,128]{2,1,0:T(8,128)S(1)} %get-tuple-element.39.e_s, ...), custom_call_target="tpu_custom_call" | custom-call | tf_op jit(solution)/shard_map/pallas_call | solution.py:454
  64.2 1.0 %collective-permute-done.11.y_other = bf16[128,512]{1,0:T(8,128)(2,1)S(1)} collective-permute-done((bf16[128,512]{1,0:T(8,128)(2,1)S(1)}, bf16[128,512]{1,0:T(8,128)(2,1)S(1)}, u32[]{:S(2)}, u32[]{:S(2)}) %collective-permute-start.11) | collective-permute-done | bytes 131104 | tf_op jit(solution)/shard_map/ppermute | solution.py:485
  65.1 2.6 %shard_map.94 = bf16[128,2048]{1,0:T(8,128)(2,1)} custom-call(s32[6]{0:T(128)S(1)} %compare_select_fusion.1.meta, bf16[128,512]{1,0:T(8,128)(2,1)S(1)} %get-tuple-element.63.y_own, bf16[128,512]{1,0:T(8,128)(2,1)S(1)} %collective-permute-done.11.y_other, bf16[64,2048]{1,0:T(8,128)(2,1)} %own.1, bf16[64,2048]{1,0:T(8,128)(2,1)S(1)} %collective-permute-done.12.other, ...), custom_call_target="tpu_custom_call" | custom-call | tf_op jit(solution)/shard_map/pallas_call | solution.py:454
  (54 shorter events, 5.3 us)
Async XLA Ops:
  0.0 14.7 %copy-start = (bf16[128,1024]{1,0:T(8,128)(2,1)S(1)}, bf16[128,1024]{1,0:T(8,128)(2,1)}, u32[]{:S(2)}) copy-start(bf16[128,1024]{1,0:T(8,128)(2,1)} %vo.1) | copy-start | bytes 786436
  0.0 13.4 %collective-permute-start.1 = (bf16[128,1024]{1,0:T(8,128)(2,1)}, bf16[128,1024]{1,0:T(8,128)(2,1)S(1)}, u32[]{:S(2)}, u32[]{:S(2)}) collective-permute-start(bf16[128,1024]{1,0:T(8,128)(2,1)} %vo.1), channel_id=1, source_target_pairs={{0,1},{1,0},{2,3},{3,2},{4,5},{5,4},{6,7},{7,6},{8,9},{9,8},{10,11... | collective-permute-start | bytes 786440 | tf_op jit(solution)/shard_map/ppermute | solution.py:485
  0.5 14.2 %collective-permute-start = (bf16[128,1024]{1,0:T(8,128)(2,1)}, bf16[128,1024]{1,0:T(8,128)(2,1)S(1)}, u32[]{:S(2)}, u32[]{:S(2)}) collective-permute-start(bf16[128,1024]{1,0:T(8,128)(2,1)} %ko.1), channel_id=1, source_target_pairs={{0,1},{1,0},{2,3},{3,2},{4,5},{5,4},{6,7},{7,6},{8,9},{9,8},{10,11... | collective-permute-start | bytes 786440 | tf_op jit(solution)/shard_map/ppermute | solution.py:485
  2.0 10.6 %collective-permute-start.15 = (bf16[1,64,1024]{2,1,0:T(8,128)(2,1)S(1)}, bf16[1,64,1024]{2,1,0:T(8,128)(2,1)S(1)}, u32[]{:S(2)}, u32[]{:S(2)}) collective-permute-start(bf16[1,64,1024]{2,1,0:T(8,128)(2,1)S(1)} %shard_map.91), channel_id=1, source_target_pairs={{0,8},{1,9},{2,10},{3,11},{4,12},{5,13},{6,14},{7,15},{8,0},{9,1},... | collective-permute-start | bytes 393224 | tf_op jit(solution)/shard_map/ppermute | solution.py:485
  6.1 1.2 %collective-permute-start.2 = (f32[8,128]{1,0:T(8,128)S(1)}, f32[8,128]{1,0:T(8,128)S(1)}, u32[]{:S(2)}, u32[]{:S(2)}) collective-permute-start(f32[8,128]{1,0:T(8,128)S(1)} %copy-done.3), channel_id=1, source_target_pairs={{0,1},{1,0},{2,3},{3,2},{4,5},{5,4},{6,7},{7,6},{8,9},{9,8},{10,11... | collective-permute-start | bytes 12296 | tf_op jit(solution)/shard_map/ppermute | solution.py:485
  6.1 1.3 %collective-permute-start.3 = (f32[8,128]{1,0:T(8,128)S(1)}, f32[8,128]{1,0:T(8,128)S(1)}, u32[]{:S(2)}, u32[]{:S(2)}) collective-permute-start(f32[8,128]{1,0:T(8,128)S(1)} %copy-done.4), channel_id=1, source_target_pairs={{0,1},{1,0},{2,3},{3,2},{4,5},{5,4},{6,7},{7,6},{8,9},{9,8},{10,11... | collective-permute-start | bytes 12296 | tf_op jit(solution)/shard_map/ppermute | solution.py:485
  7.3 13.0 %collective-permute-start.4 = (bf16[128,1024]{1,0:T(8,128)(2,1)}, bf16[128,1024]{1,0:T(8,128)(2,1)S(1)}, u32[]{:S(2)}, u32[]{:S(2)}) collective-permute-start(bf16[128,1024]{1,0:T(8,128)(2,1)} %qo.1), channel_id=1, source_target_pairs={{0,1},{1,0},{2,3},{3,2},{4,5},{5,4},{6,7},{7,6},{8,9},{9,8},{10,11... | collective-permute-start | bytes 786440 | tf_op jit(solution)/shard_map/ppermute | solution.py:485
  7.5 14.9 %collective-permute-start.13 = (bf16[64,2048]{1,0:T(8,128)(2,1)}, bf16[64,2048]{1,0:T(8,128)(2,1)S(1)}, u32[]{:S(2)}, u32[]{:S(2)}) collective-permute-start(bf16[64,2048]{1,0:T(8,128)(2,1)} %own.1), channel_id=1, source_target_pairs={{0,2},{1,3},{2,0},{3,1},{4,6},{5,7},{6,4},{7,5},{8,10},{9,11},{10,... | collective-permute-start | bytes 786440 | tf_op jit(solution)/shard_map/ppermute | solution.py:485
  12.7 6.3 %collective-permute-start.16 = (bf16[1,64,1024]{2,1,0:T(8,128)(2,1)S(1)}, bf16[1,64,1024]{2,1,0:T(8,128)(2,1)S(1)}, u32[]{:S(2)}, u32[]{:S(2)}) collective-permute-start(bf16[1,64,1024]{2,1,0:T(8,128)(2,1)S(1)} %shard_map.91), channel_id=1, source_target_pairs={{0,4},{1,5},{2,6},{3,7},{4,0},{5,1},{6,2},{7,3},{8,12},{9,13},{10,... | collective-permute-start | bytes 393224 | tf_op jit(solution)/shard_map/ppermute | solution.py:485
  13.4 7.7 %collective-permute-start.24 = (bf16[1,64,1024]{2,1,0:T(8,128)(2,1)S(1)}, bf16[1,64,1024]{2,1,0:T(8,128)(2,1)S(1)}, u32[]{:S(2)}, u32[]{:S(2)}) collective-permute-start(bf16[1,64,1024]{2,1,0:T(8,128)(2,1)S(1)} %collective-permute-done.15.a), channel_id=1, source_target_pairs={{0,4},{1,5},{2,6},{3,7},{4,0},{5,1},{6,2},{7,3},{8,12},{9,13},{10,... | collective-permute-start | bytes 393224 | tf_op jit(solution)/shard_map/ppermute | solution.py:485
  14.7 13.1 %collective-permute-start.12 = (bf16[64,2048]{1,0:T(8,128)(2,1)}, bf16[64,2048]{1,0:T(8,128)(2,1)S(1)}, u32[]{:S(2)}, u32[]{:S(2)}) collective-permute-start(bf16[64,2048]{1,0:T(8,128)(2,1)} %own.1), channel_id=1, source_target_pairs={{0,1},{1,0},{2,3},{3,2},{4,5},{5,4},{6,7},{7,6},{8,9},{9,8},{10,11... | collective-permute-start | bytes 786440 | tf_op jit(solution)/shard_map/ppermute | solution.py:485
  18.9 5.3 %collective-permute-start.5 = (bf16[4,80,128]{2,1,0:T(8,128)(2,1)S(1)}, bf16[4,80,128]{2,1,0:T(8,128)(2,1)S(1)}, u32[]{:S(2)}, u32[]{:S(2)}) collective-permute-start(bf16[4,80,128]{2,1,0:T(8,128)(2,1)S(1)} %get-tuple-element.43), channel_id=1, source_target_pairs={{0,2},{1,3},{2,0},{3,1},{4,6},{5,7},{6,4},{7,5},{8,10},{9,11},{10,... | collective-permute-start | bytes 245768 | tf_op jit(solution)/shard_map/ppermute | solution.py:485
  20.3 6.8 %collective-permute-start.8 = (bf16[4,128,128]{2,1,0:T(8,128)(2,1)S(1)}, bf16[4,128,128]{2,1,0:T(8,128)(2,1)S(1)}, u32[]{:S(2)}, u32[]{:S(2)}) collective-permute-start(bf16[4,128,128]{2,1,0:T(8,128)(2,1)S(1)} %get-tuple-element.57), channel_id=1, source_target_pairs={{0,2},{1,3},{2,0},{3,1},{4,6},{5,7},{6,4},{7,5},{8,10},{9,11},{10,... | collective-permute-start | bytes 393224 | tf_op jit(solution)/shard_map/ppermute | solution.py:485
  21.1 14.2 %collective-permute-start.20 = (bf16[2,64,1024]{2,1,0:T(8,128)(2,1)S(1)}, bf16[2,64,1024]{2,1,0:T(8,128)(2,1)S(1)}, u32[]{:S(2)}, u32[]{:S(2)}) collective-permute-start(bf16[2,64,1024]{2,1,0:T(8,128)(2,1)S(1)} %shard_map.92.rest_2_), channel_id=1, source_target_pairs={{0,2},{1,3},{2,0},{3,1},{4,6},{5,7},{6,4},{7,5},{8,10},{9,11},{10,... | collective-permute-start | bytes 786440 | tf_op jit(solution)/shard_map/ppermute | solution.py:485
  22.4 12.9 %collective-permute-start.18 = (bf16[2,64,1024]{2,1,0:T(8,128)(2,1)S(1)}, bf16[2,64,1024]{2,1,0:T(8,128)(2,1)S(1)}, u32[]{:S(2)}, u32[]{:S(2)}) collective-permute-start(bf16[2,64,1024]{2,1,0:T(8,128)(2,1)S(1)} %shard_map.92.rest_2_), channel_id=1, source_target_pairs={{0,16},{16,0},{1,17},{17,1},{2,18},{18,2},{3,19},{19,3},{4,20},{20... | collective-permute-start | bytes 786440 | tf_op jit(solution)/shard_map/ppermute | solution.py:485
  24.3 10.3 %collective-permute-start.25 = (bf16[1,64,1024]{2,1,0:T(8,128)(2,1)S(1)}, bf16[1,64,1024]{2,1,0:T(8,128)(2,1)S(1)}, u32[]{:S(2)}, u32[]{:S(2)}) collective-permute-start(bf16[1,64,1024]{2,1,0:T(8,128)(2,1)S(1)} %collective-permute-done.24.a), channel_id=1, source_target_pairs={{0,2},{1,3},{2,0},{3,1},{4,6},{5,7},{6,4},{7,5},{8,10},{9,11},{10,... | collective-permute-start | bytes 393224 | tf_op jit(solution)/shard_map/ppermute | solution.py:485
  27.1 16.3 %collective-permute-start.17 = (bf16[2,64,1024]{2,1,0:T(8,128)(2,1)S(1)}, bf16[2,64,1024]{2,1,0:T(8,128)(2,1)S(1)}, u32[]{:S(2)}, u32[]{:S(2)}) collective-permute-start(bf16[2,64,1024]{2,1,0:T(8,128)(2,1)S(1)} %shard_map.92.rest_2_), channel_id=1, source_target_pairs={{0,1},{1,0},{2,3},{3,2},{4,5},{5,4},{6,7},{7,6},{8,9},{9,8},{10,11... | collective-permute-start | bytes 786440 | tf_op jit(solution)/shard_map/ppermute | solution.py:485
  27.8 13.2 %collective-permute-start.9 = (bf16[4,128,128]{2,1,0:T(8,128)(2,1)S(1)}, bf16[4,128,128]{2,1,0:T(8,128)(2,1)S(1)}, u32[]{:S(2)}, u32[]{:S(2)}) collective-permute-start(bf16[4,128,128]{2,1,0:T(8,128)(2,1)S(1)} %get-tuple-element.59), channel_id=1, source_target_pairs={{0,4},{1,5},{2,6},{3,7},{4,0},{5,1},{6,2},{7,3},{8,12},{9,13},{10,... | collective-permute-start | bytes 393224 | tf_op jit(solution)/shard_map/ppermute | solution.py:485
  34.6 4.4 %collective-permute-start.6 = (bf16[4,80,128]{2,1,0:T(8,128)(2,1)S(1)}, bf16[4,80,128]{2,1,0:T(8,128)(2,1)S(1)}, u32[]{:S(2)}, u32[]{:S(2)}) collective-permute-start(bf16[4,80,128]{2,1,0:T(8,128)(2,1)S(1)} %get-tuple-element.45), channel_id=1, source_target_pairs={{0,4},{1,5},{2,6},{3,7},{4,0},{5,1},{6,2},{7,3},{8,12},{9,13},{10,... | collective-permute-start | bytes 245768 | tf_op jit(solution)/shard_map/ppermute | solution.py:485
  35.3 14.1 %collective-permute-start.14 = (bf16[64,2048]{1,0:T(8,128)(2,1)S(1)}, bf16[64,2048]{1,0:T(8,128)(2,1)S(1)}, u32[]{:S(2)}, u32[]{:S(2)}) collective-permute-start(bf16[64,2048]{1,0:T(8,128)(2,1)S(1)} %collective-permute-done.13.rest_0_), channel_id=1, source_target_pairs={{0,1},{1,0},{2,3},{3,2},{4,5},{5,4},{6,7},{7,6},{8,9},{9,8},{10,11... | collective-permute-start | bytes 786440 | tf_op jit(solution)/shard_map/ppermute | solution.py:485
  35.3 16.9 %collective-permute-start.27 = (bf16[2,64,1024]{2,1,0:T(8,128)(2,1)S(1)}, bf16[2,64,1024]{2,1,0:T(8,128)(2,1)S(1)}, u32[]{:S(2)}, u32[]{:S(2)}) collective-permute-start(bf16[2,64,1024]{2,1,0:T(8,128)(2,1)S(1)} %shard_map.93.rest_10_), channel_id=1, source_target_pairs={{0,16},{16,0},{1,17},{17,1},{2,18},{18,2},{3,19},{19,3},{4,20},{20... | collective-permute-start | bytes 786440 | tf_op jit(solution)/shard_map/ppermute | solution.py:485
  39.0 13.6 %collective-permute-start.22 = (bf16[2,64,1024]{2,1,0:T(8,128)(2,1)S(1)}, bf16[2,64,1024]{2,1,0:T(8,128)(2,1)S(1)}, u32[]{:S(2)}, u32[]{:S(2)}) collective-permute-start(bf16[2,64,1024]{2,1,0:T(8,128)(2,1)S(1)} %collective-permute-done.20.rest_6_), channel_id=1, source_target_pairs={{0,16},{16,0},{1,17},{17,1},{2,18},{18,2},{3,19},{19,3},{4,20},{20... | collective-permute-start | bytes 786440 | tf_op jit(solution)/shard_map/ppermute | solution.py:485
  41.0 8.4 %collective-permute-start.7 = (bf16[4,80,128]{2,1,0:T(8,128)(2,1)S(1)}, bf16[4,80,128]{2,1,0:T(8,128)(2,1)S(1)}, u32[]{:S(2)}, u32[]{:S(2)}) collective-permute-start(bf16[4,80,128]{2,1,0:T(8,128)(2,1)S(1)} %get-tuple-element.48), channel_id=1, source_target_pairs={{0,8},{1,9},{2,10},{3,11},{4,12},{5,13},{6,14},{7,15},{8,0},{9,1},... | collective-permute-start | bytes 245768 | tf_op jit(solution)/shard_map/ppermute | solution.py:485
  43.3 9.4 %copy-start.1 = (bf16[128,1024]{1,0:T(8,128)(2,1)S(1)}, bf16[128,1024]{1,0:T(8,128)(2,1)}, u32[]{:S(2)}) copy-start(bf16[128,1024]{1,0:T(8,128)(2,1)} %qo.1) | copy-start | bytes 786436
  43.4 9.4 %copy-start.6 = (f32[8]{0:T(128)S(1)}, f32[8]{0:T(128)}, u32[]{:S(2)}) copy-start(f32[8]{0:T(128)} %ridge.3) | copy-start | bytes 100
  43.4 8.8 %collective-permute-start.10 = (bf16[4,128,128]{2,1,0:T(8,128)(2,1)S(1)}, bf16[4,128,128]{2,1,0:T(8,128)(2,1)S(1)}, u32[]{:S(2)}, u32[]{:S(2)}) collective-permute-start(bf16[4,128,128]{2,1,0:T(8,128)(2,1)S(1)} %get-tuple-element.62), channel_id=1, source_target_pairs={{0,8},{1,9},{2,10},{3,11},{4,12},{5,13},{6,14},{7,15},{8,0},{9,1},... | collective-permute-start | bytes 393224 | tf_op jit(solution)/shard_map/ppermute | solution.py:485
  49.4 14.3 %collective-permute-start.26 = (bf16[2,64,1024]{2,1,0:T(8,128)(2,1)S(1)}, bf16[2,64,1024]{2,1,0:T(8,128)(2,1)S(1)}, u32[]{:S(2)}, u32[]{:S(2)}) collective-permute-start(bf16[2,64,1024]{2,1,0:T(8,128)(2,1)S(1)} %shard_map.93.rest_10_), channel_id=1, source_target_pairs={{0,1},{1,0},{2,3},{3,2},{4,5},{5,4},{6,7},{7,6},{8,9},{9,8},{10,11... | collective-permute-start | bytes 786440 | tf_op jit(solution)/shard_map/ppermute | solution.py:485
  49.4 14.8 %collective-permute-start.21 = (bf16[2,64,1024]{2,1,0:T(8,128)(2,1)S(1)}, bf16[2,64,1024]{2,1,0:T(8,128)(2,1)S(1)}, u32[]{:S(2)}, u32[]{:S(2)}) collective-permute-start(bf16[2,64,1024]{2,1,0:T(8,128)(2,1)S(1)} %collective-permute-done.20.rest_6_), channel_id=1, source_target_pairs={{0,1},{1,0},{2,3},{3,2},{4,5},{5,4},{6,7},{7,6},{8,9},{9,8},{10,11... | collective-permute-start | bytes 786440 | tf_op jit(solution)/shard_map/ppermute | solution.py:485
  52.2 12.0 %collective-permute-start.19 = (bf16[2,64,1024]{2,1,0:T(8,128)(2,1)S(1)}, bf16[2,64,1024]{2,1,0:T(8,128)(2,1)S(1)}, u32[]{:S(2)}, u32[]{:S(2)}) collective-permute-start(bf16[2,64,1024]{2,1,0:T(8,128)(2,1)S(1)} %collective-permute-done.18.rest_4_), channel_id=1, source_target_pairs={{0,1},{1,0},{2,3},{3,2},{4,5},{5,4},{6,7},{7,6},{8,9},{9,8},{10,11... | collective-permute-start | bytes 786440 | tf_op jit(solution)/shard_map/ppermute | solution.py:485
  52.2 13.0 %collective-permute-start.28 = (bf16[2,64,1024]{2,1,0:T(8,128)(2,1)S(1)}, bf16[2,64,1024]{2,1,0:T(8,128)(2,1)S(1)}, u32[]{:S(2)}, u32[]{:S(2)}) collective-permute-start(bf16[2,64,1024]{2,1,0:T(8,128)(2,1)S(1)} %collective-permute-done.27.rest_12_), channel_id=1, source_target_pairs={{0,1},{1,0},{2,3},{3,2},{4,5},{5,4},{6,7},{7,6},{8,9},{9,8},{10,11... | collective-permute-start | bytes 786440 | tf_op jit(solution)/shard_map/ppermute | solution.py:485
  52.7 12.5 %collective-permute-start.23 = (bf16[2,64,1024]{2,1,0:T(8,128)(2,1)S(1)}, bf16[2,64,1024]{2,1,0:T(8,128)(2,1)S(1)}, u32[]{:S(2)}, u32[]{:S(2)}) collective-permute-start(bf16[2,64,1024]{2,1,0:T(8,128)(2,1)S(1)} %collective-permute-done.22.rest_8_), channel_id=1, source_target_pairs={{0,1},{1,0},{2,3},{3,2},{4,5},{5,4},{6,7},{7,6},{8,9},{9,8},{10,11... | collective-permute-start | bytes 786440 | tf_op jit(solution)/shard_map/ppermute | solution.py:485
  63.6 1.5 %collective-permute-start.11 = (bf16[128,512]{1,0:T(8,128)(2,1)S(1)}, bf16[128,512]{1,0:T(8,128)(2,1)S(1)}, u32[]{:S(2)}, u32[]{:S(2)}) collective-permute-start(bf16[128,512]{1,0:T(8,128)(2,1)S(1)} %get-tuple-element.64), channel_id=1, source_target_pairs={{0,1},{1,0},{2,3},{3,2},{4,5},{5,4},{6,7},{7,6},{8,9},{9,8},{10,11... | collective-permute-start | bytes 393224 | tf_op jit(solution)/shard_map/ppermute | solution.py:485
  (4 other events, 12.8 us)

commit v2 on v1

--- a/solution.py
+++ b/solution.py
@@ -32,10 +32,6 @@
     return jnp.dot(a, b, preferred_element_type=F32)
 
 
-def dot_t(a, b):
-    return lax.dot_general(a, b, (((0,), (0,)), ((), ())), preferred_element_type=F32)
-
-
 def wide(pair):
     high, low = pair
     return jnp.concatenate([high, low, high], axis=1)
@@ -55,6 +51,8 @@
 
 
 def columns(ref, core, h, half, width):
+    if ref.shape[1] == half * width:
+        return ref[:, h * width : (h + 1) * width]
     return ref[:, pl.ds(pl.multiple_of((core * half + h) * width, width), width)]
 
 
@@ -67,6 +65,10 @@
         ],
         axis=0,
     )
+
+
+def ridge_of(row, core, h, half):
+    return jnp.where(core == 0, row[:, h : h + 1], row[:, half + h : half + h + 1])
 
 
 def running_sum(a):
@@ -109,18 +111,35 @@
     return out.astype(BF16)
 
 
-def sums_kernel(meta, ko, kr, vr, fo, fr, go, gr, values, pg, tg, pw, tw, gf, uf, ks, vo, sem):
+def load_kernel(meta, *refs):
+    count = (len(refs) - 1) // 2
+    sources, outs, sem = refs[:count], refs[count : 2 * count], refs[-1]
+    copies = []
+    for i, (source, out) in enumerate(zip(sources, outs)):
+        if len(out.shape) == 3:
+            size = out.shape[2]
+            share = meta[meta.shape[0] - 1]
+            source, out = source.at[:, pl.ds(pl.multiple_of(share * size, size), size)], out.at[0]
+        elif out.shape[1] < source.shape[1]:
+            size = out.shape[1]
+            source = source.at[:, pl.ds(pl.multiple_of(meta[0] * size, size), size)]
+        copies.append(pltpu.make_async_copy(source, out, sem.at[i]))
+    for copy in copies:
+        copy.start()
+    for copy in copies:
+        copy.wait()
+
+
+def sums_kernel(meta, ko, kr, vo, vr, fo, fr, go, gr, pg, tg, pw, tw, gf, uf, ks, kt):
     half = gf.shape[0]
     width = gf.shape[1]
-    fetch = pltpu.make_async_copy(values, vo, sem)
-    fetch.start()
     body = width // 2
     core = meta[0]
     forget = gates(fo, fr, core, half)
     beta = gates(go, gr, core, half)
     level = running_sum(forget)
     last = level[:, width - 1 :]
-    tails = (jnp.exp(last - level) * beta).T
+    tails = jnp.exp(last - level) * beta
     decay = jnp.exp(last)
     first = core == 0
     weighted = {}
@@ -129,13 +148,12 @@
         for side, kref in enumerate((ko, kr)):
             p = h + side * half
             k = unit_rows(columns(kref, core, h, half, width).astype(F32))
-            tk = split(k * tails[:, p : p + 1])
+            turned = k.T
             kk = split(k)
             ks[p, 0], ks[p, 1] = kk
-            weighted[p] = jnp.concatenate(tk, axis=0)
-            grams.append(
-                dot_t(jnp.concatenate([tk[0], tk[1], tk[0]], axis=0), jnp.concatenate([kk[0], kk[0], kk[1]], axis=0))
-            )
+            kt[p, 0], kt[p, 1] = split(turned)
+            weighted[p] = split(turned * tails[p : p + 1])
+            grams.append(dot(wide(weighted[p]), tall(kk)))
         early = pick(first, grams[0], grams[1])
         late = pick(first, grams[1], grams[0])
         shrink = pick(first, decay[half + h : half + h + 1], decay[h : h + 1])
@@ -146,12 +164,13 @@
         tg[h, body:] = tail_rows(diag, total)
         pg[h, :body] = packed.astype(BF16)
         pg[h, body:] = tail_sent(diag, total)
-    fetch.wait()
     for h in range(half):
         states = []
         for side, vref in enumerate((vo, vr)):
             v = columns(vref, core, h, half, width)
-            states.append(dot_t(weighted[h + side * half], jnp.concatenate([v, v], axis=0)))
+            states.append(
+                dot(jnp.concatenate(weighted[h + side * half], axis=1), jnp.concatenate([v, v], axis=0))
+            )
         early_state = pick(first, states[0], states[1])
         late_state = pick(first, states[1], states[0])
         shrink = pick(first, decay[half + h : half + h + 1], decay[h : h + 1])
@@ -211,26 +230,22 @@
         before_new[h] = before[h] + add if has_prefix else add
 
 
-def prepare_kernel(meta, ridge, ks, qo, qr, fo, fr, go, gr, q_s, kt, m_s, e_s, base):
+def prepare_kernel(meta, ridge, ks, kt, qo, qr, fo, fr, go, gr, q_s, m_s, e_s, base):
     pairs, _, tokens, width = ks.shape
     half = pairs // 2
     core = meta[0]
     beta = gates(go, gr, core, half)
     level = running_sum(gates(fo, fr, core, half))
     level_t = level.T
-    beta_t = beta.T
     square = (tokens, tokens)
     lower = rows_of(square) >= lanes_of(square)
     eye = (rows_of((width, width)) == lanes_of((width, width))).astype(F32)
     for side, qref in enumerate((qo, qr)):
         for h in range(half):
             p = h + side * half
-            kh, kl = ks[p, 0], ks[p, 1]
-            kt[p, 0], kt[p, 1] = kh.T, kl.T
-            k = kh.astype(F32) + kl.astype(F32)
-            bk = split(k * beta_t[:, p : p + 1])
-            cross = dot_t(jnp.concatenate([bk[0], bk[1], bk[0]], axis=0), jnp.concatenate([kh, kh, kl], axis=0))
-            base[p] = cross + ridge[core * half + h] * eye
+            turned = kt[p, 0].astype(F32) + kt[p, 1].astype(F32)
+            cross = dot(wide(split(turned * beta[p : p + 1])), tall((ks[p, 0], ks[p, 1])))
+            base[p] = cross + ridge_of(ridge, core, h, half) * eye
             column = level_t[:, p : p + 1]
             m_s[p] = jnp.where(lower, jnp.exp(jnp.minimum(column - level[p : p + 1], 0.0)) * beta[p : p + 1], 0.0)
             e_s[p] = jnp.broadcast_to(jnp.exp(column), square)
@@ -277,7 +292,7 @@
             left.append(eye - dot(wide((a_s[p, 0], a_s[p, 1])), tall(split(p_s[p]))))
         for p, rest in zip(group, left):
             now = p_s[p]
-            p_s[p] = now + dot(wide(split(now)), tall(split(rest)))
+            p_s[p] = now + dot(now.astype(BF16), rest.astype(BF16))
 
 
 def correct_kernel(meta, ridge, q_s, kt, m_s, e_s, ks, s_s, p_s, vo, vr, xs, part, x_s):
@@ -299,7 +314,7 @@
             applied.append(
                 e_s[p] * both[p][:, :width]
                 + dot(scores.astype(BF16), ks[p, 0])
-                + ridge[core * half + p % half] * x_s[p]
+                + ridge_of(ridge, core, p % half, half) * x_s[p]
             )
         for p in range(pairs):
             x_s[p] = x_s[p] + dot((q_s[p] - applied[p]).astype(BF16), p_s[p].astype(BF16))
@@ -315,8 +330,8 @@
             scores = m_s[p] * found[:, width:]
             applied.append(
                 e_s[p] * found[:, :width]
-                + dot(wide(split(scores)), tall((ks[p, 0], ks[p, 1])))
-                + ridge[core * half + p - start] * x_s[p]
+                + dot(scores.astype(BF16), ks[p, 0])
+                + ridge_of(ridge, core, p - start, half) * x_s[p]
             )
         solved = []
         for p, found in zip(group, applied):
@@ -332,9 +347,7 @@
             part[p] = dot(jnp.concatenate([sh, sl], axis=1), jnp.concatenate([v, v], axis=0))
 
 
-def read_kernel(which, meta, xs, part, e_s, fo, fr, uf, before_g, before, got, far_gain, y_own, y_other, gain, sem):
-    fetch = pltpu.make_async_copy(far_gain, gain, sem)
-    fetch.start()
+def read_kernel(which, meta, xs, part, e_s, fo, fr, uf, before_g, before, got, gain, y_own, y_other):
     half = uf.shape[0]
     width = uf.shape[1]
     body = width // 2
@@ -343,30 +356,19 @@
     bit = meta[which] == 1
     decay = jnp.exp(jnp.sum(gates(fo, fr, core, half), axis=1, keepdims=True))
     sides = ((y_own, first), (y_other, jnp.logical_not(first)))
-    normed = {}
     for h in range(half):
+        cols = slice(h * width, (h + 1) * width)
         e = jnp.where(bit, jnp.exp(before_g[h, body + 1 : body + 2]), 0.0)
         start = before[h] + e * got[h].astype(F32)
-        for side, (_, is_early) in enumerate(sides):
+        scale = columns(gain, core, h, half, width)
+        for side, (out, is_early) in enumerate(sides):
             p = h + side * half
             other = h + (1 - side) * half
             state = jnp.where(is_early, start, decay[other : other + 1] * start + uf[h])
             read = dot(wide((xs[p, 0], xs[p, 1])), tall(split(state)))
             o = e_s[p] * read + part[p]
-            normed[p] = o * lax.rsqrt(jnp.mean(o * o, axis=-1, keepdims=True) + 1e-6)
-    fetch.wait()
-    for h in range(half):
-        scale = columns(gain, core, h, half, width)
-        for side, (out, _) in enumerate(sides):
-            out[:, h * width : (h + 1) * width] = (normed[h + side * half] * scale).astype(BF16)
-
-
-def share_kernel(meta, w, out, sem):
-    size = out.shape[2]
-    share = meta[meta.shape[0] - 1]
-    fetch = pltpu.make_async_copy(w.at[:, pl.ds(pl.multiple_of(share * size, size), size)], out.at[0], sem)
-    fetch.start()
-    fetch.wait()
+            o = o * lax.rsqrt(jnp.mean(o * o, axis=-1, keepdims=True) + 1e-6)
+            out[:, cols] = (o * scale).astype(BF16)
 
 
 def stack_kernel(a, b, out):
@@ -451,12 +453,13 @@
 def call(kernel, outs, scalars, ins, scratch=(), far=()):
     spec = pl.BlockSpec(memory_space=VMEM)
     near = [pltpu.with_memory_space_constraint(a, VMEM) for a in ins]
+    far = [pltpu.with_memory_space_constraint(a, pltpu.HBM) for a in far]
     return pl.pallas_call(
         kernel,
         out_shape=outs,
         in_specs=[pl.BlockSpec(memory_space=SMEM)] * len(scalars)
         + [spec] * len(near)
-        + [pl.BlockSpec(memory_space=pl.ANY)] * len(far),
+        + [pl.BlockSpec(memory_space=pltpu.HBM)] * len(far),
         out_specs=jax.tree.map(lambda _: spec, outs),
         scratch_shapes=scratch,
         compiler_params=pltpu.CompilerParams(vmem_limit_bytes=GRANT),
@@ -487,8 +490,21 @@
     keys_o = swap(keys, 1)
     forget_o, gate_o = swap(log_forget, 1), swap(input_gate, 1)
     values_o, queries_o = swap(values, 1), swap(queries, 1)
-    forgets = (log_forget, forget_o)
-    gate_args = (*forgets, input_gate, gate_o)
+    mine = VMEM((tokens, half * width), BF16)
+    small = VMEM(log_forget.shape, F32)
+    size = out_columns // parts
+    far_args = (out_weight, keys, values, queries, log_forget, input_gate)
+    far_args += (gain.reshape(1, features), ridge.reshape(1, heads))
+    own, keys_m, values_m, queries_m, forget_m, gate_m, gain_row, ridge_row = call(
+        load_kernel,
+        (VMEM((1, rows, size), BF16), mine, mine, mine, small, small, VMEM((1, features), F32), VMEM((1, heads), F32)),
+        (meta,),
+        (),
+        (pltpu.SemaphoreType.DMA((len(far_args),)),),
+        far_args,
+    )
+    forgets = (forget_m, forget_o)
+    gate_args = (*forgets, gate_m, gate_o)
 
     packed = (half, body + 8, width)
     sent = (half, body + 16, width)
@@ -496,14 +512,12 @@
     many = (pairs, width, width)
     two = (pairs, 2, width, width)
 
-    pg, tg, pw, tw, gf, uf, ks = call(
+    pg, tg, pw, tw, gf, uf, ks, kt = call(
         sums_kernel,
         (VMEM(sent, BF16), VMEM(packed, F32), VMEM(full, BF16), VMEM(full, F32), VMEM(full, F32), VMEM(full, F32),
-         VMEM(two, BF16)),
+         VMEM(two, BF16), VMEM(two, BF16)),
         (meta,),
-        (keys, keys_o, values_o, *gate_args),
-        (VMEM(values.shape, BF16), pltpu.SemaphoreType.DMA),
-        (values,),
+        (keys_m, keys_o, values_m, values_o, *gate_args),
     )
 
     before = before_w = None
@@ -530,9 +544,6 @@
         )
     last = bits
 
-    size = out_columns // parts
-    own = call(share_kernel, VMEM((1, rows, size), BF16), (meta,), (), (pltpu.SemaphoreType.DMA,), (out_weight,))
-
     def stack(a, b):
         return call(stack_kernel, VMEM((a.shape[0] + b.shape[0], rows, size), BF16), (), (a, b))
 
@@ -550,7 +561,6 @@
         near = swap(out_weight, 2)
         both = stack(far, mid)
         groups.append(((4, 2), both))
-        groups.append(((5, 3), swap(both, 2)))
         groups.append(((6, 7), stack(farther, swap(farther, 2))))
         keep((1,), None, near, 0)
         keep((1,), None, swap(near, 1), 1)
@@ -561,22 +571,25 @@
             groups.append(fresh)
             if bit:
                 held = (held[0] + fresh[0], stack(held[1], fresh[1]))
-    for offsets, array in groups:
+    for g, (offsets, array) in enumerate(groups):
         shares = [(0, array)]
         step = 1
         while step < parts:
             shares += [(q ^ step, swap(a, step, "parts")) for q, a in shares]
             step *= 2
+        if bits == 3 and g == 0:
+            shares += [(q + parts, swap(a, 2)) for q, a in shares]
         for q, a in shares:
-            keep(offsets, q, a, 0)
-            keep(offsets, q, swap(a, 1), 1)
+            at = offsets if q < parts else tuple(o ^ 1 for o in offsets)
+            keep(at, q % parts, a, 0)
+            keep(at, q % parts, swap(a, 1), 1)
     weight_o = swap(out_weight, 1)
 
-    q_s, kt, m_s, e_s, base = call(
+    q_s, m_s, e_s, base = call(
         prepare_kernel,
-        (VMEM(many, F32), VMEM(two, BF16), VMEM(many, F32), VMEM(many, F32), VMEM(many, F32)),
-        (meta, ridge),
-        (ks, queries, queries_o, *gate_args),
+        (VMEM(many, F32), VMEM(many, F32), VMEM(many, F32), VMEM(many, F32)),
+        (meta,),
+        (ridge_row, ks, kt, queries_m, queries_o, *gate_args),
     )
     s_s, p_s = call(
         functools.partial(inverse_kernel, last),
@@ -588,17 +601,15 @@
     xs, part = call(
         correct_kernel,
         (VMEM(two, BF16), VMEM(many, F32)),
-        (meta, ridge),
-        (q_s, kt, m_s, e_s, ks, s_s, p_s, values, values_o),
+        (meta,),
+        (ridge_row, q_s, kt, m_s, e_s, ks, s_s, p_s, values_m, values_o),
         (VMEM(many, F32),),
     )
     y_own, y_other = call(
         functools.partial(read_kernel, last),
         (VMEM((tokens, half * width), BF16),) * 2,
         (meta,),
-        (xs, part, e_s, *forgets, uf, before, before_w, got_w),
-        (VMEM((1, features), F32), pltpu.SemaphoreType.DMA),
-        (gain.reshape(1, features),),
+        (xs, part, e_s, *forgets, uf, before, before_w, got_w, gain_row),
     )
     y_got = swap(y_other, 1)
 

time: 67.9 us -> 65.9 us (0.971)
  local copies, waits for them, and re-layouts: 1.65 us -> 0.02 us
  Pallas kernels: 17.8 us -> 16.6 us
    unnamed x14 -> x8, local copies, waits for them, and re-layouts: 1.65 us -> 0.02 us
    pallas_call x13, Pallas kernels: 17.8 us -> 16.6 us  [call(): pl.pallas_call(kernel, out_shape=outs, in_specs=[pl.BlockSpec(memory_spac...]
  transfers between devices with their start and end apart: 29 -> 29, of which waited for: 10 -> 10; matrix products, arithmetic and copies ran while one was open for 0% -> 0% of each run, Pallas kernels for 23% -> 22%
where the time goes in v2:
time: 65.9 us; the launch traced here: 65.8 us
  starting transfers between devices  24.6 us (37%)
  waiting for transfers between devices  24.4 us (37%)
  Pallas kernels  16.6 us (25%)
    ppermute x29, starting transfers between devices, swap(): return lax.ppermute(array, axis, [(i, i ^ distance) for i in range(count)])  24.6 us
    ppermute x29, waiting for transfers between devices, swap(): return lax.ppermute(array, axis, [(i, i ^ distance) for i in range(count)])  24.4 us
    pallas_call x13, Pallas kernels, call(): pl.pallas_call(kernel, out_shape=outs, in_specs=[pl.BlockSpec(memory_spac...  16.6 us
  transfers between devices with their start and end apart: 29, of which 10 were waited for; matrix products, arithmetic and copies ran while one was open for 0% of the time, Pallas kernels for 22%

profile of v2, /device:TPU:0, one launch (start us, length us, event | category | flops | bytes accessed | tf_op | source)
XLA Modules:
  0.0 65.8 jit_solution(3054450833997894283)
XLA Ops:
  0.5 1.7 %shard_map.82 = (bf16[1,64,1024]{2,1,0:T(8,128)(2,1)S(1)}, bf16[128,512]{1,0:T(8,128)(2,1)S(1)}, bf16[128,512]{1,0:T(8,128)(2,1)S(1)}, bf16[128,512]{1,0:T(8,128...) custom-call(s32[6]{0:T(128)S(1)} %compare_select_fusion.1.meta, ...), custom_call_target="tpu_custom_call" | custom-call | tf_op jit(solution)/shard_map/pallas_call | solution.py:457
  2.3 4.1 %collective-permute-start.15 = (bf16[1,64,1024]{2,1,0:T(8,128)(2,1)S(1)}, bf16[1,64,1024]{2,1,0:T(8,128)(2,1)S(1)}, u32[]{:S(2)}, u32[]{:S(2)}) collective-permute-start(bf16[1,64,1024]{2,1,0:T(8,128)(2,1)S(1)} %get-tuple-element.80), channel_id=1, source_target_pairs={{0,8},{1,9},{2,10},{3,11},{4,12},{5,13},{6,14},{7,15},{8,0},{9,1},... | collective-permute-start | bytes 393224 | tf_op jit(solution)/shard_map/ppermute | solution.py:488
  6.9 0.7 collective-permute-done.2.fr
  7.8 1.5 %collective-permute-start.13 = (bf16[64,2048]{1,0:T(8,128)(2,1)S(1)}, bf16[64,2048]{1,0:T(8,128)(2,1)S(1)}, u32[]{:S(2)}, u32[]{:S(2)}) collective-permute-start(bf16[64,2048]{1,0:T(8,128)(2,1)S(1)} %copy-done), channel_id=1, source_target_pairs={{0,2},{1,3},{2,0},{3,1},{4,6},{5,7},{6,4},{7,5},{8,10},{9,11},{10,... | collective-permute-start | bytes 786440 | tf_op jit(solution)/shard_map/ppermute | solution.py:488
  9.3 3.6 %collective-permute-done.15.a = bf16[1,64,1024]{2,1,0:T(8,128)(2,1)S(1)} collective-permute-done((bf16[1,64,1024]{2,1,0:T(8,128)(2,1)S(1)}, bf16[1,64,1024]{2,1,0:T(8,128)(2,1)S(1)}, u32[]{:S(2)}, u32[]{:S(2)}) %collective-permute-start.15) | collective-permute-done | bytes 131104 | tf_op jit(solution)/shard_map/ppermute | solution.py:488
  12.9 0.7 %collective-permute-start.16 = (bf16[1,64,1024]{2,1,0:T(8,128)(2,1)S(1)}, bf16[1,64,1024]{2,1,0:T(8,128)(2,1)S(1)}, u32[]{:S(2)}, u32[]{:S(2)}) collective-permute-start(bf16[1,64,1024]{2,1,0:T(8,128)(2,1)S(1)} %get-tuple-element.80), channel_id=1, source_target_pairs={{0,4},{1,5},{2,6},{3,7},{4,0},{5,1},{6,2},{7,3},{8,12},{9,13},{10,... | collective-permute-start | bytes 393224 | tf_op jit(solution)/shard_map/ppermute | solution.py:488
  13.6 1.3 %collective-permute-start.24 = (bf16[1,64,1024]{2,1,0:T(8,128)(2,1)S(1)}, bf16[1,64,1024]{2,1,0:T(8,128)(2,1)S(1)}, u32[]{:S(2)}, u32[]{:S(2)}) collective-permute-start(bf16[1,64,1024]{2,1,0:T(8,128)(2,1)S(1)} %collective-permute-done.15.a), channel_id=1, source_target_pairs={{0,4},{1,5},{2,6},{3,7},{4,0},{5,1},{6,2},{7,3},{8,12},{9,13},{10,... | collective-permute-start | bytes 393224 | tf_op jit(solution)/shard_map/ppermute | solution.py:488
  14.9 1.5 %shard_map.83 = (bf16[4,80,128]{2,1,0:T(8,128)(2,1)S(1)}, f32[4,72,128]{2,1,0:T(8,128)S(1)}, bf16[4,128,128]{2,1,0:T(8,128)(2,1)S(1)}, f32[4,128,128]{2,1,0:T(8,...) custom-call(s32[6]{0:T(128)S(1)} %compare_select_fusion.1.meta, ...), custom_call_target="tpu_custom_call" | custom-call | tf_op jit(solution)/shard_map/pallas_call | solution.py:457
  16.5 2.7 %collective-permute-done.16.b = bf16[1,64,1024]{2,1,0:T(8,128)(2,1)S(1)} collective-permute-done((bf16[1,64,1024]{2,1,0:T(8,128)(2,1)S(1)}, bf16[1,64,1024]{2,1,0:T(8,128)(2,1)S(1)}, u32[]{:S(2)}, u32[]{:S(2)}) %collective-permute-start.16) | collective-permute-done | bytes 131104 | tf_op jit(solution)/shard_map/ppermute | solution.py:488
  19.1 1.3 %collective-permute-start.5 = (bf16[4,80,128]{2,1,0:T(8,128)(2,1)S(1)}, bf16[4,80,128]{2,1,0:T(8,128)(2,1)S(1)}, u32[]{:S(2)}, u32[]{:S(2)}) collective-permute-start(bf16[4,80,128]{2,1,0:T(8,128)(2,1)S(1)} %get-tuple-element.57), channel_id=1, source_target_pairs={{0,2},{1,3},{2,0},{3,1},{4,6},{5,7},{6,4},{7,5},{8,10},{9,11},{10,... | collective-permute-start | bytes 245768 | tf_op jit(solution)/shard_map/ppermute | solution.py:488
  20.5 0.8 %collective-permute-start.8 = (bf16[4,128,128]{2,1,0:T(8,128)(2,1)S(1)}, bf16[4,128,128]{2,1,0:T(8,128)(2,1)S(1)}, u32[]{:S(2)}, u32[]{:S(2)}) collective-permute-start(bf16[4,128,128]{2,1,0:T(8,128)(2,1)S(1)} %get-tuple-element.71), channel_id=1, source_target_pairs={{0,2},{1,3},{2,0},{3,1},{4,6},{5,7},{6,4},{7,5},{8,10},{9,11},{10,... | collective-permute-start | bytes 393224 | tf_op jit(solution)/shard_map/ppermute | solution.py:488
  21.3 1.3 %collective-permute-start.18 = (bf16[2,64,1024]{2,1,0:T(8,128)(2,1)S(1)}, bf16[2,64,1024]{2,1,0:T(8,128)(2,1)S(1)}, u32[]{:S(2)}, u32[]{:S(2)}) collective-permute-start(bf16[2,64,1024]{2,1,0:T(8,128)(2,1)S(1)} %shard_map.92.rest_2_), channel_id=1, source_target_pairs={{0,16},{16,0},{1,17},{17,1},{2,18},{18,2},{3,19},{19,3},{4,20},{20... | collective-permute-start | bytes 786440 | tf_op jit(solution)/shard_map/ppermute | solution.py:488
  22.5 1.5 %collective-permute-start.20 = (bf16[2,64,1024]{2,1,0:T(8,128)(2,1)S(1)}, bf16[2,64,1024]{2,1,0:T(8,128)(2,1)S(1)}, u32[]{:S(2)}, u32[]{:S(2)}) collective-permute-start(bf16[2,64,1024]{2,1,0:T(8,128)(2,1)S(1)} %shard_map.92.rest_2_), channel_id=1, source_target_pairs={{0,2},{1,3},{2,0},{3,1},{4,6},{5,7},{6,4},{7,5},{8,10},{9,11},{10,... | collective-permute-start | bytes 786440 | tf_op jit(solution)/shard_map/ppermute | solution.py:488
  24.5 1.3 %collective-permute-start.25 = (bf16[1,64,1024]{2,1,0:T(8,128)(2,1)S(1)}, bf16[1,64,1024]{2,1,0:T(8,128)(2,1)S(1)}, u32[]{:S(2)}, u32[]{:S(2)}) collective-permute-start(bf16[1,64,1024]{2,1,0:T(8,128)(2,1)S(1)} %collective-permute-done.24.a), channel_id=1, source_target_pairs={{0,2},{1,3},{2,0},{3,1},{4,6},{5,7},{6,4},{7,5},{8,10},{9,11},{10,... | collective-permute-start | bytes 393224 | tf_op jit(solution)/shard_map/ppermute | solution.py:488
  25.7 1.5 %collective-permute-done.8.got = bf16[4,128,128]{2,1,0:T(8,128)(2,1)S(1)} collective-permute-done((bf16[4,128,128]{2,1,0:T(8,128)(2,1)S(1)}, bf16[4,128,128]{2,1,0:T(8,128)(2,1)S(1)}, u32[]{:S(2)}, u32[]{:S(2)}) %collective-permute-start.8) | collective-permute-done | bytes 131104 | tf_op jit(solution)/shard_map/ppermute | solution.py:488
  27.3 0.6 shard_map.85
  27.9 0.8 %collective-permute-start.9 = (bf16[4,128,128]{2,1,0:T(8,128)(2,1)S(1)}, bf16[4,128,128]{2,1,0:T(8,128)(2,1)S(1)}, u32[]{:S(2)}, u32[]{:S(2)}) collective-permute-start(bf16[4,128,128]{2,1,0:T(8,128)(2,1)S(1)} %get-tuple-element.73), channel_id=1, source_target_pairs={{0,4},{1,5},{2,6},{3,7},{4,0},{5,1},{6,2},{7,3},{8,12},{9,13},{10,... | collective-permute-start | bytes 393224 | tf_op jit(solution)/shard_map/ppermute | solution.py:488
  28.7 4.5 %collective-permute-done.25.b = bf16[1,64,1024]{2,1,0:T(8,128)(2,1)S(1)} collective-permute-done((bf16[1,64,1024]{2,1,0:T(8,128)(2,1)S(1)}, bf16[1,64,1024]{2,1,0:T(8,128)(2,1)S(1)}, u32[]{:S(2)}, u32[]{:S(2)}) %collective-permute-start.25) | collective-permute-done | bytes 131104 | tf_op jit(solution)/shard_map/ppermute | solution.py:488
  33.2 1.5 %collective-permute-start.6 = (bf16[4,80,128]{2,1,0:T(8,128)(2,1)S(1)}, bf16[4,80,128]{2,1,0:T(8,128)(2,1)S(1)}, u32[]{:S(2)}, u32[]{:S(2)}) collective-permute-start(bf16[4,80,128]{2,1,0:T(8,128)(2,1)S(1)} %get-tuple-element.59), channel_id=1, source_target_pairs={{0,4},{1,5},{2,6},{3,7},{4,0},{5,1},{6,2},{7,3},{8,12},{9,13},{10,... | collective-permute-start | bytes 245768 | tf_op jit(solution)/shard_map/ppermute | solution.py:488
  34.7 1.2 %collective-permute-start.27 = (bf16[2,64,1024]{2,1,0:T(8,128)(2,1)S(1)}, bf16[2,64,1024]{2,1,0:T(8,128)(2,1)S(1)}, u32[]{:S(2)}, u32[]{:S(2)}) collective-permute-start(bf16[2,64,1024]{2,1,0:T(8,128)(2,1)S(1)} %shard_map.93.rest_10_), channel_id=1, source_target_pairs={{0,16},{16,0},{1,17},{17,1},{2,18},{18,2},{3,19},{19,3},{4,20},{20... | collective-permute-start | bytes 786440 | tf_op jit(solution)/shard_map/ppermute | solution.py:488
  35.9 1.8 %collective-permute-done.6.got = bf16[4,80,128]{2,1,0:T(8,128)(2,1)S(1)} collective-permute-done((bf16[4,80,128]{2,1,0:T(8,128)(2,1)S(1)}, bf16[4,80,128]{2,1,0:T(8,128)(2,1)S(1)}, u32[]{:S(2)}, u32[]{:S(2)}) %collective-permute-start.6) | collective-permute-done | bytes 81952 | tf_op jit(solution)/shard_map/ppermute | solution.py:488
  37.6 1.5 %collective-permute-start.22 = (bf16[2,64,1024]{2,1,0:T(8,128)(2,1)S(1)}, bf16[2,64,1024]{2,1,0:T(8,128)(2,1)S(1)}, u32[]{:S(2)}, u32[]{:S(2)}) collective-permute-start(bf16[2,64,1024]{2,1,0:T(8,128)(2,1)S(1)} %collective-permute-done.18.rest_4_), channel_id=1, source_target_pairs={{0,2},{1,3},{2,0},{3,1},{4,6},{5,7},{6,4},{7,5},{8,10},{9,11},{10,... | collective-permute-start | bytes 786440 | tf_op jit(solution)/shard_map/ppermute | solution.py:488
  39.1 0.6 shard_map.86
  39.8 2.6 %collective-permute-start.7 = (bf16[4,80,128]{2,1,0:T(8,128)(2,1)S(1)}, bf16[4,80,128]{2,1,0:T(8,128)(2,1)S(1)}, u32[]{:S(2)}, u32[]{:S(2)}) collective-permute-start(bf16[4,80,128]{2,1,0:T(8,128)(2,1)S(1)} %get-tuple-element.62), channel_id=1, source_target_pairs={{0,8},{1,9},{2,10},{3,11},{4,12},{5,13},{6,14},{7,15},{8,0},{9,1},... | collective-permute-start | bytes 245768 | tf_op jit(solution)/shard_map/ppermute | solution.py:488
  42.9 5.2 %collective-permute-done.7.got = bf16[4,80,128]{2,1,0:T(8,128)(2,1)S(1)} collective-permute-done((bf16[4,80,128]{2,1,0:T(8,128)(2,1)S(1)}, bf16[4,80,128]{2,1,0:T(8,128)(2,1)S(1)}, u32[]{:S(2)}, u32[]{:S(2)}) %collective-permute-start.7) | collective-permute-done | bytes 81952 | tf_op jit(solution)/shard_map/ppermute | solution.py:488
  48.6 3.0 %collective-permute-done.10.got = bf16[4,128,128]{2,1,0:T(8,128)(2,1)S(1)} collective-permute-done((bf16[4,128,128]{2,1,0:T(8,128)(2,1)S(1)}, bf16[4,128,128]{2,1,0:T(8,128)(2,1)S(1)}, u32[]{:S(2)}, u32[]{:S(2)}) %collective-permute-start.10) | collective-permute-done | bytes 131104 | tf_op jit(solution)/shard_map/ppermute | solution.py:488
  52.3 1.7 %shard_map.84 = (f32[8,128,128]{2,1,0:T(8,128)S(1)}, f32[8,128,128]{2,1,0:T(8,128)S(1)}, f32[8,128,128]{2,1,0:T(8,128)S(1)}, f32[8,128,128]{2,1,0:T(8,128)S(1)}) custom-call(s32[6]{0:T(128)S(1)} %compare_select_fusion.1.meta, f32[1,8]{1,0:T(1,128)S(1)} %get-tuple-element.43.ridge, bf16[8,2,128,128]{3,2,1,0:T(8,128)(2,1)S(1)} %get-tuple-element.48.ks, ...), custom_call_target="tpu_custom_call" | custom-call | tf_op jit(solution)/shard_map/pallas_call | solution.py:457
  54.0 3.5 %shard_map.87 = (bf16[8,2,128,128]{3,2,1,0:T(8,128)(2,1)S(1)}, f32[8,128,128]{2,1,0:T(8,128)S(1)}) custom-call(s32[6]{0:T(128)S(1)} %compare_select_fusion.1.meta, f32[8,128,128]{2,1,0:T(8,128)S(1)} %get-tuple-element.54.base, f32[8,128]{1,0:T(8,128)S(1)} %get-tuple-element.46.fo, f32[8,128]{1,0:T(8,128)S(1)} %collective-permute-done.2.fr, ...), custom_call_target="tpu_custom_call" | custom-call | tf_op jit(solution)/shard_map/pallas_call | solution.py:457
  57.6 3.4 %shard_map.88 = (bf16[8,2,128,128]{3,2,1,0:T(8,128)(2,1)S(1)}, f32[8,128,128]{2,1,0:T(8,128)S(1)}) custom-call(s32[6]{0:T(128)S(1)} %compare_select_fusion.1.meta, f32[1,8]{1,0:T(1,128)S(1)} %get-tuple-element.43.ridge, f32[8,128,128]{2,1,0:T(8,128)S(1)} %get-tuple-element.51.q_s, bf16[8,2,128,128]{3,2,1,0:T(8,128)(2,1)S(1)} %get-tuple-element.49.kt, ...), custom_call_target="tpu_custom_call" | custom-call | tf_op jit(solution)/shard_map/pallas_call | solution.py:457
  61.0 1.1 %shard_map.91 = (bf16[128,512]{1,0:T(8,128)(2,1)S(1)}, bf16[128,512]{1,0:T(8,128)(2,1)S(1)}) custom-call(s32[6]{0:T(128)S(1)} %compare_select_fusion.1.meta, bf16[8,2,128,128]{3,2,1,0:T(8,128)(2,1)S(1)} %get-tuple-element.65.xs, f32[8,128,128]{2,1,0:T(8,128)S(1)} %get-tuple-element.66.part, f32[8,128,128]{2,1,0:T(8,128)S(1)} %get-tuple-element.53.e_s, ...), custom_call_target="tpu_custom_call" | custom-call | tf_op jit(solution)/shard_map/pallas_call | solution.py:457
  62.6 1.0 %collective-permute-done.11.y_other = bf16[128,512]{1,0:T(8,128)(2,1)S(1)} collective-permute-done((bf16[128,512]{1,0:T(8,128)(2,1)S(1)}, bf16[128,512]{1,0:T(8,128)(2,1)S(1)}, u32[]{:S(2)}, u32[]{:S(2)}) %collective-permute-start.11) | collective-permute-done | bytes 131104 | tf_op jit(solution)/shard_map/ppermute | solution.py:488
  63.6 2.1 %shard_map.94 = bf16[128,2048]{1,0:T(8,128)(2,1)} custom-call(s32[6]{0:T(128)S(1)} %compare_select_fusion.1.meta, bf16[128,512]{1,0:T(8,128)(2,1)S(1)} %get-tuple-element.78.y_own, bf16[128,512]{1,0:T(8,128)(2,1)S(1)} %collective-permute-done.11.y_other, bf16[64,2048]{1,0:T(8,128)(2,1)S(1)} %copy-done, bf16[64,2048]{1,0:T(8,128)(2,1)S(1)} %collective-permute-done.12.other, ...), custom_call_target="tpu_custom_call" | custom-call | tf_op jit(solution)/shard_map/pallas_call | solution.py:457
  (48 shorter events, 3.9 us)
Async XLA Ops:
  0.0 13.6 %collective-permute-start.1 = (bf16[128,1024]{1,0:T(8,128)(2,1)}, bf16[128,1024]{1,0:T(8,128)(2,1)S(1)}, u32[]{:S(2)}, u32[]{:S(2)}) collective-permute-start(bf16[128,1024]{1,0:T(8,128)(2,1)} %refs_2_.1), channel_id=1, source_target_pairs={{0,1},{1,0},{2,3},{3,2},{4,5},{5,4},{6,7},{7,6},{8,9},{9,8},{10,11... | collective-permute-start | bytes 786440 | tf_op jit(solution)/shard_map/ppermute | solution.py:488
  0.5 14.4 %collective-permute-start = (bf16[128,1024]{1,0:T(8,128)(2,1)}, bf16[128,1024]{1,0:T(8,128)(2,1)S(1)}, u32[]{:S(2)}, u32[]{:S(2)}) collective-permute-start(bf16[128,1024]{1,0:T(8,128)(2,1)} %refs_1_.1), channel_id=1, source_target_pairs={{0,1},{1,0},{2,3},{3,2},{4,5},{5,4},{6,7},{7,6},{8,9},{9,8},{10,11... | collective-permute-start | bytes 786440 | tf_op jit(solution)/shard_map/ppermute | solution.py:488
  0.5 5.9 %copy-start.3 = (f32[8,128]{1,0:T(8,128)S(1)}, f32[8,128]{1,0:T(8,128)}, u32[]{:S(2)}) copy-start(f32[8,128]{1,0:T(8,128)} %refs_5_.1) | copy-start | bytes 12292
  0.5 7.1 %copy-start.1 = (bf16[128,1024]{1,0:T(8,128)(2,1)S(1)}, bf16[128,1024]{1,0:T(8,128)(2,1)}, u32[]{:S(2)}) copy-start(bf16[128,1024]{1,0:T(8,128)(2,1)} %refs_3_.1) | copy-start | bytes 786436
  0.5 7.2 %copy-start = (bf16[64,2048]{1,0:T(8,128)(2,1)S(1)}, bf16[64,2048]{1,0:T(8,128)(2,1)}, u32[]{:S(2)}) copy-start(bf16[64,2048]{1,0:T(8,128)(2,1)} %own.1) | copy-start | bytes 786436
  2.3 10.6 %collective-permute-start.15 = (bf16[1,64,1024]{2,1,0:T(8,128)(2,1)S(1)}, bf16[1,64,1024]{2,1,0:T(8,128)(2,1)S(1)}, u32[]{:S(2)}, u32[]{:S(2)}) collective-permute-start(bf16[1,64,1024]{2,1,0:T(8,128)(2,1)S(1)} %get-tuple-element.80), channel_id=1, source_target_pairs={{0,8},{1,9},{2,10},{3,11},{4,12},{5,13},{6,14},{7,15},{8,0},{9,1},... | collective-permute-start | bytes 393224 | tf_op jit(solution)/shard_map/ppermute | solution.py:488
  6.4 1.2 %collective-permute-start.2 = (f32[8,128]{1,0:T(8,128)S(1)}, f32[8,128]{1,0:T(8,128)S(1)}, u32[]{:S(2)}, u32[]{:S(2)}) collective-permute-start(f32[8,128]{1,0:T(8,128)S(1)} %copy-done.2), channel_id=1, source_target_pairs={{0,1},{1,0},{2,3},{3,2},{4,5},{5,4},{6,7},{7,6},{8,9},{9,8},{10,11... | collective-permute-start | bytes 12296 | tf_op jit(solution)/shard_map/ppermute | solution.py:488
  6.4 1.3 %collective-permute-start.3 = (f32[8,128]{1,0:T(8,128)S(1)}, f32[8,128]{1,0:T(8,128)S(1)}, u32[]{:S(2)}, u32[]{:S(2)}) collective-permute-start(f32[8,128]{1,0:T(8,128)S(1)} %copy-done.3), channel_id=1, source_target_pairs={{0,1},{1,0},{2,3},{3,2},{4,5},{5,4},{6,7},{7,6},{8,9},{9,8},{10,11... | collective-permute-start | bytes 12296 | tf_op jit(solution)/shard_map/ppermute | solution.py:488
  7.6 12.9 %collective-permute-start.4 = (bf16[128,1024]{1,0:T(8,128)(2,1)S(1)}, bf16[128,1024]{1,0:T(8,128)(2,1)S(1)}, u32[]{:S(2)}, u32[]{:S(2)}) collective-permute-start(bf16[128,1024]{1,0:T(8,128)(2,1)S(1)} %copy-done.1), channel_id=1, source_target_pairs={{0,1},{1,0},{2,3},{3,2},{4,5},{5,4},{6,7},{7,6},{8,9},{9,8},{10,11... | collective-permute-start | bytes 786440 | tf_op jit(solution)/shard_map/ppermute | solution.py:488
  7.8 14.8 %collective-permute-start.13 = (bf16[64,2048]{1,0:T(8,128)(2,1)S(1)}, bf16[64,2048]{1,0:T(8,128)(2,1)S(1)}, u32[]{:S(2)}, u32[]{:S(2)}) collective-permute-start(bf16[64,2048]{1,0:T(8,128)(2,1)S(1)} %copy-done), channel_id=1, source_target_pairs={{0,2},{1,3},{2,0},{3,1},{4,6},{5,7},{6,4},{7,5},{8,10},{9,11},{10,... | collective-permute-start | bytes 786440 | tf_op jit(solution)/shard_map/ppermute | solution.py:488
  12.9 6.2 %collective-permute-start.16 = (bf16[1,64,1024]{2,1,0:T(8,128)(2,1)S(1)}, bf16[1,64,1024]{2,1,0:T(8,128)(2,1)S(1)}, u32[]{:S(2)}, u32[]{:S(2)}) collective-permute-start(bf16[1,64,1024]{2,1,0:T(8,128)(2,1)S(1)} %get-tuple-element.80), channel_id=1, source_target_pairs={{0,4},{1,5},{2,6},{3,7},{4,0},{5,1},{6,2},{7,3},{8,12},{9,13},{10,... | collective-permute-start | bytes 393224 | tf_op jit(solution)/shard_map/ppermute | solution.py:488
  13.6 7.6 %collective-permute-start.24 = (bf16[1,64,1024]{2,1,0:T(8,128)(2,1)S(1)}, bf16[1,64,1024]{2,1,0:T(8,128)(2,1)S(1)}, u32[]{:S(2)}, u32[]{:S(2)}) collective-permute-start(bf16[1,64,1024]{2,1,0:T(8,128)(2,1)S(1)} %collective-permute-done.15.a), channel_id=1, source_target_pairs={{0,4},{1,5},{2,6},{3,7},{4,0},{5,1},{6,2},{7,3},{8,12},{9,13},{10,... | collective-permute-start | bytes 393224 | tf_op jit(solution)/shard_map/ppermute | solution.py:488
  14.9 13.0 %collective-permute-start.12 = (bf16[64,2048]{1,0:T(8,128)(2,1)S(1)}, bf16[64,2048]{1,0:T(8,128)(2,1)S(1)}, u32[]{:S(2)}, u32[]{:S(2)}) collective-permute-start(bf16[64,2048]{1,0:T(8,128)(2,1)S(1)} %copy-done), channel_id=1, source_target_pairs={{0,1},{1,0},{2,3},{3,2},{4,5},{5,4},{6,7},{7,6},{8,9},{9,8},{10,11... | collective-permute-start | bytes 786440 | tf_op jit(solution)/shard_map/ppermute | solution.py:488
  19.1 5.3 %collective-permute-start.5 = (bf16[4,80,128]{2,1,0:T(8,128)(2,1)S(1)}, bf16[4,80,128]{2,1,0:T(8,128)(2,1)S(1)}, u32[]{:S(2)}, u32[]{:S(2)}) collective-permute-start(bf16[4,80,128]{2,1,0:T(8,128)(2,1)S(1)} %get-tuple-element.57), channel_id=1, source_target_pairs={{0,2},{1,3},{2,0},{3,1},{4,6},{5,7},{6,4},{7,5},{8,10},{9,11},{10,... | collective-permute-start | bytes 245768 | tf_op jit(solution)/shard_map/ppermute | solution.py:488
  20.5 6.8 %collective-permute-start.8 = (bf16[4,128,128]{2,1,0:T(8,128)(2,1)S(1)}, bf16[4,128,128]{2,1,0:T(8,128)(2,1)S(1)}, u32[]{:S(2)}, u32[]{:S(2)}) collective-permute-start(bf16[4,128,128]{2,1,0:T(8,128)(2,1)S(1)} %get-tuple-element.71), channel_id=1, source_target_pairs={{0,2},{1,3},{2,0},{3,1},{4,6},{5,7},{6,4},{7,5},{8,10},{9,11},{10,... | collective-permute-start | bytes 393224 | tf_op jit(solution)/shard_map/ppermute | solution.py:488
  21.3 13.4 %collective-permute-start.18 = (bf16[2,64,1024]{2,1,0:T(8,128)(2,1)S(1)}, bf16[2,64,1024]{2,1,0:T(8,128)(2,1)S(1)}, u32[]{:S(2)}, u32[]{:S(2)}) collective-permute-start(bf16[2,64,1024]{2,1,0:T(8,128)(2,1)S(1)} %shard_map.92.rest_2_), channel_id=1, source_target_pairs={{0,16},{16,0},{1,17},{17,1},{2,18},{18,2},{3,19},{19,3},{4,20},{20... | collective-permute-start | bytes 786440 | tf_op jit(solution)/shard_map/ppermute | solution.py:488
  22.5 12.2 %collective-permute-start.20 = (bf16[2,64,1024]{2,1,0:T(8,128)(2,1)S(1)}, bf16[2,64,1024]{2,1,0:T(8,128)(2,1)S(1)}, u32[]{:S(2)}, u32[]{:S(2)}) collective-permute-start(bf16[2,64,1024]{2,1,0:T(8,128)(2,1)S(1)} %shard_map.92.rest_2_), channel_id=1, source_target_pairs={{0,2},{1,3},{2,0},{3,1},{4,6},{5,7},{6,4},{7,5},{8,10},{9,11},{10,... | collective-permute-start | bytes 786440 | tf_op jit(solution)/shard_map/ppermute | solution.py:488
  24.5 8.7 %collective-permute-start.25 = (bf16[1,64,1024]{2,1,0:T(8,128)(2,1)S(1)}, bf16[1,64,1024]{2,1,0:T(8,128)(2,1)S(1)}, u32[]{:S(2)}, u32[]{:S(2)}) collective-permute-start(bf16[1,64,1024]{2,1,0:T(8,128)(2,1)S(1)} %collective-permute-done.24.a), channel_id=1, source_target_pairs={{0,2},{1,3},{2,0},{3,1},{4,6},{5,7},{6,4},{7,5},{8,10},{9,11},{10,... | collective-permute-start | bytes 393224 | tf_op jit(solution)/shard_map/ppermute | solution.py:488
  27.3 15.2 %collective-permute-start.17 = (bf16[2,64,1024]{2,1,0:T(8,128)(2,1)S(1)}, bf16[2,64,1024]{2,1,0:T(8,128)(2,1)S(1)}, u32[]{:S(2)}, u32[]{:S(2)}) collective-permute-start(bf16[2,64,1024]{2,1,0:T(8,128)(2,1)S(1)} %shard_map.92.rest_2_), channel_id=1, source_target_pairs={{0,1},{1,0},{2,3},{3,2},{4,5},{5,4},{6,7},{7,6},{8,9},{9,8},{10,11... | collective-permute-start | bytes 786440 | tf_op jit(solution)/shard_map/ppermute | solution.py:488
  27.9 11.8 %collective-permute-start.9 = (bf16[4,128,128]{2,1,0:T(8,128)(2,1)S(1)}, bf16[4,128,128]{2,1,0:T(8,128)(2,1)S(1)}, u32[]{:S(2)}, u32[]{:S(2)}) collective-permute-start(bf16[4,128,128]{2,1,0:T(8,128)(2,1)S(1)} %get-tuple-element.73), channel_id=1, source_target_pairs={{0,4},{1,5},{2,6},{3,7},{4,0},{5,1},{6,2},{7,3},{8,12},{9,13},{10,... | collective-permute-start | bytes 393224 | tf_op jit(solution)/shard_map/ppermute | solution.py:488
  33.2 4.4 %collective-permute-start.6 = (bf16[4,80,128]{2,1,0:T(8,128)(2,1)S(1)}, bf16[4,80,128]{2,1,0:T(8,128)(2,1)S(1)}, u32[]{:S(2)}, u32[]{:S(2)}) collective-permute-start(bf16[4,80,128]{2,1,0:T(8,128)(2,1)S(1)} %get-tuple-element.59), channel_id=1, source_target_pairs={{0,4},{1,5},{2,6},{3,7},{4,0},{5,1},{6,2},{7,3},{8,12},{9,13},{10,... | collective-permute-start | bytes 245768 | tf_op jit(solution)/shard_map/ppermute | solution.py:488
  34.7 13.5 %collective-permute-start.14 = (bf16[64,2048]{1,0:T(8,128)(2,1)S(1)}, bf16[64,2048]{1,0:T(8,128)(2,1)S(1)}, u32[]{:S(2)}, u32[]{:S(2)}) collective-permute-start(bf16[64,2048]{1,0:T(8,128)(2,1)S(1)} %collective-permute-done.13.rest_0_), channel_id=1, source_target_pairs={{0,1},{1,0},{2,3},{3,2},{4,5},{5,4},{6,7},{7,6},{8,9},{9,8},{10,11... | collective-permute-start | bytes 786440 | tf_op jit(solution)/shard_map/ppermute | solution.py:488
  34.7 17.0 %collective-permute-start.27 = (bf16[2,64,1024]{2,1,0:T(8,128)(2,1)S(1)}, bf16[2,64,1024]{2,1,0:T(8,128)(2,1)S(1)}, u32[]{:S(2)}, u32[]{:S(2)}) collective-permute-start(bf16[2,64,1024]{2,1,0:T(8,128)(2,1)S(1)} %shard_map.93.rest_10_), channel_id=1, source_target_pairs={{0,16},{16,0},{1,17},{17,1},{2,18},{18,2},{3,19},{19,3},{4,20},{20... | collective-permute-start | bytes 786440 | tf_op jit(solution)/shard_map/ppermute | solution.py:488
  37.6 14.6 %collective-permute-start.22 = (bf16[2,64,1024]{2,1,0:T(8,128)(2,1)S(1)}, bf16[2,64,1024]{2,1,0:T(8,128)(2,1)S(1)}, u32[]{:S(2)}, u32[]{:S(2)}) collective-permute-start(bf16[2,64,1024]{2,1,0:T(8,128)(2,1)S(1)} %collective-permute-done.18.rest_4_), channel_id=1, source_target_pairs={{0,2},{1,3},{2,0},{3,1},{4,6},{5,7},{6,4},{7,5},{8,10},{9,11},{10,... | collective-permute-start | bytes 786440 | tf_op jit(solution)/shard_map/ppermute | solution.py:488
  39.8 8.3 %collective-permute-start.7 = (bf16[4,80,128]{2,1,0:T(8,128)(2,1)S(1)}, bf16[4,80,128]{2,1,0:T(8,128)(2,1)S(1)}, u32[]{:S(2)}, u32[]{:S(2)}) collective-permute-start(bf16[4,80,128]{2,1,0:T(8,128)(2,1)S(1)} %get-tuple-element.62), channel_id=1, source_target_pairs={{0,8},{1,9},{2,10},{3,11},{4,12},{5,13},{6,14},{7,15},{8,0},{9,1},... | collective-permute-start | bytes 245768 | tf_op jit(solution)/shard_map/ppermute | solution.py:488
  42.4 9.2 %collective-permute-start.10 = (bf16[4,128,128]{2,1,0:T(8,128)(2,1)S(1)}, bf16[4,128,128]{2,1,0:T(8,128)(2,1)S(1)}, u32[]{:S(2)}, u32[]{:S(2)}) collective-permute-start(bf16[4,128,128]{2,1,0:T(8,128)(2,1)S(1)} %get-tuple-element.76), channel_id=1, source_target_pairs={{0,8},{1,9},{2,10},{3,11},{4,12},{5,13},{6,14},{7,15},{8,0},{9,1},... | collective-permute-start | bytes 393224 | tf_op jit(solution)/shard_map/ppermute | solution.py:488
  48.1 14.0 %collective-permute-start.26 = (bf16[2,64,1024]{2,1,0:T(8,128)(2,1)S(1)}, bf16[2,64,1024]{2,1,0:T(8,128)(2,1)S(1)}, u32[]{:S(2)}, u32[]{:S(2)}) collective-permute-start(bf16[2,64,1024]{2,1,0:T(8,128)(2,1)S(1)} %shard_map.93.rest_10_), channel_id=1, source_target_pairs={{0,1},{1,0},{2,3},{3,2},{4,5},{5,4},{6,7},{7,6},{8,9},{9,8},{10,11... | collective-permute-start | bytes 786440 | tf_op jit(solution)/shard_map/ppermute | solution.py:488
  48.1 14.5 %collective-permute-start.19 = (bf16[2,64,1024]{2,1,0:T(8,128)(2,1)S(1)}, bf16[2,64,1024]{2,1,0:T(8,128)(2,1)S(1)}, u32[]{:S(2)}, u32[]{:S(2)}) collective-permute-start(bf16[2,64,1024]{2,1,0:T(8,128)(2,1)S(1)} %collective-permute-done.18.rest_4_), channel_id=1, source_target_pairs={{0,1},{1,0},{2,3},{3,2},{4,5},{5,4},{6,7},{7,6},{8,9},{9,8},{10,11... | collective-permute-start | bytes 786440 | tf_op jit(solution)/shard_map/ppermute | solution.py:488
  51.7 11.0 %collective-permute-start.21 = (bf16[2,64,1024]{2,1,0:T(8,128)(2,1)S(1)}, bf16[2,64,1024]{2,1,0:T(8,128)(2,1)S(1)}, u32[]{:S(2)}, u32[]{:S(2)}) collective-permute-start(bf16[2,64,1024]{2,1,0:T(8,128)(2,1)S(1)} %collective-permute-done.20.rest_6_), channel_id=1, source_target_pairs={{0,1},{1,0},{2,3},{3,2},{4,5},{5,4},{6,7},{7,6},{8,9},{9,8},{10,11... | collective-permute-start | bytes 786440 | tf_op jit(solution)/shard_map/ppermute | solution.py:488
  51.7 11.9 %collective-permute-start.28 = (bf16[2,64,1024]{2,1,0:T(8,128)(2,1)S(1)}, bf16[2,64,1024]{2,1,0:T(8,128)(2,1)S(1)}, u32[]{:S(2)}, u32[]{:S(2)}) collective-permute-start(bf16[2,64,1024]{2,1,0:T(8,128)(2,1)S(1)} %collective-permute-done.27.rest_12_), channel_id=1, source_target_pairs={{0,1},{1,0},{2,3},{3,2},{4,5},{5,4},{6,7},{7,6},{8,9},{9,8},{10,11... | collective-permute-start | bytes 786440 | tf_op jit(solution)/shard_map/ppermute | solution.py:488
  52.2 11.4 %collective-permute-start.23 = (bf16[2,64,1024]{2,1,0:T(8,128)(2,1)S(1)}, bf16[2,64,1024]{2,1,0:T(8,128)(2,1)S(1)}, u32[]{:S(2)}, u32[]{:S(2)}) collective-permute-start(bf16[2,64,1024]{2,1,0:T(8,128)(2,1)S(1)} %collective-permute-done.22.rest_8_), channel_id=1, source_target_pairs={{0,1},{1,0},{2,3},{3,2},{4,5},{5,4},{6,7},{7,6},{8,9},{9,8},{10,11... | collective-permute-start | bytes 786440 | tf_op jit(solution)/shard_map/ppermute | solution.py:488
  62.1 1.5 %collective-permute-start.11 = (bf16[128,512]{1,0:T(8,128)(2,1)S(1)}, bf16[128,512]{1,0:T(8,128)(2,1)S(1)}, u32[]{:S(2)}, u32[]{:S(2)}) collective-permute-start(bf16[128,512]{1,0:T(8,128)(2,1)S(1)} %get-tuple-element.79), channel_id=1, source_target_pairs={{0,1},{1,0},{2,3},{3,2},{4,5},{5,4},{6,7},{7,6},{8,9},{9,8},{10,11... | collective-permute-start | bytes 393224 | tf_op jit(solution)/shard_map/ppermute | solution.py:488
  (1 other events, 5.9 us)

commit v3 on v2

--- a/solution.py
+++ b/solution.py
@@ -21,6 +21,10 @@
 
 def lanes_of(shape):
     return lax.broadcasted_iota(jnp.int32, shape, 1)
+
+
+def bit_of(i):
+    return (lax.axis_index("seq") >> i) & 1
 
 
 def split(x):
@@ -111,18 +115,18 @@
     return out.astype(BF16)
 
 
-def load_kernel(meta, *refs):
+def load_kernel(*refs):
     count = (len(refs) - 1) // 2
     sources, outs, sem = refs[:count], refs[count : 2 * count], refs[-1]
     copies = []
     for i, (source, out) in enumerate(zip(sources, outs)):
         if len(out.shape) == 3:
             size = out.shape[2]
-            share = meta[meta.shape[0] - 1]
+            share = lax.axis_index("parts")
             source, out = source.at[:, pl.ds(pl.multiple_of(share * size, size), size)], out.at[0]
         elif out.shape[1] < source.shape[1]:
             size = out.shape[1]
-            source = source.at[:, pl.ds(pl.multiple_of(meta[0] * size, size), size)]
+            source = source.at[:, pl.ds(pl.multiple_of(bit_of(0) * size, size), size)]
         copies.append(pltpu.make_async_copy(source, out, sem.at[i]))
     for copy in copies:
         copy.start()
@@ -130,11 +134,11 @@
         copy.wait()
 
 
-def sums_kernel(meta, ko, kr, vo, vr, fo, fr, go, gr, pg, tg, pw, tw, gf, uf, ks, kt):
+def sums_kernel(ko, kr, vo, vr, fo, fr, go, gr, pg, tg, pw, tw, gf, uf, ks, kt):
     half = gf.shape[0]
     width = gf.shape[1]
     body = width // 2
-    core = meta[0]
+    core = bit_of(0)
     forget = gates(fo, fr, core, half)
     beta = gates(go, gr, core, half)
     level = running_sum(forget)
@@ -180,39 +184,46 @@
         pw[h] = state.astype(BF16)
 
 
-def join_kernel(which, has_prefix, goes_on, meta, t, got, *rest):
+def join_kernel(which, has_prefix, goes_on, t, got, *rest):
     sent, before_new, coef = rest[has_prefix : has_prefix + 3]
     before = rest[0]
     t_new = rest[-1]
-    bit = meta[which] == 1
+    bit = bit_of(which) == 1
     half, rows, width = t.shape
     body = rows - 8
+    tails = t[:, body:]
+    ends = got[:, body:].astype(F32)
+    mine = tails[:, 1:2]
+    theirs = ends[:, 1:2] + ends[:, 2:3] + ends[:, 3:4]
+    a = jnp.where(bit, 1.0, jnp.exp(theirs))
+    b = jnp.where(bit, jnp.exp(mine), 1.0)
+    arrived = got[:, :body].astype(F32)
+    packed = a * t[:, :body] + b * arrived
+    diag = a * tails[:, :1] + b * ends[:, :1]
+    level = mine + theirs
+    if has_prefix:
+        old = before[:, body:]
+        e = jnp.where(bit, jnp.exp(old[:, 1:2]), 0.0)
+        prefix = before[:, :body] + e * arrived
+        prefix_diag = old[:, :1] + e * ends[:, :1]
+        prefix_level = old[:, 1:2] + jnp.where(bit, theirs, 0.0)
+    else:
+        e = jnp.where(bit, jnp.ones_like(mine), 0.0)
+        prefix = e * arrived
+        prefix_diag = e * ends[:, :1]
+        prefix_level = jnp.where(bit, theirs, 0.0)
+    r = rows_of((8, width))
+    sent[:, :body] = packed.astype(BF16)
     for h in range(half):
-        tail = t[h, body:]
-        mine = tail[1:2]
-        ends = got[h, body:].astype(F32)
-        theirs = ends[1:2] + ends[2:3] + ends[3:4]
-        a = jnp.where(bit, 1.0, jnp.exp(theirs))
-        b = jnp.where(bit, jnp.exp(mine), 1.0)
-        arrived = got[h, :body].astype(F32)
-        packed = a * t[h, :body] + b * arrived
-        diag = a * tail[:1] + b * ends[:1]
-        if goes_on:
-            t_new[h, :body] = packed
-            t_new[h, body:] = tail_rows(diag, mine + theirs)
-        sent[h, :body] = packed.astype(BF16)
-        sent[h, body:] = tail_sent(diag, mine + theirs)
-        if has_prefix:
-            old = before[h, body:]
-            e = jnp.where(bit, jnp.exp(old[1:2]), 0.0)
-            before_new[h, :body] = before[h, :body] + e * arrived
-            before_new[h, body:] = tail_rows(old[:1] + e * ends[:1], old[1:2] + jnp.where(bit, theirs, 0.0))
-        else:
-            e = jnp.where(bit, jnp.ones_like(mine), 0.0)
-            before_new[h, :body] = e * arrived
-            before_new[h, body:] = tail_rows(e * ends[:1], jnp.where(bit, theirs, 0.0))
-        r = rows_of((8, width))
-        coef[h] = jnp.where(r == 0, a, jnp.where(r == 1, b, jnp.where(r == 2, e, 0.0)))
+        sent[h, body:] = tail_sent(diag[h], level[h])
+    before_new[:, :body] = prefix
+    for h in range(half):
+        before_new[h, body:] = tail_rows(prefix_diag[h], prefix_level[h])
+        coef[h] = jnp.where(r == 0, a[h], jnp.where(r == 1, b[h], jnp.where(r == 2, e[h], 0.0)))
+    if goes_on:
+        t_new[:, :body] = packed
+        for h in range(half):
+            t_new[h, body:] = tail_rows(diag[h], level[h])
 
 
 def join_state_kernel(has_prefix, goes_on, coef, t, got, *rest):
@@ -230,13 +241,14 @@
         before_new[h] = before[h] + add if has_prefix else add
 
 
-def prepare_kernel(meta, ridge, ks, kt, qo, qr, fo, fr, go, gr, q_s, m_s, e_s, base):
+def prepare_kernel(ridge, ks, kt, qo, qr, fo, fr, go, gr, q_s, m_s, e_s, base):
     pairs, _, tokens, width = ks.shape
     half = pairs // 2
-    core = meta[0]
+    core = bit_of(0)
     beta = gates(go, gr, core, half)
     level = running_sum(gates(fo, fr, core, half))
     level_t = level.T
+    scale_t = jnp.exp(level_t)
     square = (tokens, tokens)
     lower = rows_of(square) >= lanes_of(square)
     eye = (rows_of((width, width)) == lanes_of((width, width))).astype(F32)
@@ -248,17 +260,17 @@
             base[p] = cross + ridge_of(ridge, core, h, half) * eye
             column = level_t[:, p : p + 1]
             m_s[p] = jnp.where(lower, jnp.exp(jnp.minimum(column - level[p : p + 1], 0.0)) * beta[p : p + 1], 0.0)
-            e_s[p] = jnp.broadcast_to(jnp.exp(column), square)
+            e_s[p] = jnp.broadcast_to(scale_t[:, p : p + 1], square)
             q_s[p] = unit_rows(columns(qref, core, h, half, width).astype(F32))
 
 
-def inverse_kernel(which, meta, base, fo, fr, gf, before, got, s_s, p_s, a_s):
+def inverse_kernel(which, base, fo, fr, gf, before, got, s_s, p_s, a_s):
     half, width, _ = gf.shape
     body = width // 2
     pairs = 2 * half
-    core = meta[0]
+    core = bit_of(0)
     first = core == 0
-    bit = meta[which] == 1
+    bit = bit_of(which) == 1
     forget = gates(fo, fr, core, half)
     decay = jnp.exp(jnp.sum(forget, axis=1, keepdims=True))
     eye = (rows_of((width, width)) == lanes_of((width, width))).astype(F32)
@@ -295,10 +307,10 @@
             p_s[p] = now + dot(now.astype(BF16), rest.astype(BF16))
 
 
-def correct_kernel(meta, ridge, q_s, kt, m_s, e_s, ks, s_s, p_s, vo, vr, xs, part, x_s):
+def correct_kernel(ridge, q_s, kt, m_s, e_s, ks, s_s, p_s, vo, vr, xs, part, x_s):
     pairs, _, width = q_s.shape
     half = pairs // 2
-    core = meta[0]
+    core = bit_of(0)
 
     def both_of(p, i):
         return jnp.concatenate([s_s[p, i], kt[p, i]], axis=1)
@@ -347,13 +359,13 @@
             part[p] = dot(jnp.concatenate([sh, sl], axis=1), jnp.concatenate([v, v], axis=0))
 
 
-def read_kernel(which, meta, xs, part, e_s, fo, fr, uf, before_g, before, got, gain, y_own, y_other):
+def read_kernel(which, xs, part, e_s, fo, fr, uf, before_g, before, got, gain, y_own, y_other):
     half = uf.shape[0]
     width = uf.shape[1]
     body = width // 2
-    core = meta[0]
+    core = bit_of(0)
     first = core == 0
-    bit = meta[which] == 1
+    bit = bit_of(which) == 1
     decay = jnp.exp(jnp.sum(gates(fo, fr, core, half), axis=1, keepdims=True))
     sides = ((y_own, first), (y_other, jnp.logical_not(first)))
     for h in range(half):
@@ -376,19 +388,19 @@
     out[a.shape[0] :] = b[...]
 
 
-def gathered_rows(meta, y_own, y_other, y):
-    core = meta[0]
+def gathered_rows(y_own, y_other, y):
+    core = bit_of(0)
     size = y_own.shape[1]
     y[:, pl.ds(pl.multiple_of(core * size, size), size)] = y_own[...]
     y[:, pl.ds(pl.multiple_of((1 - core) * size, size), size)] = y_other[...]
 
 
-def project_kernel(table, chips, shares, meta, y_own, y_other, own, other, *rest):
+def project_kernel(table, chips, shares, y_own, y_other, own, other, *rest):
     out, y = rest[-2:]
-    core = meta[0]
-    place = meta[meta.shape[0] - 2]
-    share = meta[meta.shape[0] - 1]
-    gathered_rows(meta, y_own, y_other, y)
+    core = bit_of(0)
+    place = lax.axis_index("seq") >> 1
+    share = lax.axis_index("parts")
+    gathered_rows(y_own, y_other, y)
     width = 2 * own.shape[0]
     size = own.shape[1] // shares
     tokens = y.shape[0]
@@ -417,12 +429,12 @@
         out[:, where] = total.astype(BF16)
 
 
-def project_copy_kernel(table, meta, y_own, y_other, own, other, *rest):
+def project_copy_kernel(table, y_own, y_other, own, other, *rest):
     pieces = rest[:-4]
     out, w, y, sem = rest[-4:]
-    core = meta[0]
-    place = meta[meta.shape[0] - 2]
-    share = meta[meta.shape[0] - 1]
+    core = bit_of(0)
+    place = lax.axis_index("seq") >> 1
+    share = lax.axis_index("parts")
     rows = own.shape[0]
     size = pieces[0].shape[2]
 
@@ -441,7 +453,7 @@
         )
     for copy in copies:
         copy.start()
-    gathered_rows(meta, y_own, y_other, y)
+    gathered_rows(y_own, y_other, y)
     for copy in copies:
         copy.wait()
     out[...] = dot(y[...], w[...]).astype(BF16)
@@ -477,11 +489,6 @@
     chips = sections // 2
     bits = chips.bit_length() - 1
     rows, out_columns = out_weight.shape
-    index = lax.axis_index("seq")
-    steps = lax.iota(jnp.int32, bits + 3)
-    meta = jnp.where(
-        steps == bits + 2, lax.axis_index("parts"), jnp.where(steps == bits + 1, index >> 1, (index >> steps) & 1)
-    )
 
     def swap(array, distance, axis="seq"):
         count = mesh.shape[axis]
@@ -498,7 +505,7 @@
     own, keys_m, values_m, queries_m, forget_m, gate_m, gain_row, ridge_row = call(
         load_kernel,
         (VMEM((1, rows, size), BF16), mine, mine, mine, small, small, VMEM((1, features), F32), VMEM((1, heads), F32)),
-        (meta,),
+        (),
         (),
         (pltpu.SemaphoreType.DMA((len(far_args),)),),
         far_args,
@@ -516,7 +523,7 @@
         sums_kernel,
         (VMEM(sent, BF16), VMEM(packed, F32), VMEM(full, BF16), VMEM(full, F32), VMEM(full, F32), VMEM(full, F32),
          VMEM(two, BF16), VMEM(two, BF16)),
-        (meta,),
+        (),
         (keys_m, keys_o, values_m, values_o, *gate_args),
     )
 
@@ -532,7 +539,7 @@
         pg, before, coef, *tg = call(
             functools.partial(join_kernel, r + 1, len(extra), goes_on),
             (VMEM(sent, BF16), VMEM(packed, F32), VMEM((half, 8, width), F32), *[VMEM(packed, F32)] * goes_on),
-            (meta,),
+            (),
             (*tg, got, *extra),
         )
         extra = () if before_w is None else (before_w,)
@@ -588,27 +595,27 @@
     q_s, m_s, e_s, base = call(
         prepare_kernel,
         (VMEM(many, F32), VMEM(many, F32), VMEM(many, F32), VMEM(many, F32)),
-        (meta,),
+        (),
         (ridge_row, ks, kt, queries_m, queries_o, *gate_args),
     )
     s_s, p_s = call(
         functools.partial(inverse_kernel, last),
         (VMEM(two, BF16), VMEM(many, F32)),
-        (meta,),
+        (),
         (base, *forgets, gf, before, got),
         (VMEM(two, BF16),),
     )
     xs, part = call(
         correct_kernel,
         (VMEM(two, BF16), VMEM(many, F32)),
-        (meta,),
+        (),
         (ridge_row, q_s, kt, m_s, e_s, ks, s_s, p_s, values_m, values_o),
         (VMEM(many, F32),),
     )
     y_own, y_other = call(
         functools.partial(read_kernel, last),
         (VMEM((tokens, half * width), BF16),) * 2,
-        (meta,),
+        (),
         (xs, part, e_s, *forgets, uf, before, before_w, got_w, gain_row),
     )
     y_got = swap(y_other, 1)
@@ -619,7 +626,7 @@
         return call(
             functools.partial(project_kernel, table, chips, parts),
             result,
-            (meta,),
+            (),
             (y_own, y_got, out_weight, weight_o, *pieces),
             (y_full,),
         )
@@ -627,12 +634,12 @@
     return pl.pallas_call(
         functools.partial(project_copy_kernel, table),
         out_shape=result,
-        in_specs=[pl.BlockSpec(memory_space=SMEM), here, here] + [pl.BlockSpec(memory_space=pl.ANY)] * (2 + len(pieces)),
+        in_specs=[here, here] + [pl.BlockSpec(memory_space=pl.ANY)] * (2 + len(pieces)),
         out_specs=here,
         scratch_shapes=[
             VMEM((features, out_columns), BF16), y_full, pltpu.SemaphoreType.DMA((2 + len(table),))
         ],
-    )(meta, y_own, y_got, out_weight, weight_o, *pieces)
+    )(y_own, y_got, out_weight, weight_o, *pieces)
 
 
 def solution(mesh):

time: 65.9 us -> 62.1 us (0.942)
  Pallas kernels: 16.6 us -> 11.7 us
  waiting for transfers between devices: 24.4 us -> 25.4 us
    pallas_call x13, Pallas kernels: 16.6 us -> 11.7 us  [call(): pl.pallas_call(kernel, out_shape=outs, in_specs=[pl.BlockSpec(memory_spac...]
    ppermute x29, waiting for transfers between devices: 24.4 us -> 25.4 us  [swap(): return lax.ppermute(array, axis, [(i, i ^ distance) for i in range(count)])]
  transfers between devices with their start and end apart: 29 -> 29, of which waited for: 10 -> 10; matrix products, arithmetic and copies ran while one was open for 0% -> 0% of each run, Pallas kernels for 22% -> 16%
where the time goes in v3:
time: 62.1 us; the launch traced here: 61.9 us
  waiting for transfers between devices  25.4 us (41%)
  starting transfers between devices  24.7 us (40%)
  Pallas kernels  11.7 us (19%)
    ppermute x29, waiting for transfers between devices, swap(): return lax.ppermute(array, axis, [(i, i ^ distance) for i in range(count)])  25.4 us
    ppermute x29, starting transfers between devices, swap(): return lax.ppermute(array, axis, [(i, i ^ distance) for i in range(count)])  24.7 us
    pallas_call x13, Pallas kernels, call(): pl.pallas_call(kernel, out_shape=outs, in_specs=[pl.BlockSpec(memory_spac...  11.7 us
  transfers between devices with their start and end apart: 29, of which 10 were waited for; matrix products, arithmetic and copies ran while one was open for 0% of the time, Pallas kernels for 16%

profile of v3, /device:TPU:0, one launch (start us, length us, event | category | flops | bytes accessed | tf_op | source)
XLA Modules:
  0.0 61.9 jit_solution(15818345736899691507)
XLA Ops:
  0.5 1.2 %shard_map.82 = (bf16[1,64,1024]{2,1,0:T(8,128)(2,1)S(1)}, bf16[128,512]{1,0:T(8,128)(2,1)S(1)}, bf16[128,512]{1,0:T(8,128)(2,1)S(1)}, bf16[128,512]{1,0:T(8,128...) custom-call(bf16[64,2048]{1,0:T(8,128)(2,1)} %own.1, ...), custom_call_target="tpu_custom_call" | custom-call | tf_op jit(solution)/shard_map/pallas_call | solution.py:469
  1.8 4.1 %collective-permute-start.15 = (bf16[1,64,1024]{2,1,0:T(8,128)(2,1)S(1)}, bf16[1,64,1024]{2,1,0:T(8,128)(2,1)S(1)}, u32[]{:S(2)}, u32[]{:S(2)}) collective-permute-start(bf16[1,64,1024]{2,1,0:T(8,128)(2,1)S(1)} %get-tuple-element.80), channel_id=1, source_target_pairs={{0,8},{1,9},{2,10},{3,11},{4,12},{5,13},{6,14},{7,15},{8,0},{9,1},... | collective-permute-start | bytes 393224 | tf_op jit(solution)/shard_map/ppermute | solution.py:495
  6.4 0.7 %collective-permute-done.2.fr = f32[8,128]{1,0:T(8,128)S(1)} collective-permute-done((f32[8,128]{1,0:T(8,128)S(1)}, f32[8,128]{1,0:T(8,128)S(1)}, u32[]{:S(2)}, u32[]{:S(2)}) %collective-permute-start.2) | collective-permute-done | bytes 4128 | tf_op jit(solution)/shard_map/ppermute | solution.py:495
  7.2 1.5 %collective-permute-start.13 = (bf16[64,2048]{1,0:T(8,128)(2,1)S(1)}, bf16[64,2048]{1,0:T(8,128)(2,1)S(1)}, u32[]{:S(2)}, u32[]{:S(2)}) collective-permute-start(bf16[64,2048]{1,0:T(8,128)(2,1)S(1)} %copy-done), channel_id=1, source_target_pairs={{0,2},{1,3},{2,0},{3,1},{4,6},{5,7},{6,4},{7,5},{8,10},{9,11},{10,... | collective-permute-start | bytes 786440 | tf_op jit(solution)/shard_map/ppermute | solution.py:495
  8.8 3.6 %collective-permute-done.15.a = bf16[1,64,1024]{2,1,0:T(8,128)(2,1)S(1)} collective-permute-done((bf16[1,64,1024]{2,1,0:T(8,128)(2,1)S(1)}, bf16[1,64,1024]{2,1,0:T(8,128)(2,1)S(1)}, u32[]{:S(2)}, u32[]{:S(2)}) %collective-permute-start.15) | collective-permute-done | bytes 131104 | tf_op jit(solution)/shard_map/ppermute | solution.py:495
  12.4 0.7 %collective-permute-start.16 = (bf16[1,64,1024]{2,1,0:T(8,128)(2,1)S(1)}, bf16[1,64,1024]{2,1,0:T(8,128)(2,1)S(1)}, u32[]{:S(2)}, u32[]{:S(2)}) collective-permute-start(bf16[1,64,1024]{2,1,0:T(8,128)(2,1)S(1)} %get-tuple-element.80), channel_id=1, source_target_pairs={{0,4},{1,5},{2,6},{3,7},{4,0},{5,1},{6,2},{7,3},{8,12},{9,13},{10,... | collective-permute-start | bytes 393224 | tf_op jit(solution)/shard_map/ppermute | solution.py:495
  13.1 1.3 %collective-permute-start.24 = (bf16[1,64,1024]{2,1,0:T(8,128)(2,1)S(1)}, bf16[1,64,1024]{2,1,0:T(8,128)(2,1)S(1)}, u32[]{:S(2)}, u32[]{:S(2)}) collective-permute-start(bf16[1,64,1024]{2,1,0:T(8,128)(2,1)S(1)} %collective-permute-done.15.a), channel_id=1, source_target_pairs={{0,4},{1,5},{2,6},{3,7},{4,0},{5,1},{6,2},{7,3},{8,12},{9,13},{10,... | collective-permute-start | bytes 393224 | tf_op jit(solution)/shard_map/ppermute | solution.py:495
  14.4 1.0 %shard_map.83 = (bf16[4,80,128]{2,1,0:T(8,128)(2,1)S(1)}, f32[4,72,128]{2,1,0:T(8,128)S(1)}, bf16[4,128,128]{2,1,0:T(8,128)(2,1)S(1)}, f32[4,128,128]{2,1,0:T(8,...) custom-call(bf16[128,512]{1,0:T(8,128)(2,1)S(1)} %get-tuple-element., ...), custom_call_target="tpu_custom_call" | custom-call | tf_op jit(solution)/shard_map/pallas_call | solution.py:469
  15.4 3.2 %collective-permute-done.16.b = bf16[1,64,1024]{2,1,0:T(8,128)(2,1)S(1)} collective-permute-done((bf16[1,64,1024]{2,1,0:T(8,128)(2,1)S(1)}, bf16[1,64,1024]{2,1,0:T(8,128)(2,1)S(1)}, u32[]{:S(2)}, u32[]{:S(2)}) %collective-permute-start.16) | collective-permute-done | bytes 131104 | tf_op jit(solution)/shard_map/ppermute | solution.py:495
  18.6 1.3 %collective-permute-start.5 = (bf16[4,80,128]{2,1,0:T(8,128)(2,1)S(1)}, bf16[4,80,128]{2,1,0:T(8,128)(2,1)S(1)}, u32[]{:S(2)}, u32[]{:S(2)}) collective-permute-start(bf16[4,80,128]{2,1,0:T(8,128)(2,1)S(1)} %get-tuple-element.57), channel_id=1, source_target_pairs={{0,2},{1,3},{2,0},{3,1},{4,6},{5,7},{6,4},{7,5},{8,10},{9,11},{10,... | collective-permute-start | bytes 245768 | tf_op jit(solution)/shard_map/ppermute | solution.py:495
  19.9 0.8 %collective-permute-start.8 = (bf16[4,128,128]{2,1,0:T(8,128)(2,1)S(1)}, bf16[4,128,128]{2,1,0:T(8,128)(2,1)S(1)}, u32[]{:S(2)}, u32[]{:S(2)}) collective-permute-start(bf16[4,128,128]{2,1,0:T(8,128)(2,1)S(1)} %get-tuple-element.71), channel_id=1, source_target_pairs={{0,2},{1,3},{2,0},{3,1},{4,6},{5,7},{6,4},{7,5},{8,10},{9,11},{10,... | collective-permute-start | bytes 393224 | tf_op jit(solution)/shard_map/ppermute | solution.py:495
  20.8 1.3 %collective-permute-start.18 = (bf16[2,64,1024]{2,1,0:T(8,128)(2,1)S(1)}, bf16[2,64,1024]{2,1,0:T(8,128)(2,1)S(1)}, u32[]{:S(2)}, u32[]{:S(2)}) collective-permute-start(bf16[2,64,1024]{2,1,0:T(8,128)(2,1)S(1)} %shard_map.92.rest_2_), channel_id=1, source_target_pairs={{0,16},{16,0},{1,17},{17,1},{2,18},{18,2},{3,19},{19,3},{4,20},{20... | collective-permute-start | bytes 786440 | tf_op jit(solution)/shard_map/ppermute | solution.py:495
  22.0 1.5 %collective-permute-start.20 = (bf16[2,64,1024]{2,1,0:T(8,128)(2,1)S(1)}, bf16[2,64,1024]{2,1,0:T(8,128)(2,1)S(1)}, u32[]{:S(2)}, u32[]{:S(2)}) collective-permute-start(bf16[2,64,1024]{2,1,0:T(8,128)(2,1)S(1)} %shard_map.92.rest_2_), channel_id=1, source_target_pairs={{0,2},{1,3},{2,0},{3,1},{4,6},{5,7},{6,4},{7,5},{8,10},{9,11},{10,... | collective-permute-start | bytes 786440 | tf_op jit(solution)/shard_map/ppermute | solution.py:495
  23.9 1.3 %collective-permute-start.25 = (bf16[1,64,1024]{2,1,0:T(8,128)(2,1)S(1)}, bf16[1,64,1024]{2,1,0:T(8,128)(2,1)S(1)}, u32[]{:S(2)}, u32[]{:S(2)}) collective-permute-start(bf16[1,64,1024]{2,1,0:T(8,128)(2,1)S(1)} %collective-permute-done.24.a), channel_id=1, source_target_pairs={{0,2},{1,3},{2,0},{3,1},{4,6},{5,7},{6,4},{7,5},{8,10},{9,11},{10,... | collective-permute-start | bytes 393224 | tf_op jit(solution)/shard_map/ppermute | solution.py:495
  25.2 1.5 %collective-permute-done.8.got = bf16[4,128,128]{2,1,0:T(8,128)(2,1)S(1)} collective-permute-done((bf16[4,128,128]{2,1,0:T(8,128)(2,1)S(1)}, bf16[4,128,128]{2,1,0:T(8,128)(2,1)S(1)}, u32[]{:S(2)}, u32[]{:S(2)}) %collective-permute-start.8) | collective-permute-done | bytes 131104 | tf_op jit(solution)/shard_map/ppermute | solution.py:495
  26.9 0.8 %collective-permute-start.9 = (bf16[4,128,128]{2,1,0:T(8,128)(2,1)S(1)}, bf16[4,128,128]{2,1,0:T(8,128)(2,1)S(1)}, u32[]{:S(2)}, u32[]{:S(2)}) collective-permute-start(bf16[4,128,128]{2,1,0:T(8,128)(2,1)S(1)} %get-tuple-element.73), channel_id=1, source_target_pairs={{0,4},{1,5},{2,6},{3,7},{4,0},{5,1},{6,2},{7,3},{8,12},{9,13},{10,... | collective-permute-start | bytes 393224 | tf_op jit(solution)/shard_map/ppermute | solution.py:495
  27.7 5.0 %collective-permute-done.25.b = bf16[1,64,1024]{2,1,0:T(8,128)(2,1)S(1)} collective-permute-done((bf16[1,64,1024]{2,1,0:T(8,128)(2,1)S(1)}, bf16[1,64,1024]{2,1,0:T(8,128)(2,1)S(1)}, u32[]{:S(2)}, u32[]{:S(2)}) %collective-permute-start.25) | collective-permute-done | bytes 131104 | tf_op jit(solution)/shard_map/ppermute | solution.py:495
  32.6 1.5 %collective-permute-start.6 = (bf16[4,80,128]{2,1,0:T(8,128)(2,1)S(1)}, bf16[4,80,128]{2,1,0:T(8,128)(2,1)S(1)}, u32[]{:S(2)}, u32[]{:S(2)}) collective-permute-start(bf16[4,80,128]{2,1,0:T(8,128)(2,1)S(1)} %get-tuple-element.59), channel_id=1, source_target_pairs={{0,4},{1,5},{2,6},{3,7},{4,0},{5,1},{6,2},{7,3},{8,12},{9,13},{10,... | collective-permute-start | bytes 245768 | tf_op jit(solution)/shard_map/ppermute | solution.py:495
  34.2 1.2 %collective-permute-start.27 = (bf16[2,64,1024]{2,1,0:T(8,128)(2,1)S(1)}, bf16[2,64,1024]{2,1,0:T(8,128)(2,1)S(1)}, u32[]{:S(2)}, u32[]{:S(2)}) collective-permute-start(bf16[2,64,1024]{2,1,0:T(8,128)(2,1)S(1)} %shard_map.93.rest_10_), channel_id=1, source_target_pairs={{0,16},{16,0},{1,17},{17,1},{2,18},{18,2},{3,19},{19,3},{4,20},{20... | collective-permute-start | bytes 786440 | tf_op jit(solution)/shard_map/ppermute | solution.py:495
  35.3 1.7 %collective-permute-done.6.got = bf16[4,80,128]{2,1,0:T(8,128)(2,1)S(1)} collective-permute-done((bf16[4,80,128]{2,1,0:T(8,128)(2,1)S(1)}, bf16[4,80,128]{2,1,0:T(8,128)(2,1)S(1)}, u32[]{:S(2)}, u32[]{:S(2)}) %collective-permute-start.6) | collective-permute-done | bytes 81952 | tf_op jit(solution)/shard_map/ppermute | solution.py:495
  37.1 1.5 %collective-permute-start.22 = (bf16[2,64,1024]{2,1,0:T(8,128)(2,1)S(1)}, bf16[2,64,1024]{2,1,0:T(8,128)(2,1)S(1)}, u32[]{:S(2)}, u32[]{:S(2)}) collective-permute-start(bf16[2,64,1024]{2,1,0:T(8,128)(2,1)S(1)} %collective-permute-done.18.rest_4_), channel_id=1, source_target_pairs={{0,2},{1,3},{2,0},{3,1},{4,6},{5,7},{6,4},{7,5},{8,10},{9,11},{10,... | collective-permute-start | bytes 786440 | tf_op jit(solution)/shard_map/ppermute | solution.py:495
  38.7 2.6 %collective-permute-start.7 = (bf16[4,80,128]{2,1,0:T(8,128)(2,1)S(1)}, bf16[4,80,128]{2,1,0:T(8,128)(2,1)S(1)}, u32[]{:S(2)}, u32[]{:S(2)}) collective-permute-start(bf16[4,80,128]{2,1,0:T(8,128)(2,1)S(1)} %get-tuple-element.62), channel_id=1, source_target_pairs={{0,8},{1,9},{2,10},{3,11},{4,12},{5,13},{6,14},{7,15},{8,0},{9,1},... | collective-permute-start | bytes 245768 | tf_op jit(solution)/shard_map/ppermute | solution.py:495
  41.8 5.1 %collective-permute-done.7.got = bf16[4,80,128]{2,1,0:T(8,128)(2,1)S(1)} collective-permute-done((bf16[4,80,128]{2,1,0:T(8,128)(2,1)S(1)}, bf16[4,80,128]{2,1,0:T(8,128)(2,1)S(1)}, u32[]{:S(2)}, u32[]{:S(2)}) %collective-permute-start.7) | collective-permute-done | bytes 81952 | tf_op jit(solution)/shard_map/ppermute | solution.py:495
  46.9 0.5 collective-permute-start.19
  47.5 3.1 %collective-permute-done.10.got = bf16[4,128,128]{2,1,0:T(8,128)(2,1)S(1)} collective-permute-done((bf16[4,128,128]{2,1,0:T(8,128)(2,1)S(1)}, bf16[4,128,128]{2,1,0:T(8,128)(2,1)S(1)}, u32[]{:S(2)}, u32[]{:S(2)}) %collective-permute-start.10) | collective-permute-done | bytes 131104 | tf_op jit(solution)/shard_map/ppermute | solution.py:495
  51.2 1.2 %shard_map.84 = (f32[8,128,128]{2,1,0:T(8,128)S(1)}, f32[8,128,128]{2,1,0:T(8,128)S(1)}, f32[8,128,128]{2,1,0:T(8,128)S(1)}, f32[8,128,128]{2,1,0:T(8,128)S(1)}) custom-call(f32[1,8]{1,0:T(1,128)S(1)} %get-tuple-element.43.ridge, bf16[8,2,128,128]{3,2,1,0:T(8,128)(2,1)S(1)} %get-tuple-element.48.ks, bf16[8,2,128,128]{3,2,1,0:T(8,128)(2,1)S(1)} %get-tuple-element.49.kt, ...), custom_call_target="tpu_custom_call" | custom-call | tf_op jit(solution)/shard_map/pallas_call | solution.py:469
  52.3 3.0 %shard_map.87 = (bf16[8,2,128,128]{3,2,1,0:T(8,128)(2,1)S(1)}, f32[8,128,128]{2,1,0:T(8,128)S(1)}) custom-call(f32[8,128,128]{2,1,0:T(8,128)S(1)} %get-tuple-element.54.base, f32[8,128]{1,0:T(8,128)S(1)} %get-tuple-element.46.fo, f32[8,128]{1,0:T(8,128)S(1)} %collective-permute-done.2.fr, f32[4,128,128]{2,1,0:T(8,128)S(1)} %get-tuple-element.55.gf, ...), custom_call_target="tpu_custom_call" | custom-call | tf_op jit(solution)/shard_map/pallas_call | solution.py:469
  55.4 2.9 %shard_map.88 = (bf16[8,2,128,128]{3,2,1,0:T(8,128)(2,1)S(1)}, f32[8,128,128]{2,1,0:T(8,128)S(1)}) custom-call(f32[1,8]{1,0:T(1,128)S(1)} %get-tuple-element.43.ridge, f32[8,128,128]{2,1,0:T(8,128)S(1)} %get-tuple-element.51.q_s, bf16[8,2,128,128]{3,2,1,0:T(8,128)(2,1)S(1)} %get-tuple-element.49.kt, f32[8,128,128]{2,1,0:T(8,128)S(1)} %get-tuple-element.52.m_s, ...), custom_call_target="tpu_custom_call" | custom-call | tf_op jit(solution)/shard_map/pallas_call | solution.py:469
  58.2 0.6 shard_map.91
  58.8 0.5 collective-permute-start.11
  59.3 1.0 %collective-permute-done.11.y_other = bf16[128,512]{1,0:T(8,128)(2,1)S(1)} collective-permute-done((bf16[128,512]{1,0:T(8,128)(2,1)S(1)}, bf16[128,512]{1,0:T(8,128)(2,1)S(1)}, u32[]{:S(2)}, u32[]{:S(2)}) %collective-permute-start.11) | collective-permute-done | bytes 131104 | tf_op jit(solution)/shard_map/ppermute | solution.py:495
  60.3 1.6 %shard_map.94 = bf16[128,2048]{1,0:T(8,128)(2,1)} custom-call(bf16[128,512]{1,0:T(8,128)(2,1)S(1)} %get-tuple-element.78.y_own, bf16[128,512]{1,0:T(8,128)(2,1)S(1)} %collective-permute-done.11.y_other, bf16[64,2048]{1,0:T(8,128)(2,1)S(1)} %copy-done, bf16[64,2048]{1,0:T(8,128)(2,1)S(1)} %collective-permute-done.12.other, ...), custom_call_target="tpu_custom_call" | custom-call | tf_op jit(solution)/shard_map/pallas_call | solution.py:469
  (47 shorter events, 2.9 us)
Async XLA Ops:
  0.0 13.1 %collective-permute-start.1 = (bf16[128,1024]{1,0:T(8,128)(2,1)}, bf16[128,1024]{1,0:T(8,128)(2,1)S(1)}, u32[]{:S(2)}, u32[]{:S(2)}) collective-permute-start(bf16[128,1024]{1,0:T(8,128)(2,1)} %refs_2_.1), channel_id=1, source_target_pairs={{0,1},{1,0},{2,3},{3,2},{4,5},{5,4},{6,7},{7,6},{8,9},{9,8},{10,11... | collective-permute-start | bytes 786440 | tf_op jit(solution)/shard_map/ppermute | solution.py:495
  0.5 13.9 %collective-permute-start = (bf16[128,1024]{1,0:T(8,128)(2,1)}, bf16[128,1024]{1,0:T(8,128)(2,1)S(1)}, u32[]{:S(2)}, u32[]{:S(2)}) collective-permute-start(bf16[128,1024]{1,0:T(8,128)(2,1)} %refs_1_.1), channel_id=1, source_target_pairs={{0,1},{1,0},{2,3},{3,2},{4,5},{5,4},{6,7},{7,6},{8,9},{9,8},{10,11... | collective-permute-start | bytes 786440 | tf_op jit(solution)/shard_map/ppermute | solution.py:495
  0.5 5.4 %copy-start.3 = (f32[8,128]{1,0:T(8,128)S(1)}, f32[8,128]{1,0:T(8,128)}, u32[]{:S(2)}) copy-start(f32[8,128]{1,0:T(8,128)} %refs_5_.1) | copy-start | bytes 12292
  0.5 6.6 %copy-start.1 = (bf16[128,1024]{1,0:T(8,128)(2,1)S(1)}, bf16[128,1024]{1,0:T(8,128)(2,1)}, u32[]{:S(2)}) copy-start(bf16[128,1024]{1,0:T(8,128)(2,1)} %refs_3_.1) | copy-start | bytes 786436
  0.5 6.7 %copy-start = (bf16[64,2048]{1,0:T(8,128)(2,1)S(1)}, bf16[64,2048]{1,0:T(8,128)(2,1)}, u32[]{:S(2)}) copy-start(bf16[64,2048]{1,0:T(8,128)(2,1)} %own.1) | copy-start | bytes 786436
  1.8 10.6 %collective-permute-start.15 = (bf16[1,64,1024]{2,1,0:T(8,128)(2,1)S(1)}, bf16[1,64,1024]{2,1,0:T(8,128)(2,1)S(1)}, u32[]{:S(2)}, u32[]{:S(2)}) collective-permute-start(bf16[1,64,1024]{2,1,0:T(8,128)(2,1)S(1)} %get-tuple-element.80), channel_id=1, source_target_pairs={{0,8},{1,9},{2,10},{3,11},{4,12},{5,13},{6,14},{7,15},{8,0},{9,1},... | collective-permute-start | bytes 393224 | tf_op jit(solution)/shard_map/ppermute | solution.py:495
  5.9 1.2 %collective-permute-start.2 = (f32[8,128]{1,0:T(8,128)S(1)}, f32[8,128]{1,0:T(8,128)S(1)}, u32[]{:S(2)}, u32[]{:S(2)}) collective-permute-start(f32[8,128]{1,0:T(8,128)S(1)} %copy-done.2), channel_id=1, source_target_pairs={{0,1},{1,0},{2,3},{3,2},{4,5},{5,4},{6,7},{7,6},{8,9},{9,8},{10,11... | collective-permute-start | bytes 12296 | tf_op jit(solution)/shard_map/ppermute | solution.py:495
  5.9 1.3 %collective-permute-start.3 = (f32[8,128]{1,0:T(8,128)S(1)}, f32[8,128]{1,0:T(8,128)S(1)}, u32[]{:S(2)}, u32[]{:S(2)}) collective-permute-start(f32[8,128]{1,0:T(8,128)S(1)} %copy-done.3), channel_id=1, source_target_pairs={{0,1},{1,0},{2,3},{3,2},{4,5},{5,4},{6,7},{7,6},{8,9},{9,8},{10,11... | collective-permute-start | bytes 12296 | tf_op jit(solution)/shard_map/ppermute | solution.py:495
  7.1 12.9 %collective-permute-start.4 = (bf16[128,1024]{1,0:T(8,128)(2,1)S(1)}, bf16[128,1024]{1,0:T(8,128)(2,1)S(1)}, u32[]{:S(2)}, u32[]{:S(2)}) collective-permute-start(bf16[128,1024]{1,0:T(8,128)(2,1)S(1)} %copy-done.1), channel_id=1, source_target_pairs={{0,1},{1,0},{2,3},{3,2},{4,5},{5,4},{6,7},{7,6},{8,9},{9,8},{10,11... | collective-permute-start | bytes 786440 | tf_op jit(solution)/shard_map/ppermute | solution.py:495
  7.2 14.8 %collective-permute-start.13 = (bf16[64,2048]{1,0:T(8,128)(2,1)S(1)}, bf16[64,2048]{1,0:T(8,128)(2,1)S(1)}, u32[]{:S(2)}, u32[]{:S(2)}) collective-permute-start(bf16[64,2048]{1,0:T(8,128)(2,1)S(1)} %copy-done), channel_id=1, source_target_pairs={{0,2},{1,3},{2,0},{3,1},{4,6},{5,7},{6,4},{7,5},{8,10},{9,11},{10,... | collective-permute-start | bytes 786440 | tf_op jit(solution)/shard_map/ppermute | solution.py:495
  12.4 6.2 %collective-permute-start.16 = (bf16[1,64,1024]{2,1,0:T(8,128)(2,1)S(1)}, bf16[1,64,1024]{2,1,0:T(8,128)(2,1)S(1)}, u32[]{:S(2)}, u32[]{:S(2)}) collective-permute-start(bf16[1,64,1024]{2,1,0:T(8,128)(2,1)S(1)} %get-tuple-element.80), channel_id=1, source_target_pairs={{0,4},{1,5},{2,6},{3,7},{4,0},{5,1},{6,2},{7,3},{8,12},{9,13},{10,... | collective-permute-start | bytes 393224 | tf_op jit(solution)/shard_map/ppermute | solution.py:495
  13.1 7.6 %collective-permute-start.24 = (bf16[1,64,1024]{2,1,0:T(8,128)(2,1)S(1)}, bf16[1,64,1024]{2,1,0:T(8,128)(2,1)S(1)}, u32[]{:S(2)}, u32[]{:S(2)}) collective-permute-start(bf16[1,64,1024]{2,1,0:T(8,128)(2,1)S(1)} %collective-permute-done.15.a), channel_id=1, source_target_pairs={{0,4},{1,5},{2,6},{3,7},{4,0},{5,1},{6,2},{7,3},{8,12},{9,13},{10,... | collective-permute-start | bytes 393224 | tf_op jit(solution)/shard_map/ppermute | solution.py:495
  14.4 12.5 %collective-permute-start.12 = (bf16[64,2048]{1,0:T(8,128)(2,1)S(1)}, bf16[64,2048]{1,0:T(8,128)(2,1)S(1)}, u32[]{:S(2)}, u32[]{:S(2)}) collective-permute-start(bf16[64,2048]{1,0:T(8,128)(2,1)S(1)} %copy-done), channel_id=1, source_target_pairs={{0,1},{1,0},{2,3},{3,2},{4,5},{5,4},{6,7},{7,6},{8,9},{9,8},{10,11... | collective-permute-start | bytes 786440 | tf_op jit(solution)/shard_map/ppermute | solution.py:495
  18.6 5.3 %collective-permute-start.5 = (bf16[4,80,128]{2,1,0:T(8,128)(2,1)S(1)}, bf16[4,80,128]{2,1,0:T(8,128)(2,1)S(1)}, u32[]{:S(2)}, u32[]{:S(2)}) collective-permute-start(bf16[4,80,128]{2,1,0:T(8,128)(2,1)S(1)} %get-tuple-element.57), channel_id=1, source_target_pairs={{0,2},{1,3},{2,0},{3,1},{4,6},{5,7},{6,4},{7,5},{8,10},{9,11},{10,... | collective-permute-start | bytes 245768 | tf_op jit(solution)/shard_map/ppermute | solution.py:495
  19.9 6.8 %collective-permute-start.8 = (bf16[4,128,128]{2,1,0:T(8,128)(2,1)S(1)}, bf16[4,128,128]{2,1,0:T(8,128)(2,1)S(1)}, u32[]{:S(2)}, u32[]{:S(2)}) collective-permute-start(bf16[4,128,128]{2,1,0:T(8,128)(2,1)S(1)} %get-tuple-element.71), channel_id=1, source_target_pairs={{0,2},{1,3},{2,0},{3,1},{4,6},{5,7},{6,4},{7,5},{8,10},{9,11},{10,... | collective-permute-start | bytes 393224 | tf_op jit(solution)/shard_map/ppermute | solution.py:495
  20.8 13.4 %collective-permute-start.18 = (bf16[2,64,1024]{2,1,0:T(8,128)(2,1)S(1)}, bf16[2,64,1024]{2,1,0:T(8,128)(2,1)S(1)}, u32[]{:S(2)}, u32[]{:S(2)}) collective-permute-start(bf16[2,64,1024]{2,1,0:T(8,128)(2,1)S(1)} %shard_map.92.rest_2_), channel_id=1, source_target_pairs={{0,16},{16,0},{1,17},{17,1},{2,18},{18,2},{3,19},{19,3},{4,20},{20... | collective-permute-start | bytes 786440 | tf_op jit(solution)/shard_map/ppermute | solution.py:495
  22.0 12.2 %collective-permute-start.20 = (bf16[2,64,1024]{2,1,0:T(8,128)(2,1)S(1)}, bf16[2,64,1024]{2,1,0:T(8,128)(2,1)S(1)}, u32[]{:S(2)}, u32[]{:S(2)}) collective-permute-start(bf16[2,64,1024]{2,1,0:T(8,128)(2,1)S(1)} %shard_map.92.rest_2_), channel_id=1, source_target_pairs={{0,2},{1,3},{2,0},{3,1},{4,6},{5,7},{6,4},{7,5},{8,10},{9,11},{10,... | collective-permute-start | bytes 786440 | tf_op jit(solution)/shard_map/ppermute | solution.py:495
  23.9 8.7 %collective-permute-start.25 = (bf16[1,64,1024]{2,1,0:T(8,128)(2,1)S(1)}, bf16[1,64,1024]{2,1,0:T(8,128)(2,1)S(1)}, u32[]{:S(2)}, u32[]{:S(2)}) collective-permute-start(bf16[1,64,1024]{2,1,0:T(8,128)(2,1)S(1)} %collective-permute-done.24.a), channel_id=1, source_target_pairs={{0,2},{1,3},{2,0},{3,1},{4,6},{5,7},{6,4},{7,5},{8,10},{9,11},{10,... | collective-permute-start | bytes 393224 | tf_op jit(solution)/shard_map/ppermute | solution.py:495
  26.8 14.6 %collective-permute-start.17 = (bf16[2,64,1024]{2,1,0:T(8,128)(2,1)S(1)}, bf16[2,64,1024]{2,1,0:T(8,128)(2,1)S(1)}, u32[]{:S(2)}, u32[]{:S(2)}) collective-permute-start(bf16[2,64,1024]{2,1,0:T(8,128)(2,1)S(1)} %shard_map.92.rest_2_), channel_id=1, source_target_pairs={{0,1},{1,0},{2,3},{3,2},{4,5},{5,4},{6,7},{7,6},{8,9},{9,8},{10,11... | collective-permute-start | bytes 786440 | tf_op jit(solution)/shard_map/ppermute | solution.py:495
  26.9 11.8 %collective-permute-start.9 = (bf16[4,128,128]{2,1,0:T(8,128)(2,1)S(1)}, bf16[4,128,128]{2,1,0:T(8,128)(2,1)S(1)}, u32[]{:S(2)}, u32[]{:S(2)}) collective-permute-start(bf16[4,128,128]{2,1,0:T(8,128)(2,1)S(1)} %get-tuple-element.73), channel_id=1, source_target_pairs={{0,4},{1,5},{2,6},{3,7},{4,0},{5,1},{6,2},{7,3},{8,12},{9,13},{10,... | collective-permute-start | bytes 393224 | tf_op jit(solution)/shard_map/ppermute | solution.py:495
  32.6 4.4 %collective-permute-start.6 = (bf16[4,80,128]{2,1,0:T(8,128)(2,1)S(1)}, bf16[4,80,128]{2,1,0:T(8,128)(2,1)S(1)}, u32[]{:S(2)}, u32[]{:S(2)}) collective-permute-start(bf16[4,80,128]{2,1,0:T(8,128)(2,1)S(1)} %get-tuple-element.59), channel_id=1, source_target_pairs={{0,4},{1,5},{2,6},{3,7},{4,0},{5,1},{6,2},{7,3},{8,12},{9,13},{10,... | collective-permute-start | bytes 245768 | tf_op jit(solution)/shard_map/ppermute | solution.py:495
  34.2 12.8 %collective-permute-start.14 = (bf16[64,2048]{1,0:T(8,128)(2,1)S(1)}, bf16[64,2048]{1,0:T(8,128)(2,1)S(1)}, u32[]{:S(2)}, u32[]{:S(2)}) collective-permute-start(bf16[64,2048]{1,0:T(8,128)(2,1)S(1)} %collective-permute-done.13.rest_0_), channel_id=1, source_target_pairs={{0,1},{1,0},{2,3},{3,2},{4,5},{5,4},{6,7},{7,6},{8,9},{9,8},{10,11... | collective-permute-start | bytes 786440 | tf_op jit(solution)/shard_map/ppermute | solution.py:495
  34.2 16.4 %collective-permute-start.27 = (bf16[2,64,1024]{2,1,0:T(8,128)(2,1)S(1)}, bf16[2,64,1024]{2,1,0:T(8,128)(2,1)S(1)}, u32[]{:S(2)}, u32[]{:S(2)}) collective-permute-start(bf16[2,64,1024]{2,1,0:T(8,128)(2,1)S(1)} %shard_map.93.rest_10_), channel_id=1, source_target_pairs={{0,16},{16,0},{1,17},{17,1},{2,18},{18,2},{3,19},{19,3},{4,20},{20... | collective-permute-start | bytes 786440 | tf_op jit(solution)/shard_map/ppermute | solution.py:495
  37.1 14.0 %collective-permute-start.22 = (bf16[2,64,1024]{2,1,0:T(8,128)(2,1)S(1)}, bf16[2,64,1024]{2,1,0:T(8,128)(2,1)S(1)}, u32[]{:S(2)}, u32[]{:S(2)}) collective-permute-start(bf16[2,64,1024]{2,1,0:T(8,128)(2,1)S(1)} %collective-permute-done.18.rest_4_), channel_id=1, source_target_pairs={{0,2},{1,3},{2,0},{3,1},{4,6},{5,7},{6,4},{7,5},{8,10},{9,11},{10,... | collective-permute-start | bytes 786440 | tf_op jit(solution)/shard_map/ppermute | solution.py:495
  38.7 8.3 %collective-permute-start.7 = (bf16[4,80,128]{2,1,0:T(8,128)(2,1)S(1)}, bf16[4,80,128]{2,1,0:T(8,128)(2,1)S(1)}, u32[]{:S(2)}, u32[]{:S(2)}) collective-permute-start(bf16[4,80,128]{2,1,0:T(8,128)(2,1)S(1)} %get-tuple-element.62), channel_id=1, source_target_pairs={{0,8},{1,9},{2,10},{3,11},{4,12},{5,13},{6,14},{7,15},{8,0},{9,1},... | collective-permute-start | bytes 245768 | tf_op jit(solution)/shard_map/ppermute | solution.py:495
  41.4 9.2 %collective-permute-start.10 = (bf16[4,128,128]{2,1,0:T(8,128)(2,1)S(1)}, bf16[4,128,128]{2,1,0:T(8,128)(2,1)S(1)}, u32[]{:S(2)}, u32[]{:S(2)}) collective-permute-start(bf16[4,128,128]{2,1,0:T(8,128)(2,1)S(1)} %get-tuple-element.76), channel_id=1, source_target_pairs={{0,8},{1,9},{2,10},{3,11},{4,12},{5,13},{6,14},{7,15},{8,0},{9,1},... | collective-permute-start | bytes 393224 | tf_op jit(solution)/shard_map/ppermute | solution.py:495
  46.9 11.9 %collective-permute-start.26 = (bf16[2,64,1024]{2,1,0:T(8,128)(2,1)S(1)}, bf16[2,64,1024]{2,1,0:T(8,128)(2,1)S(1)}, u32[]{:S(2)}, u32[]{:S(2)}) collective-permute-start(bf16[2,64,1024]{2,1,0:T(8,128)(2,1)S(1)} %shard_map.93.rest_10_), channel_id=1, source_target_pairs={{0,1},{1,0},{2,3},{3,2},{4,5},{5,4},{6,7},{7,6},{8,9},{9,8},{10,11... | collective-permute-start | bytes 786440 | tf_op jit(solution)/shard_map/ppermute | solution.py:495
  46.9 12.4 %collective-permute-start.19 = (bf16[2,64,1024]{2,1,0:T(8,128)(2,1)S(1)}, bf16[2,64,1024]{2,1,0:T(8,128)(2,1)S(1)}, u32[]{:S(2)}, u32[]{:S(2)}) collective-permute-start(bf16[2,64,1024]{2,1,0:T(8,128)(2,1)S(1)} %collective-permute-done.18.rest_4_), channel_id=1, source_target_pairs={{0,1},{1,0},{2,3},{3,2},{4,5},{5,4},{6,7},{7,6},{8,9},{9,8},{10,11... | collective-permute-start | bytes 786440 | tf_op jit(solution)/shard_map/ppermute | solution.py:495
  50.6 8.8 %collective-permute-start.21 = (bf16[2,64,1024]{2,1,0:T(8,128)(2,1)S(1)}, bf16[2,64,1024]{2,1,0:T(8,128)(2,1)S(1)}, u32[]{:S(2)}, u32[]{:S(2)}) collective-permute-start(bf16[2,64,1024]{2,1,0:T(8,128)(2,1)S(1)} %collective-permute-done.20.rest_6_), channel_id=1, source_target_pairs={{0,1},{1,0},{2,3},{3,2},{4,5},{5,4},{6,7},{7,6},{8,9},{9,8},{10,11... | collective-permute-start | bytes 786440 | tf_op jit(solution)/shard_map/ppermute | solution.py:495
  50.6 9.7 %collective-permute-start.28 = (bf16[2,64,1024]{2,1,0:T(8,128)(2,1)S(1)}, bf16[2,64,1024]{2,1,0:T(8,128)(2,1)S(1)}, u32[]{:S(2)}, u32[]{:S(2)}) collective-permute-start(bf16[2,64,1024]{2,1,0:T(8,128)(2,1)S(1)} %collective-permute-done.27.rest_12_), channel_id=1, source_target_pairs={{0,1},{1,0},{2,3},{3,2},{4,5},{5,4},{6,7},{7,6},{8,9},{9,8},{10,11... | collective-permute-start | bytes 786440 | tf_op jit(solution)/shard_map/ppermute | solution.py:495
  51.1 9.2 %collective-permute-start.23 = (bf16[2,64,1024]{2,1,0:T(8,128)(2,1)S(1)}, bf16[2,64,1024]{2,1,0:T(8,128)(2,1)S(1)}, u32[]{:S(2)}, u32[]{:S(2)}) collective-permute-start(bf16[2,64,1024]{2,1,0:T(8,128)(2,1)S(1)} %collective-permute-done.22.rest_8_), channel_id=1, source_target_pairs={{0,1},{1,0},{2,3},{3,2},{4,5},{5,4},{6,7},{7,6},{8,9},{9,8},{10,11... | collective-permute-start | bytes 786440 | tf_op jit(solution)/shard_map/ppermute | solution.py:495
  58.8 1.5 %collective-permute-start.11 = (bf16[128,512]{1,0:T(8,128)(2,1)S(1)}, bf16[128,512]{1,0:T(8,128)(2,1)S(1)}, u32[]{:S(2)}, u32[]{:S(2)}) collective-permute-start(bf16[128,512]{1,0:T(8,128)(2,1)S(1)} %get-tuple-element.79), channel_id=1, source_target_pairs={{0,1},{1,0},{2,3},{3,2},{4,5},{5,4},{6,7},{7,6},{8,9},{9,8},{10,11... | collective-permute-start | bytes 393224 | tf_op jit(solution)/shard_map/ppermute | solution.py:495
  (1 other events, 5.4 us)

commit v4 on v3

--- a/solution.py
+++ b/solution.py
@@ -12,6 +12,7 @@
 BF16 = jnp.bfloat16
 EXACT = lax.Precision.HIGHEST
 VMEM = pltpu.VMEM
+STRIPS = 2
 GRANT = 8 * 1024 * 1024
 
 
@@ -39,6 +40,14 @@
 def wide(pair):
     high, low = pair
     return jnp.concatenate([high, low, high], axis=1)
+
+
+def beside(pair):
+    return jnp.concatenate(pair, axis=1)
+
+
+def twice(right):
+    return jnp.concatenate([right, right], axis=0)
 
 
 def tall(pair):
@@ -157,7 +166,7 @@
             ks[p, 0], ks[p, 1] = kk
             kt[p, 0], kt[p, 1] = split(turned)
             weighted[p] = split(turned * tails[p : p + 1])
-            grams.append(dot(wide(weighted[p]), tall(kk)))
+            grams.append(dot(beside(weighted[p]), twice(kk[0])))
         early = pick(first, grams[0], grams[1])
         late = pick(first, grams[1], grams[0])
         shrink = pick(first, decay[half + h : half + h + 1], decay[h : h + 1])
@@ -173,7 +182,7 @@
         for side, vref in enumerate((vo, vr)):
             v = columns(vref, core, h, half, width)
             states.append(
-                dot(jnp.concatenate(weighted[h + side * half], axis=1), jnp.concatenate([v, v], axis=0))
+                dot(beside(weighted[h + side * half]), twice(v))
             )
         early_state = pick(first, states[0], states[1])
         late_state = pick(first, states[1], states[0])
@@ -256,7 +265,7 @@
         for h in range(half):
             p = h + side * half
             turned = kt[p, 0].astype(F32) + kt[p, 1].astype(F32)
-            cross = dot(wide(split(turned * beta[p : p + 1])), tall((ks[p, 0], ks[p, 1])))
+            cross = dot(beside(split(turned * beta[p : p + 1])), twice(ks[p, 0]))
             base[p] = cross + ridge_of(ridge, core, h, half) * eye
             column = level_t[:, p : p + 1]
             m_s[p] = jnp.where(lower, jnp.exp(jnp.minimum(column - level[p : p + 1], 0.0)) * beta[p : p + 1], 0.0)
@@ -286,11 +295,11 @@
             s_s[p, 0], s_s[p, 1] = split(gram)
             system = gram + base[p]
             bound = jnp.max(jnp.sum(jnp.abs(system), axis=0, keepdims=True), axis=1, keepdims=True)
-            a_s[p, 0], a_s[p, 1] = split(system)
+            a_s[p] = system.astype(BF16)
             p_s[p] = eye / bound
 
     def refine(_, carry):
-        left = [eye - dot(a_s[p, 0], p_s[p].astype(BF16)) for p in range(pairs)]
+        left = [eye - dot(a_s[p], p_s[p].astype(BF16)) for p in range(pairs)]
         for p in range(pairs):
             now = p_s[p]
             p_s[p] = now + dot(now.astype(BF16), left[p].astype(BF16))
@@ -301,7 +310,8 @@
         group = range(start, start + half)
         left = []
         for p in group:
-            left.append(eye - dot(wide((a_s[p, 0], a_s[p, 1])), tall(split(p_s[p]))))
+            high = a_s[p]
+            left.append(eye - dot(beside((high, high)), jnp.concatenate(split(p_s[p]), axis=0)))
         for p, rest in zip(group, left):
             now = p_s[p]
             p_s[p] = now + dot(now.astype(BF16), rest.astype(BF16))
@@ -356,7 +366,7 @@
         for p, found in zip(group, scores):
             v = columns(vref, core, p - start, half, width)
             sh, sl = split(found)
-            part[p] = dot(jnp.concatenate([sh, sl], axis=1), jnp.concatenate([v, v], axis=0))
+            part[p] = dot(beside((sh, sl)), twice(v))
 
 
 def read_kernel(which, xs, part, e_s, fo, fr, uf, before_g, before, got, gain, y_own, y_other):
@@ -396,7 +406,7 @@
 
 
 def project_kernel(table, chips, shares, y_own, y_other, own, other, *rest):
-    out, y = rest[-2:]
+    result, y, out, sem = rest[-4:]
     core = bit_of(0)
     place = lax.axis_index("seq") >> 1
     share = lax.axis_index("parts")
@@ -410,23 +420,32 @@
         rows = y[:, pl.ds(pl.multiple_of(chip * width, width), width)].astype(F32)
         rows = jnp.where(core == 0, rows, pltpu.roll(rows, width // 2, 1))
         lefts.append(rows.astype(BF16))
+    copies = []
+    strip = size // STRIPS
     for q in range(shares):
-        where = pl.ds(pl.multiple_of(jnp.bitwise_xor(share, q) * size, size), size)
-        total = jnp.zeros((tokens, size), F32)
-        for offset in range(0, chips, 2):
-            blocks = []
-            for o in (offset, offset + 1):
-                for flip in (0, 1):
-                    if o == 0:
-                        blocks.append((own, other)[flip][:, where])
-                    elif (o, flip, None) in table:
-                        blocks.append(rest[table[o, flip, None][0]][:, where])
-                    else:
-                        piece, i = table[o, flip, q]
-                        blocks.append(rest[piece][i])
-            left = jnp.concatenate([lefts[offset], lefts[offset + 1]], axis=1)
-            total = total + dot(left, jnp.concatenate(blocks, axis=0))
-        out[:, where] = total.astype(BF16)
+        for n in range(STRIPS):
+            start = jnp.bitwise_xor(share, q) * size + n * strip
+            where = pl.ds(pl.multiple_of(start, strip), strip)
+            inner = slice(n * strip, (n + 1) * strip)
+            total = jnp.zeros((tokens, strip), F32)
+            for offset in range(0, chips, 2):
+                blocks = []
+                for o in (offset, offset + 1):
+                    for flip in (0, 1):
+                        if o == 0:
+                            blocks.append((own, other)[flip][:, where])
+                        elif (o, flip, None) in table:
+                            blocks.append(rest[table[o, flip, None][0]][:, where])
+                        else:
+                            piece, i = table[o, flip, q]
+                            blocks.append(rest[piece][i, :, inner])
+                left = jnp.concatenate([lefts[offset], lefts[offset + 1]], axis=1)
+                total = total + dot(left, jnp.concatenate(blocks, axis=0))
+            out[:, where] = total.astype(BF16)
+            copies.append(pltpu.make_async_copy(out.at[:, where], result.at[:, where], sem.at[len(copies)]))
+            copies[-1].start()
+    for copy in copies:
+        copy.wait()
 
 
 def project_copy_kernel(table, y_own, y_other, own, other, *rest):
@@ -462,7 +481,7 @@
 SMEM = pltpu.SMEM
 
 
-def call(kernel, outs, scalars, ins, scratch=(), far=()):
+def call(kernel, outs, scalars, ins, scratch=(), far=(), out_space=VMEM):
     spec = pl.BlockSpec(memory_space=VMEM)
     near = [pltpu.with_memory_space_constraint(a, VMEM) for a in ins]
     far = [pltpu.with_memory_space_constraint(a, pltpu.HBM) for a in far]
@@ -472,7 +491,7 @@
         in_specs=[pl.BlockSpec(memory_space=SMEM)] * len(scalars)
         + [spec] * len(near)
         + [pl.BlockSpec(memory_space=pltpu.HBM)] * len(far),
-        out_specs=jax.tree.map(lambda _: spec, outs),
+        out_specs=jax.tree.map(lambda _: pl.BlockSpec(memory_space=out_space), outs),
         scratch_shapes=scratch,
         compiler_params=pltpu.CompilerParams(vmem_limit_bytes=GRANT),
     )(*scalars, *near, *far)
@@ -603,7 +622,7 @@
         (VMEM(two, BF16), VMEM(many, F32)),
         (),
         (base, *forgets, gf, before, got),
-        (VMEM(two, BF16),),
+        (VMEM(many, BF16),),
     )
     xs, part = call(
         correct_kernel,
@@ -628,7 +647,8 @@
             result,
             (),
             (y_own, y_got, out_weight, weight_o, *pieces),
-            (y_full,),
+            (y_full, VMEM((tokens, out_columns), BF16), pltpu.SemaphoreType.DMA((parts * STRIPS,))),
+            out_space=pl.ANY,
         )
     here = pl.BlockSpec(memory_space=VMEM)
     return pl.pallas_call(

time: 62.1 us -> 61.9 us (level)
  no operation moved by 1% of the time
where the time goes in v4:
time: 61.9 us; the launch traced here: 61.7 us
  waiting for transfers between devices  25.6 us (41%)
  starting transfers between devices  24.7 us (40%)
  Pallas kernels  11.3 us (18%)
    ppermute x29, waiting for transfers between devices, swap(): return lax.ppermute(array, axis, [(i, i ^ distance) for i in range(count)])  25.6 us
    ppermute x29, starting transfers between devices, swap(): return lax.ppermute(array, axis, [(i, i ^ distance) for i in range(count)])  24.7 us
    pallas_call x13, Pallas kernels, call(): pl.pallas_call(kernel, out_shape=outs, in_specs=[pl.BlockSpec(memory_spac...  11.3 us
  transfers between devices with their start and end apart: 29, of which 10 were waited for; matrix products, arithmetic and copies ran while one was open for 0% of the time, Pallas kernels for 16%

profile of v4, /device:TPU:0, one launch (start us, length us, event | category | flops | bytes accessed | tf_op | source)
XLA Modules:
  0.0 61.7 jit_solution(13826397737779945520)
XLA Ops:
  0.5 1.2 %shard_map.82 = (bf16[1,64,1024]{2,1,0:T(8,128)(2,1)S(1)}, bf16[128,512]{1,0:T(8,128)(2,1)S(1)}, bf16[128,512]{1,0:T(8,128)(2,1)S(1)}, bf16[128,512]{1,0:T(8,128...) custom-call(bf16[64,2048]{1,0:T(8,128)(2,1)} %own.1, ...), custom_call_target="tpu_custom_call" | custom-call | tf_op jit(solution)/shard_map/pallas_call | solution.py:488
  1.8 4.1 %collective-permute-start.15 = (bf16[1,64,1024]{2,1,0:T(8,128)(2,1)S(1)}, bf16[1,64,1024]{2,1,0:T(8,128)(2,1)S(1)}, u32[]{:S(2)}, u32[]{:S(2)}) collective-permute-start(bf16[1,64,1024]{2,1,0:T(8,128)(2,1)S(1)} %get-tuple-element.80), channel_id=1, source_target_pairs={{0,8},{1,9},{2,10},{3,11},{4,12},{5,13},{6,14},{7,15},{8,0},{9,1},... | collective-permute-start | bytes 393224 | tf_op jit(solution)/shard_map/ppermute | solution.py:514
  6.4 0.7 %collective-permute-done.2.fr = f32[8,128]{1,0:T(8,128)S(1)} collective-permute-done((f32[8,128]{1,0:T(8,128)S(1)}, f32[8,128]{1,0:T(8,128)S(1)}, u32[]{:S(2)}, u32[]{:S(2)}) %collective-permute-start.2) | collective-permute-done | bytes 4128 | tf_op jit(solution)/shard_map/ppermute | solution.py:514
  7.2 1.5 %collective-permute-start.13 = (bf16[64,2048]{1,0:T(8,128)(2,1)S(1)}, bf16[64,2048]{1,0:T(8,128)(2,1)S(1)}, u32[]{:S(2)}, u32[]{:S(2)}) collective-permute-start(bf16[64,2048]{1,0:T(8,128)(2,1)S(1)} %copy-done), channel_id=1, source_target_pairs={{0,2},{1,3},{2,0},{3,1},{4,6},{5,7},{6,4},{7,5},{8,10},{9,11},{10,... | collective-permute-start | bytes 786440 | tf_op jit(solution)/shard_map/ppermute | solution.py:514
  8.8 3.6 %collective-permute-done.15.a = bf16[1,64,1024]{2,1,0:T(8,128)(2,1)S(1)} collective-permute-done((bf16[1,64,1024]{2,1,0:T(8,128)(2,1)S(1)}, bf16[1,64,1024]{2,1,0:T(8,128)(2,1)S(1)}, u32[]{:S(2)}, u32[]{:S(2)}) %collective-permute-start.15) | collective-permute-done | bytes 131104 | tf_op jit(solution)/shard_map/ppermute | solution.py:514
  12.4 0.7 %collective-permute-start.16 = (bf16[1,64,1024]{2,1,0:T(8,128)(2,1)S(1)}, bf16[1,64,1024]{2,1,0:T(8,128)(2,1)S(1)}, u32[]{:S(2)}, u32[]{:S(2)}) collective-permute-start(bf16[1,64,1024]{2,1,0:T(8,128)(2,1)S(1)} %get-tuple-element.80), channel_id=1, source_target_pairs={{0,4},{1,5},{2,6},{3,7},{4,0},{5,1},{6,2},{7,3},{8,12},{9,13},{10,... | collective-permute-start | bytes 393224 | tf_op jit(solution)/shard_map/ppermute | solution.py:514
  13.1 1.3 %collective-permute-start.24 = (bf16[1,64,1024]{2,1,0:T(8,128)(2,1)S(1)}, bf16[1,64,1024]{2,1,0:T(8,128)(2,1)S(1)}, u32[]{:S(2)}, u32[]{:S(2)}) collective-permute-start(bf16[1,64,1024]{2,1,0:T(8,128)(2,1)S(1)} %collective-permute-done.15.a), channel_id=1, source_target_pairs={{0,4},{1,5},{2,6},{3,7},{4,0},{5,1},{6,2},{7,3},{8,12},{9,13},{10,... | collective-permute-start | bytes 393224 | tf_op jit(solution)/shard_map/ppermute | solution.py:514
  14.4 0.8 %shard_map.83 = (bf16[4,80,128]{2,1,0:T(8,128)(2,1)S(1)}, f32[4,72,128]{2,1,0:T(8,128)S(1)}, bf16[4,128,128]{2,1,0:T(8,128)(2,1)S(1)}, f32[4,128,128]{2,1,0:T(8,...) custom-call(bf16[128,512]{1,0:T(8,128)(2,1)S(1)} %get-tuple-element., ...), custom_call_target="tpu_custom_call" | custom-call | tf_op jit(solution)/shard_map/pallas_call | solution.py:488
  15.2 3.4 %collective-permute-done.16.b = bf16[1,64,1024]{2,1,0:T(8,128)(2,1)S(1)} collective-permute-done((bf16[1,64,1024]{2,1,0:T(8,128)(2,1)S(1)}, bf16[1,64,1024]{2,1,0:T(8,128)(2,1)S(1)}, u32[]{:S(2)}, u32[]{:S(2)}) %collective-permute-start.16) | collective-permute-done | bytes 131104 | tf_op jit(solution)/shard_map/ppermute | solution.py:514
  18.6 1.3 %collective-permute-start.5 = (bf16[4,80,128]{2,1,0:T(8,128)(2,1)S(1)}, bf16[4,80,128]{2,1,0:T(8,128)(2,1)S(1)}, u32[]{:S(2)}, u32[]{:S(2)}) collective-permute-start(bf16[4,80,128]{2,1,0:T(8,128)(2,1)S(1)} %get-tuple-element.57), channel_id=1, source_target_pairs={{0,2},{1,3},{2,0},{3,1},{4,6},{5,7},{6,4},{7,5},{8,10},{9,11},{10,... | collective-permute-start | bytes 245768 | tf_op jit(solution)/shard_map/ppermute | solution.py:514
  19.9 0.8 %collective-permute-start.8 = (bf16[4,128,128]{2,1,0:T(8,128)(2,1)S(1)}, bf16[4,128,128]{2,1,0:T(8,128)(2,1)S(1)}, u32[]{:S(2)}, u32[]{:S(2)}) collective-permute-start(bf16[4,128,128]{2,1,0:T(8,128)(2,1)S(1)} %get-tuple-element.71), channel_id=1, source_target_pairs={{0,2},{1,3},{2,0},{3,1},{4,6},{5,7},{6,4},{7,5},{8,10},{9,11},{10,... | collective-permute-start | bytes 393224 | tf_op jit(solution)/shard_map/ppermute | solution.py:514
  20.8 1.3 %collective-permute-start.18 = (bf16[2,64,1024]{2,1,0:T(8,128)(2,1)S(1)}, bf16[2,64,1024]{2,1,0:T(8,128)(2,1)S(1)}, u32[]{:S(2)}, u32[]{:S(2)}) collective-permute-start(bf16[2,64,1024]{2,1,0:T(8,128)(2,1)S(1)} %shard_map.92.rest_2_), channel_id=1, source_target_pairs={{0,16},{16,0},{1,17},{17,1},{2,18},{18,2},{3,19},{19,3},{4,20},{20... | collective-permute-start | bytes 786440 | tf_op jit(solution)/shard_map/ppermute | solution.py:514
  22.0 1.5 %collective-permute-start.20 = (bf16[2,64,1024]{2,1,0:T(8,128)(2,1)S(1)}, bf16[2,64,1024]{2,1,0:T(8,128)(2,1)S(1)}, u32[]{:S(2)}, u32[]{:S(2)}) collective-permute-start(bf16[2,64,1024]{2,1,0:T(8,128)(2,1)S(1)} %shard_map.92.rest_2_), channel_id=1, source_target_pairs={{0,2},{1,3},{2,0},{3,1},{4,6},{5,7},{6,4},{7,5},{8,10},{9,11},{10,... | collective-permute-start | bytes 786440 | tf_op jit(solution)/shard_map/ppermute | solution.py:514
  23.9 1.3 %collective-permute-start.25 = (bf16[1,64,1024]{2,1,0:T(8,128)(2,1)S(1)}, bf16[1,64,1024]{2,1,0:T(8,128)(2,1)S(1)}, u32[]{:S(2)}, u32[]{:S(2)}) collective-permute-start(bf16[1,64,1024]{2,1,0:T(8,128)(2,1)S(1)} %collective-permute-done.24.a), channel_id=1, source_target_pairs={{0,2},{1,3},{2,0},{3,1},{4,6},{5,7},{6,4},{7,5},{8,10},{9,11},{10,... | collective-permute-start | bytes 393224 | tf_op jit(solution)/shard_map/ppermute | solution.py:514
  25.2 1.5 %collective-permute-done.8.got = bf16[4,128,128]{2,1,0:T(8,128)(2,1)S(1)} collective-permute-done((bf16[4,128,128]{2,1,0:T(8,128)(2,1)S(1)}, bf16[4,128,128]{2,1,0:T(8,128)(2,1)S(1)}, u32[]{:S(2)}, u32[]{:S(2)}) %collective-permute-start.8) | collective-permute-done | bytes 131104 | tf_op jit(solution)/shard_map/ppermute | solution.py:514
  26.9 0.8 %collective-permute-start.9 = (bf16[4,128,128]{2,1,0:T(8,128)(2,1)S(1)}, bf16[4,128,128]{2,1,0:T(8,128)(2,1)S(1)}, u32[]{:S(2)}, u32[]{:S(2)}) collective-permute-start(bf16[4,128,128]{2,1,0:T(8,128)(2,1)S(1)} %get-tuple-element.73), channel_id=1, source_target_pairs={{0,4},{1,5},{2,6},{3,7},{4,0},{5,1},{6,2},{7,3},{8,12},{9,13},{10,... | collective-permute-start | bytes 393224 | tf_op jit(solution)/shard_map/ppermute | solution.py:514
  27.7 5.0 %collective-permute-done.25.b = bf16[1,64,1024]{2,1,0:T(8,128)(2,1)S(1)} collective-permute-done((bf16[1,64,1024]{2,1,0:T(8,128)(2,1)S(1)}, bf16[1,64,1024]{2,1,0:T(8,128)(2,1)S(1)}, u32[]{:S(2)}, u32[]{:S(2)}) %collective-permute-start.25) | collective-permute-done | bytes 131104 | tf_op jit(solution)/shard_map/ppermute | solution.py:514
  32.6 1.5 %collective-permute-start.6 = (bf16[4,80,128]{2,1,0:T(8,128)(2,1)S(1)}, bf16[4,80,128]{2,1,0:T(8,128)(2,1)S(1)}, u32[]{:S(2)}, u32[]{:S(2)}) collective-permute-start(bf16[4,80,128]{2,1,0:T(8,128)(2,1)S(1)} %get-tuple-element.59), channel_id=1, source_target_pairs={{0,4},{1,5},{2,6},{3,7},{4,0},{5,1},{6,2},{7,3},{8,12},{9,13},{10,... | collective-permute-start | bytes 245768 | tf_op jit(solution)/shard_map/ppermute | solution.py:514
  34.2 1.2 %collective-permute-start.27 = (bf16[2,64,1024]{2,1,0:T(8,128)(2,1)S(1)}, bf16[2,64,1024]{2,1,0:T(8,128)(2,1)S(1)}, u32[]{:S(2)}, u32[]{:S(2)}) collective-permute-start(bf16[2,64,1024]{2,1,0:T(8,128)(2,1)S(1)} %shard_map.93.rest_10_), channel_id=1, source_target_pairs={{0,16},{16,0},{1,17},{17,1},{2,18},{18,2},{3,19},{19,3},{4,20},{20... | collective-permute-start | bytes 786440 | tf_op jit(solution)/shard_map/ppermute | solution.py:514
  35.3 1.7 %collective-permute-done.6.got = bf16[4,80,128]{2,1,0:T(8,128)(2,1)S(1)} collective-permute-done((bf16[4,80,128]{2,1,0:T(8,128)(2,1)S(1)}, bf16[4,80,128]{2,1,0:T(8,128)(2,1)S(1)}, u32[]{:S(2)}, u32[]{:S(2)}) %collective-permute-start.6) | collective-permute-done | bytes 81952 | tf_op jit(solution)/shard_map/ppermute | solution.py:514
  37.1 1.5 %collective-permute-start.22 = (bf16[2,64,1024]{2,1,0:T(8,128)(2,1)S(1)}, bf16[2,64,1024]{2,1,0:T(8,128)(2,1)S(1)}, u32[]{:S(2)}, u32[]{:S(2)}) collective-permute-start(bf16[2,64,1024]{2,1,0:T(8,128)(2,1)S(1)} %collective-permute-done.18.rest_4_), channel_id=1, source_target_pairs={{0,2},{1,3},{2,0},{3,1},{4,6},{5,7},{6,4},{7,5},{8,10},{9,11},{10,... | collective-permute-start | bytes 786440 | tf_op jit(solution)/shard_map/ppermute | solution.py:514
  38.7 2.6 %collective-permute-start.7 = (bf16[4,80,128]{2,1,0:T(8,128)(2,1)S(1)}, bf16[4,80,128]{2,1,0:T(8,128)(2,1)S(1)}, u32[]{:S(2)}, u32[]{:S(2)}) collective-permute-start(bf16[4,80,128]{2,1,0:T(8,128)(2,1)S(1)} %get-tuple-element.62), channel_id=1, source_target_pairs={{0,8},{1,9},{2,10},{3,11},{4,12},{5,13},{6,14},{7,15},{8,0},{9,1},... | collective-permute-start | bytes 245768 | tf_op jit(solution)/shard_map/ppermute | solution.py:514
  41.8 5.1 %collective-permute-done.7.got = bf16[4,80,128]{2,1,0:T(8,128)(2,1)S(1)} collective-permute-done((bf16[4,80,128]{2,1,0:T(8,128)(2,1)S(1)}, bf16[4,80,128]{2,1,0:T(8,128)(2,1)S(1)}, u32[]{:S(2)}, u32[]{:S(2)}) %collective-permute-start.7) | collective-permute-done | bytes 81952 | tf_op jit(solution)/shard_map/ppermute | solution.py:514
  46.9 0.5 collective-permute-start.19
  47.5 3.1 %collective-permute-done.10.got = bf16[4,128,128]{2,1,0:T(8,128)(2,1)S(1)} collective-permute-done((bf16[4,128,128]{2,1,0:T(8,128)(2,1)S(1)}, bf16[4,128,128]{2,1,0:T(8,128)(2,1)S(1)}, u32[]{:S(2)}, u32[]{:S(2)}) %collective-permute-start.10) | collective-permute-done | bytes 131104 | tf_op jit(solution)/shard_map/ppermute | solution.py:514
  50.6 0.5 collective-permute-start.28
  51.2 1.2 %shard_map.84 = (f32[8,128,128]{2,1,0:T(8,128)S(1)}, f32[8,128,128]{2,1,0:T(8,128)S(1)}, f32[8,128,128]{2,1,0:T(8,128)S(1)}, f32[8,128,128]{2,1,0:T(8,128)S(1)}) custom-call(f32[1,8]{1,0:T(1,128)S(1)} %get-tuple-element.43.ridge, bf16[8,2,128,128]{3,2,1,0:T(8,128)(2,1)S(1)} %get-tuple-element.48.ks, bf16[8,2,128,128]{3,2,1,0:T(8,128)(2,1)S(1)} %get-tuple-element.49.kt, ...), custom_call_target="tpu_custom_call" | custom-call | tf_op jit(solution)/shard_map/pallas_call | solution.py:488
  52.3 2.9 %shard_map.87 = (bf16[8,2,128,128]{3,2,1,0:T(8,128)(2,1)S(1)}, f32[8,128,128]{2,1,0:T(8,128)S(1)}) custom-call(f32[8,128,128]{2,1,0:T(8,128)S(1)} %get-tuple-element.54.base, f32[8,128]{1,0:T(8,128)S(1)} %get-tuple-element.46.fo, f32[8,128]{1,0:T(8,128)S(1)} %collective-permute-done.2.fr, f32[4,128,128]{2,1,0:T(8,128)S(1)} %get-tuple-element.55.gf, ...), custom_call_target="tpu_custom_call" | custom-call | tf_op jit(solution)/shard_map/pallas_call | solution.py:488
  55.2 2.9 %shard_map.88 = (bf16[8,2,128,128]{3,2,1,0:T(8,128)(2,1)S(1)}, f32[8,128,128]{2,1,0:T(8,128)S(1)}) custom-call(f32[1,8]{1,0:T(1,128)S(1)} %get-tuple-element.43.ridge, f32[8,128,128]{2,1,0:T(8,128)S(1)} %get-tuple-element.51.q_s, bf16[8,2,128,128]{3,2,1,0:T(8,128)(2,1)S(1)} %get-tuple-element.49.kt, f32[8,128,128]{2,1,0:T(8,128)S(1)} %get-tuple-element.52.m_s, ...), custom_call_target="tpu_custom_call" | custom-call | tf_op jit(solution)/shard_map/pallas_call | solution.py:488
  58.1 0.6 shard_map.91
  59.2 1.0 %collective-permute-done.11.y_other = bf16[128,512]{1,0:T(8,128)(2,1)S(1)} collective-permute-done((bf16[128,512]{1,0:T(8,128)(2,1)S(1)}, bf16[128,512]{1,0:T(8,128)(2,1)S(1)}, u32[]{:S(2)}, u32[]{:S(2)}) %collective-permute-start.11) | collective-permute-done | bytes 131104 | tf_op jit(solution)/shard_map/ppermute | solution.py:514
  60.2 1.5 %shard_map.94 = bf16[128,2048]{1,0:T(8,128)(2,1)} custom-call(bf16[128,512]{1,0:T(8,128)(2,1)S(1)} %get-tuple-element.78.y_own, bf16[128,512]{1,0:T(8,128)(2,1)S(1)} %collective-permute-done.11.y_other, bf16[64,2048]{1,0:T(8,128)(2,1)S(1)} %copy-done, bf16[64,2048]{1,0:T(8,128)(2,1)S(1)} %collective-permute-done.12.other, ...), custom_call_target="tpu_custom_call" | custom-call | tf_op jit(solution)/shard_map/pallas_call | solution.py:488
  (47 shorter events, 2.9 us)
Async XLA Ops:
  0.0 13.1 %collective-permute-start.1 = (bf16[128,1024]{1,0:T(8,128)(2,1)}, bf16[128,1024]{1,0:T(8,128)(2,1)S(1)}, u32[]{:S(2)}, u32[]{:S(2)}) collective-permute-start(bf16[128,1024]{1,0:T(8,128)(2,1)} %refs_2_.1), channel_id=1, source_target_pairs={{0,1},{1,0},{2,3},{3,2},{4,5},{5,4},{6,7},{7,6},{8,9},{9,8},{10,11... | collective-permute-start | bytes 786440 | tf_op jit(solution)/shard_map/ppermute | solution.py:514
  0.5 13.9 %collective-permute-start = (bf16[128,1024]{1,0:T(8,128)(2,1)}, bf16[128,1024]{1,0:T(8,128)(2,1)S(1)}, u32[]{:S(2)}, u32[]{:S(2)}) collective-permute-start(bf16[128,1024]{1,0:T(8,128)(2,1)} %refs_1_.1), channel_id=1, source_target_pairs={{0,1},{1,0},{2,3},{3,2},{4,5},{5,4},{6,7},{7,6},{8,9},{9,8},{10,11... | collective-permute-start | bytes 786440 | tf_op jit(solution)/shard_map/ppermute | solution.py:514
  0.5 5.4 %copy-start.3 = (f32[8,128]{1,0:T(8,128)S(1)}, f32[8,128]{1,0:T(8,128)}, u32[]{:S(2)}) copy-start(f32[8,128]{1,0:T(8,128)} %refs_5_.1) | copy-start | bytes 12292
  0.5 6.6 %copy-start.1 = (bf16[128,1024]{1,0:T(8,128)(2,1)S(1)}, bf16[128,1024]{1,0:T(8,128)(2,1)}, u32[]{:S(2)}) copy-start(bf16[128,1024]{1,0:T(8,128)(2,1)} %refs_3_.1) | copy-start | bytes 786436
  0.5 6.7 %copy-start = (bf16[64,2048]{1,0:T(8,128)(2,1)S(1)}, bf16[64,2048]{1,0:T(8,128)(2,1)}, u32[]{:S(2)}) copy-start(bf16[64,2048]{1,0:T(8,128)(2,1)} %own.1) | copy-start | bytes 786436
  1.8 10.6 %collective-permute-start.15 = (bf16[1,64,1024]{2,1,0:T(8,128)(2,1)S(1)}, bf16[1,64,1024]{2,1,0:T(8,128)(2,1)S(1)}, u32[]{:S(2)}, u32[]{:S(2)}) collective-permute-start(bf16[1,64,1024]{2,1,0:T(8,128)(2,1)S(1)} %get-tuple-element.80), channel_id=1, source_target_pairs={{0,8},{1,9},{2,10},{3,11},{4,12},{5,13},{6,14},{7,15},{8,0},{9,1},... | collective-permute-start | bytes 393224 | tf_op jit(solution)/shard_map/ppermute | solution.py:514
  5.9 1.2 %collective-permute-start.2 = (f32[8,128]{1,0:T(8,128)S(1)}, f32[8,128]{1,0:T(8,128)S(1)}, u32[]{:S(2)}, u32[]{:S(2)}) collective-permute-start(f32[8,128]{1,0:T(8,128)S(1)} %copy-done.2), channel_id=1, source_target_pairs={{0,1},{1,0},{2,3},{3,2},{4,5},{5,4},{6,7},{7,6},{8,9},{9,8},{10,11... | collective-permute-start | bytes 12296 | tf_op jit(solution)/shard_map/ppermute | solution.py:514
  5.9 1.3 %collective-permute-start.3 = (f32[8,128]{1,0:T(8,128)S(1)}, f32[8,128]{1,0:T(8,128)S(1)}, u32[]{:S(2)}, u32[]{:S(2)}) collective-permute-start(f32[8,128]{1,0:T(8,128)S(1)} %copy-done.3), channel_id=1, source_target_pairs={{0,1},{1,0},{2,3},{3,2},{4,5},{5,4},{6,7},{7,6},{8,9},{9,8},{10,11... | collective-permute-start | bytes 12296 | tf_op jit(solution)/shard_map/ppermute | solution.py:514
  7.1 12.9 %collective-permute-start.4 = (bf16[128,1024]{1,0:T(8,128)(2,1)S(1)}, bf16[128,1024]{1,0:T(8,128)(2,1)S(1)}, u32[]{:S(2)}, u32[]{:S(2)}) collective-permute-start(bf16[128,1024]{1,0:T(8,128)(2,1)S(1)} %copy-done.1), channel_id=1, source_target_pairs={{0,1},{1,0},{2,3},{3,2},{4,5},{5,4},{6,7},{7,6},{8,9},{9,8},{10,11... | collective-permute-start | bytes 786440 | tf_op jit(solution)/shard_map/ppermute | solution.py:514
  7.2 14.8 %collective-permute-start.13 = (bf16[64,2048]{1,0:T(8,128)(2,1)S(1)}, bf16[64,2048]{1,0:T(8,128)(2,1)S(1)}, u32[]{:S(2)}, u32[]{:S(2)}) collective-permute-start(bf16[64,2048]{1,0:T(8,128)(2,1)S(1)} %copy-done), channel_id=1, source_target_pairs={{0,2},{1,3},{2,0},{3,1},{4,6},{5,7},{6,4},{7,5},{8,10},{9,11},{10,... | collective-permute-start | bytes 786440 | tf_op jit(solution)/shard_map/ppermute | solution.py:514
  12.4 6.2 %collective-permute-start.16 = (bf16[1,64,1024]{2,1,0:T(8,128)(2,1)S(1)}, bf16[1,64,1024]{2,1,0:T(8,128)(2,1)S(1)}, u32[]{:S(2)}, u32[]{:S(2)}) collective-permute-start(bf16[1,64,1024]{2,1,0:T(8,128)(2,1)S(1)} %get-tuple-element.80), channel_id=1, source_target_pairs={{0,4},{1,5},{2,6},{3,7},{4,0},{5,1},{6,2},{7,3},{8,12},{9,13},{10,... | collective-permute-start | bytes 393224 | tf_op jit(solution)/shard_map/ppermute | solution.py:514
  13.1 7.6 %collective-permute-start.24 = (bf16[1,64,1024]{2,1,0:T(8,128)(2,1)S(1)}, bf16[1,64,1024]{2,1,0:T(8,128)(2,1)S(1)}, u32[]{:S(2)}, u32[]{:S(2)}) collective-permute-start(bf16[1,64,1024]{2,1,0:T(8,128)(2,1)S(1)} %collective-permute-done.15.a), channel_id=1, source_target_pairs={{0,4},{1,5},{2,6},{3,7},{4,0},{5,1},{6,2},{7,3},{8,12},{9,13},{10,... | collective-permute-start | bytes 393224 | tf_op jit(solution)/shard_map/ppermute | solution.py:514
  14.4 12.5 %collective-permute-start.12 = (bf16[64,2048]{1,0:T(8,128)(2,1)S(1)}, bf16[64,2048]{1,0:T(8,128)(2,1)S(1)}, u32[]{:S(2)}, u32[]{:S(2)}) collective-permute-start(bf16[64,2048]{1,0:T(8,128)(2,1)S(1)} %copy-done), channel_id=1, source_target_pairs={{0,1},{1,0},{2,3},{3,2},{4,5},{5,4},{6,7},{7,6},{8,9},{9,8},{10,11... | collective-permute-start | bytes 786440 | tf_op jit(solution)/shard_map/ppermute | solution.py:514
  18.6 5.3 %collective-permute-start.5 = (bf16[4,80,128]{2,1,0:T(8,128)(2,1)S(1)}, bf16[4,80,128]{2,1,0:T(8,128)(2,1)S(1)}, u32[]{:S(2)}, u32[]{:S(2)}) collective-permute-start(bf16[4,80,128]{2,1,0:T(8,128)(2,1)S(1)} %get-tuple-element.57), channel_id=1, source_target_pairs={{0,2},{1,3},{2,0},{3,1},{4,6},{5,7},{6,4},{7,5},{8,10},{9,11},{10,... | collective-permute-start | bytes 245768 | tf_op jit(solution)/shard_map/ppermute | solution.py:514
  19.9 6.8 %collective-permute-start.8 = (bf16[4,128,128]{2,1,0:T(8,128)(2,1)S(1)}, bf16[4,128,128]{2,1,0:T(8,128)(2,1)S(1)}, u32[]{:S(2)}, u32[]{:S(2)}) collective-permute-start(bf16[4,128,128]{2,1,0:T(8,128)(2,1)S(1)} %get-tuple-element.71), channel_id=1, source_target_pairs={{0,2},{1,3},{2,0},{3,1},{4,6},{5,7},{6,4},{7,5},{8,10},{9,11},{10,... | collective-permute-start | bytes 393224 | tf_op jit(solution)/shard_map/ppermute | solution.py:514
  20.8 13.4 %collective-permute-start.18 = (bf16[2,64,1024]{2,1,0:T(8,128)(2,1)S(1)}, bf16[2,64,1024]{2,1,0:T(8,128)(2,1)S(1)}, u32[]{:S(2)}, u32[]{:S(2)}) collective-permute-start(bf16[2,64,1024]{2,1,0:T(8,128)(2,1)S(1)} %shard_map.92.rest_2_), channel_id=1, source_target_pairs={{0,16},{16,0},{1,17},{17,1},{2,18},{18,2},{3,19},{19,3},{4,20},{20... | collective-permute-start | bytes 786440 | tf_op jit(solution)/shard_map/ppermute | solution.py:514
  22.0 12.2 %collective-permute-start.20 = (bf16[2,64,1024]{2,1,0:T(8,128)(2,1)S(1)}, bf16[2,64,1024]{2,1,0:T(8,128)(2,1)S(1)}, u32[]{:S(2)}, u32[]{:S(2)}) collective-permute-start(bf16[2,64,1024]{2,1,0:T(8,128)(2,1)S(1)} %shard_map.92.rest_2_), channel_id=1, source_target_pairs={{0,2},{1,3},{2,0},{3,1},{4,6},{5,7},{6,4},{7,5},{8,10},{9,11},{10,... | collective-permute-start | bytes 786440 | tf_op jit(solution)/shard_map/ppermute | solution.py:514
  23.9 8.7 %collective-permute-start.25 = (bf16[1,64,1024]{2,1,0:T(8,128)(2,1)S(1)}, bf16[1,64,1024]{2,1,0:T(8,128)(2,1)S(1)}, u32[]{:S(2)}, u32[]{:S(2)}) collective-permute-start(bf16[1,64,1024]{2,1,0:T(8,128)(2,1)S(1)} %collective-permute-done.24.a), channel_id=1, source_target_pairs={{0,2},{1,3},{2,0},{3,1},{4,6},{5,7},{6,4},{7,5},{8,10},{9,11},{10,... | collective-permute-start | bytes 393224 | tf_op jit(solution)/shard_map/ppermute | solution.py:514
  26.8 14.6 %collective-permute-start.17 = (bf16[2,64,1024]{2,1,0:T(8,128)(2,1)S(1)}, bf16[2,64,1024]{2,1,0:T(8,128)(2,1)S(1)}, u32[]{:S(2)}, u32[]{:S(2)}) collective-permute-start(bf16[2,64,1024]{2,1,0:T(8,128)(2,1)S(1)} %shard_map.92.rest_2_), channel_id=1, source_target_pairs={{0,1},{1,0},{2,3},{3,2},{4,5},{5,4},{6,7},{7,6},{8,9},{9,8},{10,11... | collective-permute-start | bytes 786440 | tf_op jit(solution)/shard_map/ppermute | solution.py:514
  26.9 11.8 %collective-permute-start.9 = (bf16[4,128,128]{2,1,0:T(8,128)(2,1)S(1)}, bf16[4,128,128]{2,1,0:T(8,128)(2,1)S(1)}, u32[]{:S(2)}, u32[]{:S(2)}) collective-permute-start(bf16[4,128,128]{2,1,0:T(8,128)(2,1)S(1)} %get-tuple-element.73), channel_id=1, source_target_pairs={{0,4},{1,5},{2,6},{3,7},{4,0},{5,1},{6,2},{7,3},{8,12},{9,13},{10,... | collective-permute-start | bytes 393224 | tf_op jit(solution)/shard_map/ppermute | solution.py:514
  32.6 4.4 %collective-permute-start.6 = (bf16[4,80,128]{2,1,0:T(8,128)(2,1)S(1)}, bf16[4,80,128]{2,1,0:T(8,128)(2,1)S(1)}, u32[]{:S(2)}, u32[]{:S(2)}) collective-permute-start(bf16[4,80,128]{2,1,0:T(8,128)(2,1)S(1)} %get-tuple-element.59), channel_id=1, source_target_pairs={{0,4},{1,5},{2,6},{3,7},{4,0},{5,1},{6,2},{7,3},{8,12},{9,13},{10,... | collective-permute-start | bytes 245768 | tf_op jit(solution)/shard_map/ppermute | solution.py:514
  34.2 12.8 %collective-permute-start.14 = (bf16[64,2048]{1,0:T(8,128)(2,1)S(1)}, bf16[64,2048]{1,0:T(8,128)(2,1)S(1)}, u32[]{:S(2)}, u32[]{:S(2)}) collective-permute-start(bf16[64,2048]{1,0:T(8,128)(2,1)S(1)} %collective-permute-done.13.rest_0_), channel_id=1, source_target_pairs={{0,1},{1,0},{2,3},{3,2},{4,5},{5,4},{6,7},{7,6},{8,9},{9,8},{10,11... | collective-permute-start | bytes 786440 | tf_op jit(solution)/shard_map/ppermute | solution.py:514
  34.2 16.4 %collective-permute-start.27 = (bf16[2,64,1024]{2,1,0:T(8,128)(2,1)S(1)}, bf16[2,64,1024]{2,1,0:T(8,128)(2,1)S(1)}, u32[]{:S(2)}, u32[]{:S(2)}) collective-permute-start(bf16[2,64,1024]{2,1,0:T(8,128)(2,1)S(1)} %shard_map.93.rest_10_), channel_id=1, source_target_pairs={{0,16},{16,0},{1,17},{17,1},{2,18},{18,2},{3,19},{19,3},{4,20},{20... | collective-permute-start | bytes 786440 | tf_op jit(solution)/shard_map/ppermute | solution.py:514
  37.1 14.0 %collective-permute-start.22 = (bf16[2,64,1024]{2,1,0:T(8,128)(2,1)S(1)}, bf16[2,64,1024]{2,1,0:T(8,128)(2,1)S(1)}, u32[]{:S(2)}, u32[]{:S(2)}) collective-permute-start(bf16[2,64,1024]{2,1,0:T(8,128)(2,1)S(1)} %collective-permute-done.18.rest_4_), channel_id=1, source_target_pairs={{0,2},{1,3},{2,0},{3,1},{4,6},{5,7},{6,4},{7,5},{8,10},{9,11},{10,... | collective-permute-start | bytes 786440 | tf_op jit(solution)/shard_map/ppermute | solution.py:514
  38.7 8.3 %collective-permute-start.7 = (bf16[4,80,128]{2,1,0:T(8,128)(2,1)S(1)}, bf16[4,80,128]{2,1,0:T(8,128)(2,1)S(1)}, u32[]{:S(2)}, u32[]{:S(2)}) collective-permute-start(bf16[4,80,128]{2,1,0:T(8,128)(2,1)S(1)} %get-tuple-element.62), channel_id=1, source_target_pairs={{0,8},{1,9},{2,10},{3,11},{4,12},{5,13},{6,14},{7,15},{8,0},{9,1},... | collective-permute-start | bytes 245768 | tf_op jit(solution)/shard_map/ppermute | solution.py:514
  41.4 9.2 %collective-permute-start.10 = (bf16[4,128,128]{2,1,0:T(8,128)(2,1)S(1)}, bf16[4,128,128]{2,1,0:T(8,128)(2,1)S(1)}, u32[]{:S(2)}, u32[]{:S(2)}) collective-permute-start(bf16[4,128,128]{2,1,0:T(8,128)(2,1)S(1)} %get-tuple-element.76), channel_id=1, source_target_pairs={{0,8},{1,9},{2,10},{3,11},{4,12},{5,13},{6,14},{7,15},{8,0},{9,1},... | collective-permute-start | bytes 393224 | tf_op jit(solution)/shard_map/ppermute | solution.py:514
  46.9 11.7 %collective-permute-start.26 = (bf16[2,64,1024]{2,1,0:T(8,128)(2,1)S(1)}, bf16[2,64,1024]{2,1,0:T(8,128)(2,1)S(1)}, u32[]{:S(2)}, u32[]{:S(2)}) collective-permute-start(bf16[2,64,1024]{2,1,0:T(8,128)(2,1)S(1)} %shard_map.93.rest_10_), channel_id=1, source_target_pairs={{0,1},{1,0},{2,3},{3,2},{4,5},{5,4},{6,7},{7,6},{8,9},{9,8},{10,11... | collective-permute-start | bytes 786440 | tf_op jit(solution)/shard_map/ppermute | solution.py:514
  46.9 12.3 %collective-permute-start.19 = (bf16[2,64,1024]{2,1,0:T(8,128)(2,1)S(1)}, bf16[2,64,1024]{2,1,0:T(8,128)(2,1)S(1)}, u32[]{:S(2)}, u32[]{:S(2)}) collective-permute-start(bf16[2,64,1024]{2,1,0:T(8,128)(2,1)S(1)} %collective-permute-done.18.rest_4_), channel_id=1, source_target_pairs={{0,1},{1,0},{2,3},{3,2},{4,5},{5,4},{6,7},{7,6},{8,9},{9,8},{10,11... | collective-permute-start | bytes 786440 | tf_op jit(solution)/shard_map/ppermute | solution.py:514
  50.6 8.6 %collective-permute-start.21 = (bf16[2,64,1024]{2,1,0:T(8,128)(2,1)S(1)}, bf16[2,64,1024]{2,1,0:T(8,128)(2,1)S(1)}, u32[]{:S(2)}, u32[]{:S(2)}) collective-permute-start(bf16[2,64,1024]{2,1,0:T(8,128)(2,1)S(1)} %collective-permute-done.20.rest_6_), channel_id=1, source_target_pairs={{0,1},{1,0},{2,3},{3,2},{4,5},{5,4},{6,7},{7,6},{8,9},{9,8},{10,11... | collective-permute-start | bytes 786440 | tf_op jit(solution)/shard_map/ppermute | solution.py:514
  50.6 9.6 %collective-permute-start.28 = (bf16[2,64,1024]{2,1,0:T(8,128)(2,1)S(1)}, bf16[2,64,1024]{2,1,0:T(8,128)(2,1)S(1)}, u32[]{:S(2)}, u32[]{:S(2)}) collective-permute-start(bf16[2,64,1024]{2,1,0:T(8,128)(2,1)S(1)} %collective-permute-done.27.rest_12_), channel_id=1, source_target_pairs={{0,1},{1,0},{2,3},{3,2},{4,5},{5,4},{6,7},{7,6},{8,9},{9,8},{10,11... | collective-permute-start | bytes 786440 | tf_op jit(solution)/shard_map/ppermute | solution.py:514
  51.1 9.1 %collective-permute-start.23 = (bf16[2,64,1024]{2,1,0:T(8,128)(2,1)S(1)}, bf16[2,64,1024]{2,1,0:T(8,128)(2,1)S(1)}, u32[]{:S(2)}, u32[]{:S(2)}) collective-permute-start(bf16[2,64,1024]{2,1,0:T(8,128)(2,1)S(1)} %collective-permute-done.22.rest_8_), channel_id=1, source_target_pairs={{0,1},{1,0},{2,3},{3,2},{4,5},{5,4},{6,7},{7,6},{8,9},{9,8},{10,11... | collective-permute-start | bytes 786440 | tf_op jit(solution)/shard_map/ppermute | solution.py:514
  58.7 1.5 %collective-permute-start.11 = (bf16[128,512]{1,0:T(8,128)(2,1)S(1)}, bf16[128,512]{1,0:T(8,128)(2,1)S(1)}, u32[]{:S(2)}, u32[]{:S(2)}) collective-permute-start(bf16[128,512]{1,0:T(8,128)(2,1)S(1)} %get-tuple-element.79), channel_id=1, source_target_pairs={{0,1},{1,0},{2,3},{3,2},{4,5},{5,4},{6,7},{7,6},{8,9},{9,8},{10,11... | collective-permute-start | bytes 393224 | tf_op jit(solution)/shard_map/ppermute | solution.py:514
  (1 other events, 5.4 us)

commit v5 on v4

--- a/solution.py
+++ b/solution.py
@@ -369,7 +369,7 @@
             part[p] = dot(beside((sh, sl)), twice(v))
 
 
-def read_kernel(which, xs, part, e_s, fo, fr, uf, before_g, before, got, gain, y_own, y_other):
+def read_kernel(which, side, xs, part, e_s, fo, fr, uf, before_g, before, got, gain, out):
     half = uf.shape[0]
     width = uf.shape[1]
     body = width // 2
@@ -377,20 +377,19 @@
     first = core == 0
     bit = bit_of(which) == 1
     decay = jnp.exp(jnp.sum(gates(fo, fr, core, half), axis=1, keepdims=True))
-    sides = ((y_own, first), (y_other, jnp.logical_not(first)))
+    is_early = jnp.logical_not(first) if side else first
     for h in range(half):
         cols = slice(h * width, (h + 1) * width)
         e = jnp.where(bit, jnp.exp(before_g[h, body + 1 : body + 2]), 0.0)
         start = before[h] + e * got[h].astype(F32)
         scale = columns(gain, core, h, half, width)
-        for side, (out, is_early) in enumerate(sides):
-            p = h + side * half
-            other = h + (1 - side) * half
-            state = jnp.where(is_early, start, decay[other : other + 1] * start + uf[h])
-            read = dot(wide((xs[p, 0], xs[p, 1])), tall(split(state)))
-            o = e_s[p] * read + part[p]
-            o = o * lax.rsqrt(jnp.mean(o * o, axis=-1, keepdims=True) + 1e-6)
-            out[:, cols] = (o * scale).astype(BF16)
+        p = h + side * half
+        other = h + (1 - side) * half
+        state = jnp.where(is_early, start, decay[other : other + 1] * start + uf[h])
+        read = dot(wide((xs[p, 0], xs[p, 1])), tall(split(state)))
+        o = e_s[p] * read + part[p]
+        o = o * lax.rsqrt(jnp.mean(o * o, axis=-1, keepdims=True) + 1e-6)
+        out[:, cols] = (o * scale).astype(BF16)
 
 
 def stack_kernel(a, b, out):
@@ -631,13 +630,17 @@
         (ridge_row, q_s, kt, m_s, e_s, ks, s_s, p_s, values_m, values_o),
         (VMEM(many, F32),),
     )
-    y_own, y_other = call(
-        functools.partial(read_kernel, last),
-        (VMEM((tokens, half * width), BF16),) * 2,
-        (),
-        (xs, part, e_s, *forgets, uf, before, before_w, got_w, gain_row),
-    )
-    y_got = swap(y_other, 1)
+
+    def read(side):
+        return call(
+            functools.partial(read_kernel, last, side),
+            VMEM((tokens, half * width), BF16),
+            (),
+            (xs, part, e_s, *forgets, uf, before, before_w, got_w, gain_row),
+        )
+
+    y_got = swap(read(1), 1)
+    y_own = read(0)
 
     result = jax.ShapeDtypeStruct((tokens, out_columns), BF16)
     y_full = VMEM((tokens, features), BF16)

time: 61.9 us -> 61.7 us (level)
    pallas_call x13 -> x14, Pallas kernels: 11.3 us -> 11.7 us  [call(): pl.pallas_call(kernel, out_shape=outs, in_specs=[pl.BlockSpec(memory_spac...]
where the time goes in v5:
time: 61.7 us; the launch traced here: 61.6 us
  waiting for transfers between devices  25.1 us (41%)
  starting transfers between devices  24.7 us (40%)
  Pallas kernels  11.7 us (19%)
    ppermute x29, waiting for transfers between devices, swap(): return lax.ppermute(array, axis, [(i, i ^ distance) for i in range(count)])  25.1 us
    ppermute x29, starting transfers between devices, swap(): return lax.ppermute(array, axis, [(i, i ^ distance) for i in range(count)])  24.7 us
    pallas_call x14, Pallas kernels, call(): pl.pallas_call(kernel, out_shape=outs, in_specs=[pl.BlockSpec(memory_spac...  11.7 us
  transfers between devices with their start and end apart: 29, of which 10 were waited for; matrix products, arithmetic and copies ran while one was open for 0% of the time, Pallas kernels for 16%

profile of v5, /device:TPU:0, one launch (start us, length us, event | category | flops | bytes accessed | tf_op | source)
XLA Modules:
  0.0 61.6 jit_solution(2086313585757052497)
XLA Ops:
  0.5 1.2 %shard_map.82 = (bf16[1,64,1024]{2,1,0:T(8,128)(2,1)S(1)}, bf16[128,512]{1,0:T(8,128)(2,1)S(1)}, bf16[128,512]{1,0:T(8,128)(2,1)S(1)}, bf16[128,512]{1,0:T(8,128...) custom-call(bf16[64,2048]{1,0:T(8,128)(2,1)} %own.1, ...), custom_call_target="tpu_custom_call" | custom-call | tf_op jit(solution)/shard_map/pallas_call | solution.py:487
  1.8 4.1 %collective-permute-start.15 = (bf16[1,64,1024]{2,1,0:T(8,128)(2,1)S(1)}, bf16[1,64,1024]{2,1,0:T(8,128)(2,1)S(1)}, u32[]{:S(2)}, u32[]{:S(2)}) collective-permute-start(bf16[1,64,1024]{2,1,0:T(8,128)(2,1)S(1)} %get-tuple-element.76), channel_id=1, source_target_pairs={{0,8},{1,9},{2,10},{3,11},{4,12},{5,13},{6,14},{7,15},{8,0},{9,1},... | collective-permute-start | bytes 393224 | tf_op jit(solution)/shard_map/ppermute | solution.py:513
  6.4 0.7 %collective-permute-done.2.fr = f32[8,128]{1,0:T(8,128)S(1)} collective-permute-done((f32[8,128]{1,0:T(8,128)S(1)}, f32[8,128]{1,0:T(8,128)S(1)}, u32[]{:S(2)}, u32[]{:S(2)}) %collective-permute-start.2) | collective-permute-done | bytes 4128 | tf_op jit(solution)/shard_map/ppermute | solution.py:513
  7.2 1.5 %collective-permute-start.13 = (bf16[64,2048]{1,0:T(8,128)(2,1)S(1)}, bf16[64,2048]{1,0:T(8,128)(2,1)S(1)}, u32[]{:S(2)}, u32[]{:S(2)}) collective-permute-start(bf16[64,2048]{1,0:T(8,128)(2,1)S(1)} %copy-done), channel_id=1, source_target_pairs={{0,2},{1,3},{2,0},{3,1},{4,6},{5,7},{6,4},{7,5},{8,10},{9,11},{10,... | collective-permute-start | bytes 786440 | tf_op jit(solution)/shard_map/ppermute | solution.py:513
  8.8 3.6 %collective-permute-done.15.a = bf16[1,64,1024]{2,1,0:T(8,128)(2,1)S(1)} collective-permute-done((bf16[1,64,1024]{2,1,0:T(8,128)(2,1)S(1)}, bf16[1,64,1024]{2,1,0:T(8,128)(2,1)S(1)}, u32[]{:S(2)}, u32[]{:S(2)}) %collective-permute-start.15) | collective-permute-done | bytes 131104 | tf_op jit(solution)/shard_map/ppermute | solution.py:513
  12.4 0.7 %collective-permute-start.16 = (bf16[1,64,1024]{2,1,0:T(8,128)(2,1)S(1)}, bf16[1,64,1024]{2,1,0:T(8,128)(2,1)S(1)}, u32[]{:S(2)}, u32[]{:S(2)}) collective-permute-start(bf16[1,64,1024]{2,1,0:T(8,128)(2,1)S(1)} %get-tuple-element.76), channel_id=1, source_target_pairs={{0,4},{1,5},{2,6},{3,7},{4,0},{5,1},{6,2},{7,3},{8,12},{9,13},{10,... | collective-permute-start | bytes 393224 | tf_op jit(solution)/shard_map/ppermute | solution.py:513
  13.1 1.3 %collective-permute-start.24 = (bf16[1,64,1024]{2,1,0:T(8,128)(2,1)S(1)}, bf16[1,64,1024]{2,1,0:T(8,128)(2,1)S(1)}, u32[]{:S(2)}, u32[]{:S(2)}) collective-permute-start(bf16[1,64,1024]{2,1,0:T(8,128)(2,1)S(1)} %collective-permute-done.15.a), channel_id=1, source_target_pairs={{0,4},{1,5},{2,6},{3,7},{4,0},{5,1},{6,2},{7,3},{8,12},{9,13},{10,... | collective-permute-start | bytes 393224 | tf_op jit(solution)/shard_map/ppermute | solution.py:513
  14.4 0.8 %shard_map.83 = (bf16[4,80,128]{2,1,0:T(8,128)(2,1)S(1)}, f32[4,72,128]{2,1,0:T(8,128)S(1)}, bf16[4,128,128]{2,1,0:T(8,128)(2,1)S(1)}, f32[4,128,128]{2,1,0:T(8,...) custom-call(bf16[128,512]{1,0:T(8,128)(2,1)S(1)} %get-tuple-element., ...), custom_call_target="tpu_custom_call" | custom-call | tf_op jit(solution)/shard_map/pallas_call | solution.py:487
  15.2 3.4 %collective-permute-done.16.b = bf16[1,64,1024]{2,1,0:T(8,128)(2,1)S(1)} collective-permute-done((bf16[1,64,1024]{2,1,0:T(8,128)(2,1)S(1)}, bf16[1,64,1024]{2,1,0:T(8,128)(2,1)S(1)}, u32[]{:S(2)}, u32[]{:S(2)}) %collective-permute-start.16) | collective-permute-done | bytes 131104 | tf_op jit(solution)/shard_map/ppermute | solution.py:513
  18.6 1.3 %collective-permute-start.5 = (bf16[4,80,128]{2,1,0:T(8,128)(2,1)S(1)}, bf16[4,80,128]{2,1,0:T(8,128)(2,1)S(1)}, u32[]{:S(2)}, u32[]{:S(2)}) collective-permute-start(bf16[4,80,128]{2,1,0:T(8,128)(2,1)S(1)} %get-tuple-element.55), channel_id=1, source_target_pairs={{0,2},{1,3},{2,0},{3,1},{4,6},{5,7},{6,4},{7,5},{8,10},{9,11},{10,... | collective-permute-start | bytes 245768 | tf_op jit(solution)/shard_map/ppermute | solution.py:513
  19.9 0.8 %collective-permute-start.8 = (bf16[4,128,128]{2,1,0:T(8,128)(2,1)S(1)}, bf16[4,128,128]{2,1,0:T(8,128)(2,1)S(1)}, u32[]{:S(2)}, u32[]{:S(2)}) collective-permute-start(bf16[4,128,128]{2,1,0:T(8,128)(2,1)S(1)} %get-tuple-element.69), channel_id=1, source_target_pairs={{0,2},{1,3},{2,0},{3,1},{4,6},{5,7},{6,4},{7,5},{8,10},{9,11},{10,... | collective-permute-start | bytes 393224 | tf_op jit(solution)/shard_map/ppermute | solution.py:513
  20.8 1.3 %collective-permute-start.18 = (bf16[2,64,1024]{2,1,0:T(8,128)(2,1)S(1)}, bf16[2,64,1024]{2,1,0:T(8,128)(2,1)S(1)}, u32[]{:S(2)}, u32[]{:S(2)}) collective-permute-start(bf16[2,64,1024]{2,1,0:T(8,128)(2,1)S(1)} %shard_map.93.rest_2_), channel_id=1, source_target_pairs={{0,16},{16,0},{1,17},{17,1},{2,18},{18,2},{3,19},{19,3},{4,20},{20... | collective-permute-start | bytes 786440 | tf_op jit(solution)/shard_map/ppermute | solution.py:513
  22.0 1.5 %collective-permute-start.20 = (bf16[2,64,1024]{2,1,0:T(8,128)(2,1)S(1)}, bf16[2,64,1024]{2,1,0:T(8,128)(2,1)S(1)}, u32[]{:S(2)}, u32[]{:S(2)}) collective-permute-start(bf16[2,64,1024]{2,1,0:T(8,128)(2,1)S(1)} %shard_map.93.rest_2_), channel_id=1, source_target_pairs={{0,2},{1,3},{2,0},{3,1},{4,6},{5,7},{6,4},{7,5},{8,10},{9,11},{10,... | collective-permute-start | bytes 786440 | tf_op jit(solution)/shard_map/ppermute | solution.py:513
  23.9 1.3 %collective-permute-start.25 = (bf16[1,64,1024]{2,1,0:T(8,128)(2,1)S(1)}, bf16[1,64,1024]{2,1,0:T(8,128)(2,1)S(1)}, u32[]{:S(2)}, u32[]{:S(2)}) collective-permute-start(bf16[1,64,1024]{2,1,0:T(8,128)(2,1)S(1)} %collective-permute-done.24.a), channel_id=1, source_target_pairs={{0,2},{1,3},{2,0},{3,1},{4,6},{5,7},{6,4},{7,5},{8,10},{9,11},{10,... | collective-permute-start | bytes 393224 | tf_op jit(solution)/shard_map/ppermute | solution.py:513
  25.2 1.5 %collective-permute-done.8.got = bf16[4,128,128]{2,1,0:T(8,128)(2,1)S(1)} collective-permute-done((bf16[4,128,128]{2,1,0:T(8,128)(2,1)S(1)}, bf16[4,128,128]{2,1,0:T(8,128)(2,1)S(1)}, u32[]{:S(2)}, u32[]{:S(2)}) %collective-permute-start.8) | collective-permute-done | bytes 131104 | tf_op jit(solution)/shard_map/ppermute | solution.py:513
  26.9 0.8 %collective-permute-start.9 = (bf16[4,128,128]{2,1,0:T(8,128)(2,1)S(1)}, bf16[4,128,128]{2,1,0:T(8,128)(2,1)S(1)}, u32[]{:S(2)}, u32[]{:S(2)}) collective-permute-start(bf16[4,128,128]{2,1,0:T(8,128)(2,1)S(1)} %get-tuple-element.71), channel_id=1, source_target_pairs={{0,4},{1,5},{2,6},{3,7},{4,0},{5,1},{6,2},{7,3},{8,12},{9,13},{10,... | collective-permute-start | bytes 393224 | tf_op jit(solution)/shard_map/ppermute | solution.py:513
  27.7 5.0 %collective-permute-done.25.b = bf16[1,64,1024]{2,1,0:T(8,128)(2,1)S(1)} collective-permute-done((bf16[1,64,1024]{2,1,0:T(8,128)(2,1)S(1)}, bf16[1,64,1024]{2,1,0:T(8,128)(2,1)S(1)}, u32[]{:S(2)}, u32[]{:S(2)}) %collective-permute-start.25) | collective-permute-done | bytes 131104 | tf_op jit(solution)/shard_map/ppermute | solution.py:513
  32.6 1.5 %collective-permute-start.6 = (bf16[4,80,128]{2,1,0:T(8,128)(2,1)S(1)}, bf16[4,80,128]{2,1,0:T(8,128)(2,1)S(1)}, u32[]{:S(2)}, u32[]{:S(2)}) collective-permute-start(bf16[4,80,128]{2,1,0:T(8,128)(2,1)S(1)} %get-tuple-element.57), channel_id=1, source_target_pairs={{0,4},{1,5},{2,6},{3,7},{4,0},{5,1},{6,2},{7,3},{8,12},{9,13},{10,... | collective-permute-start | bytes 245768 | tf_op jit(solution)/shard_map/ppermute | solution.py:513
  34.2 1.2 %collective-permute-start.27 = (bf16[2,64,1024]{2,1,0:T(8,128)(2,1)S(1)}, bf16[2,64,1024]{2,1,0:T(8,128)(2,1)S(1)}, u32[]{:S(2)}, u32[]{:S(2)}) collective-permute-start(bf16[2,64,1024]{2,1,0:T(8,128)(2,1)S(1)} %shard_map.94.rest_10_), channel_id=1, source_target_pairs={{0,16},{16,0},{1,17},{17,1},{2,18},{18,2},{3,19},{19,3},{4,20},{20... | collective-permute-start | bytes 786440 | tf_op jit(solution)/shard_map/ppermute | solution.py:513
  35.3 1.7 %collective-permute-done.6.got = bf16[4,80,128]{2,1,0:T(8,128)(2,1)S(1)} collective-permute-done((bf16[4,80,128]{2,1,0:T(8,128)(2,1)S(1)}, bf16[4,80,128]{2,1,0:T(8,128)(2,1)S(1)}, u32[]{:S(2)}, u32[]{:S(2)}) %collective-permute-start.6) | collective-permute-done | bytes 81952 | tf_op jit(solution)/shard_map/ppermute | solution.py:513
  37.1 1.5 %collective-permute-start.22 = (bf16[2,64,1024]{2,1,0:T(8,128)(2,1)S(1)}, bf16[2,64,1024]{2,1,0:T(8,128)(2,1)S(1)}, u32[]{:S(2)}, u32[]{:S(2)}) collective-permute-start(bf16[2,64,1024]{2,1,0:T(8,128)(2,1)S(1)} %collective-permute-done.18.rest_4_), channel_id=1, source_target_pairs={{0,2},{1,3},{2,0},{3,1},{4,6},{5,7},{6,4},{7,5},{8,10},{9,11},{10,... | collective-permute-start | bytes 786440 | tf_op jit(solution)/shard_map/ppermute | solution.py:513
  38.7 2.6 %collective-permute-start.7 = (bf16[4,80,128]{2,1,0:T(8,128)(2,1)S(1)}, bf16[4,80,128]{2,1,0:T(8,128)(2,1)S(1)}, u32[]{:S(2)}, u32[]{:S(2)}) collective-permute-start(bf16[4,80,128]{2,1,0:T(8,128)(2,1)S(1)} %get-tuple-element.60), channel_id=1, source_target_pairs={{0,8},{1,9},{2,10},{3,11},{4,12},{5,13},{6,14},{7,15},{8,0},{9,1},... | collective-permute-start | bytes 245768 | tf_op jit(solution)/shard_map/ppermute | solution.py:513
  41.8 5.2 %collective-permute-done.7.got = bf16[4,80,128]{2,1,0:T(8,128)(2,1)S(1)} collective-permute-done((bf16[4,80,128]{2,1,0:T(8,128)(2,1)S(1)}, bf16[4,80,128]{2,1,0:T(8,128)(2,1)S(1)}, u32[]{:S(2)}, u32[]{:S(2)}) %collective-permute-start.7) | collective-permute-done | bytes 81952 | tf_op jit(solution)/shard_map/ppermute | solution.py:513
  47.0 0.5 collective-permute-start.19
  47.5 3.1 %collective-permute-done.10.got = bf16[4,128,128]{2,1,0:T(8,128)(2,1)S(1)} collective-permute-done((bf16[4,128,128]{2,1,0:T(8,128)(2,1)S(1)}, bf16[4,128,128]{2,1,0:T(8,128)(2,1)S(1)}, u32[]{:S(2)}, u32[]{:S(2)}) %collective-permute-start.10) | collective-permute-done | bytes 131104 | tf_op jit(solution)/shard_map/ppermute | solution.py:513
  50.6 0.5 collective-permute-start.28
  51.2 1.2 %shard_map.84 = (f32[8,128,128]{2,1,0:T(8,128)S(1)}, f32[8,128,128]{2,1,0:T(8,128)S(1)}, f32[8,128,128]{2,1,0:T(8,128)S(1)}, f32[8,128,128]{2,1,0:T(8,128)S(1)}) custom-call(f32[1,8]{1,0:T(1,128)S(1)} %get-tuple-element.41.ridge, bf16[8,2,128,128]{3,2,1,0:T(8,128)(2,1)S(1)} %get-tuple-element.46.ks, bf16[8,2,128,128]{3,2,1,0:T(8,128)(2,1)S(1)} %get-tuple-element.47.kt, ...), custom_call_target="tpu_custom_call" | custom-call | tf_op jit(solution)/shard_map/pallas_call | solution.py:487
  52.3 2.9 %shard_map.87 = (bf16[8,2,128,128]{3,2,1,0:T(8,128)(2,1)S(1)}, f32[8,128,128]{2,1,0:T(8,128)S(1)}) custom-call(f32[8,128,128]{2,1,0:T(8,128)S(1)} %get-tuple-element.52.base, f32[8,128]{1,0:T(8,128)S(1)} %get-tuple-element.44.fo, f32[8,128]{1,0:T(8,128)S(1)} %collective-permute-done.2.fr, f32[4,128,128]{2,1,0:T(8,128)S(1)} %get-tuple-element.53.gf, ...), custom_call_target="tpu_custom_call" | custom-call | tf_op jit(solution)/shard_map/pallas_call | solution.py:487
  55.2 2.9 %shard_map.88 = (bf16[8,2,128,128]{3,2,1,0:T(8,128)(2,1)S(1)}, f32[8,128,128]{2,1,0:T(8,128)S(1)}) custom-call(f32[1,8]{1,0:T(1,128)S(1)} %get-tuple-element.41.ridge, f32[8,128,128]{2,1,0:T(8,128)S(1)} %get-tuple-element.49.q_s, bf16[8,2,128,128]{3,2,1,0:T(8,128)(2,1)S(1)} %get-tuple-element.47.kt, f32[8,128,128]{2,1,0:T(8,128)S(1)} %get-tuple-element.50.m_s, ...), custom_call_target="tpu_custom_call" | custom-call | tf_op jit(solution)/shard_map/pallas_call | solution.py:487
  58.6 0.5 collective-permute-start.11
  59.6 0.5 collective-permute-done.11.y_other
  60.1 1.5 %shard_map.95 = bf16[128,2048]{1,0:T(8,128)(2,1)} custom-call(bf16[128,512]{1,0:T(8,128)(2,1)S(1)} %shard_map.91.y_own, bf16[128,512]{1,0:T(8,128)(2,1)S(1)} %collective-permute-done.11.y_other, bf16[64,2048]{1,0:T(8,128)(2,1)S(1)} %copy-done, bf16[64,2048]{1,0:T(8,128)(2,1)S(1)} %collective-permute-done.12.other, ...), custom_call_target="tpu_custom_call" | custom-call | tf_op jit(solution)/shard_map/pallas_call | solution.py:487
  (48 shorter events, 3.3 us)
Async XLA Ops:
  0.0 13.1 %collective-permute-start.1 = (bf16[128,1024]{1,0:T(8,128)(2,1)}, bf16[128,1024]{1,0:T(8,128)(2,1)S(1)}, u32[]{:S(2)}, u32[]{:S(2)}) collective-permute-start(bf16[128,1024]{1,0:T(8,128)(2,1)} %refs_2_.1), channel_id=1, source_target_pairs={{0,1},{1,0},{2,3},{3,2},{4,5},{5,4},{6,7},{7,6},{8,9},{9,8},{10,11... | collective-permute-start | bytes 786440 | tf_op jit(solution)/shard_map/ppermute | solution.py:513
  0.5 13.9 %collective-permute-start = (bf16[128,1024]{1,0:T(8,128)(2,1)}, bf16[128,1024]{1,0:T(8,128)(2,1)S(1)}, u32[]{:S(2)}, u32[]{:S(2)}) collective-permute-start(bf16[128,1024]{1,0:T(8,128)(2,1)} %refs_1_.1), channel_id=1, source_target_pairs={{0,1},{1,0},{2,3},{3,2},{4,5},{5,4},{6,7},{7,6},{8,9},{9,8},{10,11... | collective-permute-start | bytes 786440 | tf_op jit(solution)/shard_map/ppermute | solution.py:513
  0.5 5.4 %copy-start.3 = (f32[8,128]{1,0:T(8,128)S(1)}, f32[8,128]{1,0:T(8,128)}, u32[]{:S(2)}) copy-start(f32[8,128]{1,0:T(8,128)} %refs_5_.1) | copy-start | bytes 12292
  0.5 6.6 %copy-start.1 = (bf16[128,1024]{1,0:T(8,128)(2,1)S(1)}, bf16[128,1024]{1,0:T(8,128)(2,1)}, u32[]{:S(2)}) copy-start(bf16[128,1024]{1,0:T(8,128)(2,1)} %refs_3_.1) | copy-start | bytes 786436
  0.5 6.7 %copy-start = (bf16[64,2048]{1,0:T(8,128)(2,1)S(1)}, bf16[64,2048]{1,0:T(8,128)(2,1)}, u32[]{:S(2)}) copy-start(bf16[64,2048]{1,0:T(8,128)(2,1)} %own.1) | copy-start | bytes 786436
  1.8 10.6 %collective-permute-start.15 = (bf16[1,64,1024]{2,1,0:T(8,128)(2,1)S(1)}, bf16[1,64,1024]{2,1,0:T(8,128)(2,1)S(1)}, u32[]{:S(2)}, u32[]{:S(2)}) collective-permute-start(bf16[1,64,1024]{2,1,0:T(8,128)(2,1)S(1)} %get-tuple-element.76), channel_id=1, source_target_pairs={{0,8},{1,9},{2,10},{3,11},{4,12},{5,13},{6,14},{7,15},{8,0},{9,1},... | collective-permute-start | bytes 393224 | tf_op jit(solution)/shard_map/ppermute | solution.py:513
  5.9 1.2 %collective-permute-start.2 = (f32[8,128]{1,0:T(8,128)S(1)}, f32[8,128]{1,0:T(8,128)S(1)}, u32[]{:S(2)}, u32[]{:S(2)}) collective-permute-start(f32[8,128]{1,0:T(8,128)S(1)} %copy-done.2), channel_id=1, source_target_pairs={{0,1},{1,0},{2,3},{3,2},{4,5},{5,4},{6,7},{7,6},{8,9},{9,8},{10,11... | collective-permute-start | bytes 12296 | tf_op jit(solution)/shard_map/ppermute | solution.py:513
  5.9 1.3 %collective-permute-start.3 = (f32[8,128]{1,0:T(8,128)S(1)}, f32[8,128]{1,0:T(8,128)S(1)}, u32[]{:S(2)}, u32[]{:S(2)}) collective-permute-start(f32[8,128]{1,0:T(8,128)S(1)} %copy-done.3), channel_id=1, source_target_pairs={{0,1},{1,0},{2,3},{3,2},{4,5},{5,4},{6,7},{7,6},{8,9},{9,8},{10,11... | collective-permute-start | bytes 12296 | tf_op jit(solution)/shard_map/ppermute | solution.py:513
  7.1 12.9 %collective-permute-start.4 = (bf16[128,1024]{1,0:T(8,128)(2,1)S(1)}, bf16[128,1024]{1,0:T(8,128)(2,1)S(1)}, u32[]{:S(2)}, u32[]{:S(2)}) collective-permute-start(bf16[128,1024]{1,0:T(8,128)(2,1)S(1)} %copy-done.1), channel_id=1, source_target_pairs={{0,1},{1,0},{2,3},{3,2},{4,5},{5,4},{6,7},{7,6},{8,9},{9,8},{10,11... | collective-permute-start | bytes 786440 | tf_op jit(solution)/shard_map/ppermute | solution.py:513
  7.2 14.8 %collective-permute-start.13 = (bf16[64,2048]{1,0:T(8,128)(2,1)S(1)}, bf16[64,2048]{1,0:T(8,128)(2,1)S(1)}, u32[]{:S(2)}, u32[]{:S(2)}) collective-permute-start(bf16[64,2048]{1,0:T(8,128)(2,1)S(1)} %copy-done), channel_id=1, source_target_pairs={{0,2},{1,3},{2,0},{3,1},{4,6},{5,7},{6,4},{7,5},{8,10},{9,11},{10,... | collective-permute-start | bytes 786440 | tf_op jit(solution)/shard_map/ppermute | solution.py:513
  12.4 6.2 %collective-permute-start.16 = (bf16[1,64,1024]{2,1,0:T(8,128)(2,1)S(1)}, bf16[1,64,1024]{2,1,0:T(8,128)(2,1)S(1)}, u32[]{:S(2)}, u32[]{:S(2)}) collective-permute-start(bf16[1,64,1024]{2,1,0:T(8,128)(2,1)S(1)} %get-tuple-element.76), channel_id=1, source_target_pairs={{0,4},{1,5},{2,6},{3,7},{4,0},{5,1},{6,2},{7,3},{8,12},{9,13},{10,... | collective-permute-start | bytes 393224 | tf_op jit(solution)/shard_map/ppermute | solution.py:513
  13.1 7.6 %collective-permute-start.24 = (bf16[1,64,1024]{2,1,0:T(8,128)(2,1)S(1)}, bf16[1,64,1024]{2,1,0:T(8,128)(2,1)S(1)}, u32[]{:S(2)}, u32[]{:S(2)}) collective-permute-start(bf16[1,64,1024]{2,1,0:T(8,128)(2,1)S(1)} %collective-permute-done.15.a), channel_id=1, source_target_pairs={{0,4},{1,5},{2,6},{3,7},{4,0},{5,1},{6,2},{7,3},{8,12},{9,13},{10,... | collective-permute-start | bytes 393224 | tf_op jit(solution)/shard_map/ppermute | solution.py:513
  14.4 12.5 %collective-permute-start.12 = (bf16[64,2048]{1,0:T(8,128)(2,1)S(1)}, bf16[64,2048]{1,0:T(8,128)(2,1)S(1)}, u32[]{:S(2)}, u32[]{:S(2)}) collective-permute-start(bf16[64,2048]{1,0:T(8,128)(2,1)S(1)} %copy-done), channel_id=1, source_target_pairs={{0,1},{1,0},{2,3},{3,2},{4,5},{5,4},{6,7},{7,6},{8,9},{9,8},{10,11... | collective-permute-start | bytes 786440 | tf_op jit(solution)/shard_map/ppermute | solution.py:513
  18.6 5.3 %collective-permute-start.5 = (bf16[4,80,128]{2,1,0:T(8,128)(2,1)S(1)}, bf16[4,80,128]{2,1,0:T(8,128)(2,1)S(1)}, u32[]{:S(2)}, u32[]{:S(2)}) collective-permute-start(bf16[4,80,128]{2,1,0:T(8,128)(2,1)S(1)} %get-tuple-element.55), channel_id=1, source_target_pairs={{0,2},{1,3},{2,0},{3,1},{4,6},{5,7},{6,4},{7,5},{8,10},{9,11},{10,... | collective-permute-start | bytes 245768 | tf_op jit(solution)/shard_map/ppermute | solution.py:513
  19.9 6.8 %collective-permute-start.8 = (bf16[4,128,128]{2,1,0:T(8,128)(2,1)S(1)}, bf16[4,128,128]{2,1,0:T(8,128)(2,1)S(1)}, u32[]{:S(2)}, u32[]{:S(2)}) collective-permute-start(bf16[4,128,128]{2,1,0:T(8,128)(2,1)S(1)} %get-tuple-element.69), channel_id=1, source_target_pairs={{0,2},{1,3},{2,0},{3,1},{4,6},{5,7},{6,4},{7,5},{8,10},{9,11},{10,... | collective-permute-start | bytes 393224 | tf_op jit(solution)/shard_map/ppermute | solution.py:513
  20.8 13.4 %collective-permute-start.18 = (bf16[2,64,1024]{2,1,0:T(8,128)(2,1)S(1)}, bf16[2,64,1024]{2,1,0:T(8,128)(2,1)S(1)}, u32[]{:S(2)}, u32[]{:S(2)}) collective-permute-start(bf16[2,64,1024]{2,1,0:T(8,128)(2,1)S(1)} %shard_map.93.rest_2_), channel_id=1, source_target_pairs={{0,16},{16,0},{1,17},{17,1},{2,18},{18,2},{3,19},{19,3},{4,20},{20... | collective-permute-start | bytes 786440 | tf_op jit(solution)/shard_map/ppermute | solution.py:513
  22.0 12.2 %collective-permute-start.20 = (bf16[2,64,1024]{2,1,0:T(8,128)(2,1)S(1)}, bf16[2,64,1024]{2,1,0:T(8,128)(2,1)S(1)}, u32[]{:S(2)}, u32[]{:S(2)}) collective-permute-start(bf16[2,64,1024]{2,1,0:T(8,128)(2,1)S(1)} %shard_map.93.rest_2_), channel_id=1, source_target_pairs={{0,2},{1,3},{2,0},{3,1},{4,6},{5,7},{6,4},{7,5},{8,10},{9,11},{10,... | collective-permute-start | bytes 786440 | tf_op jit(solution)/shard_map/ppermute | solution.py:513
  23.9 8.7 %collective-permute-start.25 = (bf16[1,64,1024]{2,1,0:T(8,128)(2,1)S(1)}, bf16[1,64,1024]{2,1,0:T(8,128)(2,1)S(1)}, u32[]{:S(2)}, u32[]{:S(2)}) collective-permute-start(bf16[1,64,1024]{2,1,0:T(8,128)(2,1)S(1)} %collective-permute-done.24.a), channel_id=1, source_target_pairs={{0,2},{1,3},{2,0},{3,1},{4,6},{5,7},{6,4},{7,5},{8,10},{9,11},{10,... | collective-permute-start | bytes 393224 | tf_op jit(solution)/shard_map/ppermute | solution.py:513
  26.8 14.6 %collective-permute-start.17 = (bf16[2,64,1024]{2,1,0:T(8,128)(2,1)S(1)}, bf16[2,64,1024]{2,1,0:T(8,128)(2,1)S(1)}, u32[]{:S(2)}, u32[]{:S(2)}) collective-permute-start(bf16[2,64,1024]{2,1,0:T(8,128)(2,1)S(1)} %shard_map.93.rest_2_), channel_id=1, source_target_pairs={{0,1},{1,0},{2,3},{3,2},{4,5},{5,4},{6,7},{7,6},{8,9},{9,8},{10,11... | collective-permute-start | bytes 786440 | tf_op jit(solution)/shard_map/ppermute | solution.py:513
  26.9 11.8 %collective-permute-start.9 = (bf16[4,128,128]{2,1,0:T(8,128)(2,1)S(1)}, bf16[4,128,128]{2,1,0:T(8,128)(2,1)S(1)}, u32[]{:S(2)}, u32[]{:S(2)}) collective-permute-start(bf16[4,128,128]{2,1,0:T(8,128)(2,1)S(1)} %get-tuple-element.71), channel_id=1, source_target_pairs={{0,4},{1,5},{2,6},{3,7},{4,0},{5,1},{6,2},{7,3},{8,12},{9,13},{10,... | collective-permute-start | bytes 393224 | tf_op jit(solution)/shard_map/ppermute | solution.py:513
  32.6 4.4 %collective-permute-start.6 = (bf16[4,80,128]{2,1,0:T(8,128)(2,1)S(1)}, bf16[4,80,128]{2,1,0:T(8,128)(2,1)S(1)}, u32[]{:S(2)}, u32[]{:S(2)}) collective-permute-start(bf16[4,80,128]{2,1,0:T(8,128)(2,1)S(1)} %get-tuple-element.57), channel_id=1, source_target_pairs={{0,4},{1,5},{2,6},{3,7},{4,0},{5,1},{6,2},{7,3},{8,12},{9,13},{10,... | collective-permute-start | bytes 245768 | tf_op jit(solution)/shard_map/ppermute | solution.py:513
  34.2 12.8 %collective-permute-start.14 = (bf16[64,2048]{1,0:T(8,128)(2,1)S(1)}, bf16[64,2048]{1,0:T(8,128)(2,1)S(1)}, u32[]{:S(2)}, u32[]{:S(2)}) collective-permute-start(bf16[64,2048]{1,0:T(8,128)(2,1)S(1)} %collective-permute-done.13.rest_0_), channel_id=1, source_target_pairs={{0,1},{1,0},{2,3},{3,2},{4,5},{5,4},{6,7},{7,6},{8,9},{9,8},{10,11... | collective-permute-start | bytes 786440 | tf_op jit(solution)/shard_map/ppermute | solution.py:513
  34.2 16.4 %collective-permute-start.27 = (bf16[2,64,1024]{2,1,0:T(8,128)(2,1)S(1)}, bf16[2,64,1024]{2,1,0:T(8,128)(2,1)S(1)}, u32[]{:S(2)}, u32[]{:S(2)}) collective-permute-start(bf16[2,64,1024]{2,1,0:T(8,128)(2,1)S(1)} %shard_map.94.rest_10_), channel_id=1, source_target_pairs={{0,16},{16,0},{1,17},{17,1},{2,18},{18,2},{3,19},{19,3},{4,20},{20... | collective-permute-start | bytes 786440 | tf_op jit(solution)/shard_map/ppermute | solution.py:513
  37.1 14.0 %collective-permute-start.22 = (bf16[2,64,1024]{2,1,0:T(8,128)(2,1)S(1)}, bf16[2,64,1024]{2,1,0:T(8,128)(2,1)S(1)}, u32[]{:S(2)}, u32[]{:S(2)}) collective-permute-start(bf16[2,64,1024]{2,1,0:T(8,128)(2,1)S(1)} %collective-permute-done.18.rest_4_), channel_id=1, source_target_pairs={{0,2},{1,3},{2,0},{3,1},{4,6},{5,7},{6,4},{7,5},{8,10},{9,11},{10,... | collective-permute-start | bytes 786440 | tf_op jit(solution)/shard_map/ppermute | solution.py:513
  38.7 8.3 %collective-permute-start.7 = (bf16[4,80,128]{2,1,0:T(8,128)(2,1)S(1)}, bf16[4,80,128]{2,1,0:T(8,128)(2,1)S(1)}, u32[]{:S(2)}, u32[]{:S(2)}) collective-permute-start(bf16[4,80,128]{2,1,0:T(8,128)(2,1)S(1)} %get-tuple-element.60), channel_id=1, source_target_pairs={{0,8},{1,9},{2,10},{3,11},{4,12},{5,13},{6,14},{7,15},{8,0},{9,1},... | collective-permute-start | bytes 245768 | tf_op jit(solution)/shard_map/ppermute | solution.py:513
  41.4 9.2 %collective-permute-start.10 = (bf16[4,128,128]{2,1,0:T(8,128)(2,1)S(1)}, bf16[4,128,128]{2,1,0:T(8,128)(2,1)S(1)}, u32[]{:S(2)}, u32[]{:S(2)}) collective-permute-start(bf16[4,128,128]{2,1,0:T(8,128)(2,1)S(1)} %get-tuple-element.74), channel_id=1, source_target_pairs={{0,8},{1,9},{2,10},{3,11},{4,12},{5,13},{6,14},{7,15},{8,0},{9,1},... | collective-permute-start | bytes 393224 | tf_op jit(solution)/shard_map/ppermute | solution.py:513
  46.9 11.6 %collective-permute-start.26 = (bf16[2,64,1024]{2,1,0:T(8,128)(2,1)S(1)}, bf16[2,64,1024]{2,1,0:T(8,128)(2,1)S(1)}, u32[]{:S(2)}, u32[]{:S(2)}) collective-permute-start(bf16[2,64,1024]{2,1,0:T(8,128)(2,1)S(1)} %shard_map.94.rest_10_), channel_id=1, source_target_pairs={{0,1},{1,0},{2,3},{3,2},{4,5},{5,4},{6,7},{7,6},{8,9},{9,8},{10,11... | collective-permute-start | bytes 786440 | tf_op jit(solution)/shard_map/ppermute | solution.py:513
  47.0 12.6 %collective-permute-start.19 = (bf16[2,64,1024]{2,1,0:T(8,128)(2,1)S(1)}, bf16[2,64,1024]{2,1,0:T(8,128)(2,1)S(1)}, u32[]{:S(2)}, u32[]{:S(2)}) collective-permute-start(bf16[2,64,1024]{2,1,0:T(8,128)(2,1)S(1)} %collective-permute-done.18.rest_4_), channel_id=1, source_target_pairs={{0,1},{1,0},{2,3},{3,2},{4,5},{5,4},{6,7},{7,6},{8,9},{9,8},{10,11... | collective-permute-start | bytes 786440 | tf_op jit(solution)/shard_map/ppermute | solution.py:513
  50.6 9.0 %collective-permute-start.21 = (bf16[2,64,1024]{2,1,0:T(8,128)(2,1)S(1)}, bf16[2,64,1024]{2,1,0:T(8,128)(2,1)S(1)}, u32[]{:S(2)}, u32[]{:S(2)}) collective-permute-start(bf16[2,64,1024]{2,1,0:T(8,128)(2,1)S(1)} %collective-permute-done.20.rest_6_), channel_id=1, source_target_pairs={{0,1},{1,0},{2,3},{3,2},{4,5},{5,4},{6,7},{7,6},{8,9},{9,8},{10,11... | collective-permute-start | bytes 786440 | tf_op jit(solution)/shard_map/ppermute | solution.py:513
  50.6 9.5 %collective-permute-start.28 = (bf16[2,64,1024]{2,1,0:T(8,128)(2,1)S(1)}, bf16[2,64,1024]{2,1,0:T(8,128)(2,1)S(1)}, u32[]{:S(2)}, u32[]{:S(2)}) collective-permute-start(bf16[2,64,1024]{2,1,0:T(8,128)(2,1)S(1)} %collective-permute-done.27.rest_12_), channel_id=1, source_target_pairs={{0,1},{1,0},{2,3},{3,2},{4,5},{5,4},{6,7},{7,6},{8,9},{9,8},{10,11... | collective-permute-start | bytes 786440 | tf_op jit(solution)/shard_map/ppermute | solution.py:513
  51.1 9.0 %collective-permute-start.23 = (bf16[2,64,1024]{2,1,0:T(8,128)(2,1)S(1)}, bf16[2,64,1024]{2,1,0:T(8,128)(2,1)S(1)}, u32[]{:S(2)}, u32[]{:S(2)}) collective-permute-start(bf16[2,64,1024]{2,1,0:T(8,128)(2,1)S(1)} %collective-permute-done.22.rest_8_), channel_id=1, source_target_pairs={{0,1},{1,0},{2,3},{3,2},{4,5},{5,4},{6,7},{7,6},{8,9},{9,8},{10,11... | collective-permute-start | bytes 786440 | tf_op jit(solution)/shard_map/ppermute | solution.py:513
  58.6 1.5 %collective-permute-start.11 = (bf16[128,512]{1,0:T(8,128)(2,1)S(1)}, bf16[128,512]{1,0:T(8,128)(2,1)S(1)}, u32[]{:S(2)}, u32[]{:S(2)}) collective-permute-start(bf16[128,512]{1,0:T(8,128)(2,1)S(1)} %shard_map.92), channel_id=1, source_target_pairs={{0,1},{1,0},{2,3},{3,2},{4,5},{5,4},{6,7},{7,6},{8,9},{9,8},{10,11... | collective-permute-start | bytes 393224 | tf_op jit(solution)/shard_map/ppermute | solution.py:513
  (1 other events, 5.4 us)
